TPU v7x, 128 devices: a whole 4x4x4 slice. The times are simulated.
128 devices in a mesh: det: 8 (over y, core), tm: 16 (over z, x).
Axes of the slice: x: 4, y: 4, z: 4, core: 2. Of those that a mesh axis runs over, the one named last changes fastest.
Arguments:
- timestreams: float32 [256, 65536], P('det', 'tm')
- templates: float32 [256, 32], P('det')
- validity: int32 [256], P('det'), may hold values 0 or 1
- tile_index: int32 [256, 512], P('det', 'tm'), may hold values from 0 to 15, as said below
- row_offset: int32 [256, 512], P('det', 'tm'), may hold values from 0 to 63
- col_start: int32 [256, 512], P('det', 'tm'), may hold values from 0 to 127
Outputs:
- cleaned: float32 [256, 65536], P('det', 'tm')
- beamed: float32 [64, 2048], P('det', 'tm')
Inputs may be any that keep to these rules, and one draw needn't show every extreme that they name: `tile_index`: any run may name any tile.
All inputs are finite; a program needn't handle non-finite values. No bound on the sum of `validity` on one device may be relied on, other than what follows from the above.
Results may differ from a plain program's by a relative error of at most 0.00011.
Values sent between devices are 32-bit elements; how exact they have to be, the bound alone decides.
No kernel may reach another device: no remote copies, remote signals or barrier semaphores. Data moves between devices by JAX's collectives and lax.ppermute only.
A program may use at most 64 MiB of HBM per device.

v0:
```python
import math

import jax
import jax.numpy as jnp
from jax import lax
from jax.sharding import PartitionSpec as P

FKEEP = 128
RUN = 128
TROWS = 64
TCOLS = 128
TILE_DEV = 1
RADIUS = 3


def extended(cells, sides, width):
    for axis, dim in sides:
        count = lax.axis_size(axis)
        ends = count - 1
        head = lax.slice_in_dim(cells, 0, width, axis=dim)
        tail = lax.slice_in_dim(cells, cells.shape[dim] - width, cells.shape[dim], axis=dim)
        cells = jnp.concatenate(
            [
                lax.ppermute(tail, axis, [(i, (i + 1) % count) for i in range(ends)]),
                cells,
                lax.ppermute(head, axis, [((i + 1) % count, i) for i in range(ends)]),
            ],
            axis=dim,
        )
    return cells


def beam_taps():
    values = [math.exp(-(m * m) / 4.5) for m in range(-RADIUS, RADIUS + 1)]
    total = sum(values)
    return [v / total for v in values]


def rotate_runs(run_values, starts):
    rotated = run_values
    width = run_values.shape[1]
    level = 0
    while 1 << level < width:
        moved = jnp.roll(rotated, 1 << level, axis=1)
        chosen = starts >> level & 1 == 1
        rotated = jnp.where(chosen[:, None], moved, rotated)
        level = level + 1
    return rotated


def body(timestreams, templates, validity, tile_index, row_offset, col_start):
    hp = lax.Precision.HIGHEST
    seg_len = timestreams.shape[1]
    weight = validity.astype(jnp.float32)[:, None]
    gram_part = jnp.dot(templates.T, templates * weight, precision=hp)
    projected = jnp.dot(templates.T, timestreams * weight, precision=hp)
    sample_pos = jnp.arange(seg_len, dtype=jnp.int32)[:, None]
    bin_index = jnp.arange(FKEEP, dtype=jnp.int32)[None, :]
    angle = 2.0 * math.pi * (sample_pos * bin_index % seg_len).astype(jnp.float32) / seg_len
    basis = jnp.concatenate([jnp.cos(angle), jnp.sin(angle)], axis=1)
    scaling = jnp.where(jnp.arange(FKEEP) == 0, 1.0 / seg_len, 2.0 / seg_len).astype(jnp.float32)
    scaling = jnp.concatenate([scaling, scaling])
    ridge = 0.05 * jnp.eye(templates.shape[1], dtype=jnp.float32)
    mode_gram, summed = lax.psum((gram_part, projected), "det")
    factor = jnp.linalg.cholesky(mode_gram + ridge)
    amplitude = jax.scipy.linalg.cho_solve((factor, True), summed)
    spectra = jnp.dot(amplitude, basis, precision=hp)
    lowpass = lax.dot_general(
        spectra * scaling[None, :], basis, (((1,), (1,)), ((), ())), precision=hp
    )
    cleaned = weight * (timestreams - jnp.dot(templates, lowpass, precision=hp))
    tile_width = TILE_DEV * TCOLS
    n_tiles = TILE_DEV * lax.axis_size("tm")
    grid_cols = n_tiles * TCOLS
    run_count = tile_index.shape[0] * tile_index.shape[1]
    run_values = cleaned.reshape(run_count, RUN)
    rotated = rotate_runs(run_values, col_start.reshape(run_count))
    line_id = (row_offset * n_tiles + tile_index).reshape(run_count)
    line_count = TROWS * n_tiles
    onehot = (line_id[:, None] == jnp.arange(line_count, dtype=jnp.int32)[None, :]).astype(
        jnp.float32
    )
    run_weight = jnp.broadcast_to(weight, tile_index.shape).reshape(run_count, 1)
    grid_sum = lax.dot_general(onehot, rotated, (((0,), (0,)), ((), ())), precision=hp)
    line_hits = lax.dot_general(onehot, run_weight, (((0,), (0,)), ((), ())), precision=hp)
    grid_sum = grid_sum.reshape(TROWS, grid_cols)
    grid_hits = jnp.broadcast_to(line_hits, (line_count, TCOLS)).reshape(TROWS, grid_cols)
    owned_sum, owned_hits = (
        lax.psum_scatter(grid_sum, "tm", scatter_dimension=1, tiled=True),
        lax.psum_scatter(grid_hits, "tm", scatter_dimension=1, tiled=True),
    )
    binsum, hits = (
        lax.psum_scatter(owned_sum, "det", scatter_dimension=0, tiled=True),
        lax.psum_scatter(owned_hits, "det", scatter_dimension=0, tiled=True),
    )
    binned = binsum / (hits + 1.0)
    taps = beam_taps()
    row_count = binned.shape[0]
    padded = extended(binned, (("det", 0), ("tm", 1)), RADIUS)
    smoothed = jnp.zeros((row_count, padded.shape[1]), jnp.float32)
    for shift_pos in range(2 * RADIUS + 1):
        smoothed = smoothed + taps[shift_pos] * padded[shift_pos : shift_pos + row_count, :]
    beamed = jnp.zeros((row_count, tile_width), jnp.float32)
    for shift_pos in range(2 * RADIUS + 1):
        beamed = beamed + taps[shift_pos] * smoothed[:, shift_pos : shift_pos + tile_width]
    return (cleaned, beamed)


def solution(mesh):
    in_specs = (
        P("det", "tm"),
        P("det", None),
        P("det"),
        P("det", "tm"),
        P("det", "tm"),
        P("det", "tm"),
    )
    out_specs = (P("det", "tm"), P("det", "tm"))
    return jax.shard_map(body, mesh=mesh, in_specs=in_specs, out_specs=out_specs, check_vma=False)
```

profile of v0, /device:TPU:0, one launch (start us, length us, event | category | flops | bytes accessed | tf_op | source)
XLA Modules:
  0.0 251.4 jit_solution(590380900882090193)
XLA Ops:
  8.7 2.5 convolution_bitcast_fusion.1
  11.3 0.7 multiply_add_fusion.1
  12.2 7.5 %fusion.3 = f32[1,64,16]{2,0,1:T(1,128)S(1)} fusion(f32[1024,1,1]{0,1,2:T(1,128)S(1)} %reshape.150, s32[64,16]{1,0:T(8,128)S(1)} %multiply_add_fusion, s32[1024]{0:T(1024)S(1)} %eq.120), kind=kOutput, calls=%fused_computation.7 | convolution fusion | flops 13631488 | bytes 16384 | tf_op jit(solution)/shard_map/dot_general | solution.py:85
  19.9 1.0 copy.18
  21.2 9.1 %fusion.17 = (f32[4096,128]{1,0:T(8,128)S(1)}, f32[4096,128]{1,0:T(8,128)}) fusion(), kind=kLoop, calls=%fused_computation.25 | loop fusion | flops 7340032 | bytes 4194304 | tf_op jit(solution)/shard_map/sin | solution.py:60
  30.3 26.3 %psum.14 = f32[32,32]{1,0:T(8,128)S(1)} all-reduce(f32[32,32]{1,0:T(8,128)S(1)} %convolution_bitcast_fusion.2), channel_id=1, replica_groups=mesh['det'=8,'tm'=16] {'det'}, use_global_device_ids=true, to_apply=%region_0.1 | all-reduce | flops 1024 | bytes 8192 | tf_op jit(solution)/shard_map/psum | solution.py:64
  56.7 2.9 %cholesky.16 = f32[32,32]{1,0:T(8,128)S(1)} custom-call(f32[32,32]{1,0:T(8,128)S(1)} %fusion.30), custom_call_target="Cholesky" | custom-call | tf_op jit(solution)/shard_map/jit(cholesky)/cholesky | solution.py:65
  61.0 2.4 custom-call.10
  64.1 11.4 %all-reduce.6.cloned.1.call-done = f32[32,4096]{1,0:T(8,128)} async-done(((f32[32,4096]{1,0:T(8,128)}), f32[32,4096]{1,0:T(8,128)}) %all-reduce.6.cloned.1.call-update) | async-done | bytes 524304 | tf_op jit(solution)/shard_map/psum | solution.py:64
  75.5 1.8 fusion.28
  77.9 2.1 fusion.16
  80.1 3.9 %fusion.5 = f32[32,4096]{1,0:T(8,128)S(1)} fusion(f32[32,256]{1,0:T(8,128)S(1)} %fusion.16, f32[4096,128]{1,0:T(8,128)S(1)} %get-tuple-element.17, f32[4096,128]{1,0:T(8,128)S(1)} %copy-done), kind=kOutput, calls=%fused_computation.9 | convolution fusion | flops 403701760 | bytes 4751360 | tf_op jit(solution)/shard_map/dot_general | solution.py:68
  88.3 4.1 %fusion.2 = f32[1024,128]{1,0:T(8,128)S(1)} fusion(s32[1024]{0:T(1024)S(1)} %eq.120, f32[1024,128]{1,0:T(8,128)S(1)} %maximum_select_fusion.5, f32[1024,64]{1,0:T(8,128)S(1)} %get-tuple-element.5, f32[1024,64]{1,0:T(8,128)S(1)} %get-tuple-element.4, pred[1024]{0:T(1024)(128)(4,1)S(1)} %eq.125), kind=kOutput, calls=%fused_computation.6 | convolution fusion | flops 1611923456 | bytes 1577984 | tf_op jit(solution)/shard_map/dot_general | solution.py:84
  92.4 0.9 reshape.148
  93.4 2.8 %reduce-scatter.5.cloned.1.call-done = f32[64,128]{1,0:T(8,128)} async-done(((f32[64,2048]{1,0:T(8,128)}), f32[64,128]{1,0:T(8,128)}) %reduce-scatter.5.cloned.1.call-update) | async-done | bytes 32784 | tf_op jit(solution)/shard_map/reduce_scatter | solution.py:90
  96.2 74.8 %reduce-scatter.3.cloned.1.call-done = f32[64,128]{1,0:T(8,128)} async-done(((f32[64,2048]{1,0:T(8,128)}), f32[64,128]{1,0:T(8,128)}) %reduce-scatter.3.cloned.1.call-update) | async-done | bytes 32784 | tf_op jit(solution)/shard_map/reduce_scatter | solution.py:89
  172.2 57.0 %all-reduce.8.cloned.1.call-done = (f32[64,128]{1,0:T(8,128)}, f32[64,128]{1,0:T(8,128)}) async-done(((f32[64,128]{1,0:T(8,128)}, f32[64,128]{1,0:T(8,128)}), (f32[64,128]{1,0:T(8,128)}, f32[64,128]{1,0:T(8,128)})) %all-reduce.8.cloned.1.call-update) | async-done | bytes 65552
  229.2 0.7 fusion.44
  229.9 1.3 collective-permute-start
  231.2 1.3 collective-permute-start.1
  232.5 1.7 collective-permute-done.1
  234.3 3.4 %collective-permute-start.2 = (f32[14,3]{1,0:T(8,128)S(1)}, f32[14,3]{1,0:T(8,128)S(1)}, u32[]{:S(2)}, u32[]{:S(2)}) collective-permute-start(f32[14,3]{1,0:T(8,128)S(1)} %get-tuple-element.13), channel_id=1, source_target_pairs={{0,1},{1,2},{2,3},{3,4},{4,5},{5,6},{6,7},{7,8},{8,9},{9,10},{10,1... | collective-permute-start | bytes 512 | tf_op jit(solution)/shard_map/ppermute | solution.py:24
  237.7 1.3 collective-permute-start.3
  239.0 4.2 %collective-permute-done.3 = f32[14,3]{1,0:T(8,128)S(1)} collective-permute-done((f32[14,3]{1,0:T(8,128)S(1)}, f32[14,3]{1,0:T(8,128)S(1)}, u32[]{:S(2)}, u32[]{:S(2)}) %collective-permute-start.3) | collective-permute-done | bytes 200 | tf_op jit(solution)/shard_map/ppermute | solution.py:26
  (68 shorter events, 10.0 us)
Async XLA Ops:
  8.0 67.5 %all-reduce.6.cloned.1.call-start = ((), (), s32[]{:S(2)}) async-start(), calls=%async_computation.2 | async-start | bytes 1048576 | tf_op jit(solution)/shard_map/psum | solution.py:64
  11.2 9.8 %copy-start.3 = (f32[32,32]{1,0:T(8,128)S(1)}, f32[32,32]{1,0:T(8,128)}, u32[]{:S(2)}) copy-start(f32[32,32]{1,0:T(8,128)} %param.7) | copy-start | bytes 12292
  11.2 85.0 %reduce-scatter.5.cloned.1.call-start = ((), (), s32[]{:S(2)}) async-start(), calls=%async_computation.4 | async-start | bytes 557056 | tf_op jit(solution)/shard_map/reduce_scatter | solution.py:90
  20.9 150.0 %reduce-scatter.3.cloned.1.call-start = ((), (), s32[]{:S(2)}) async-start(), calls=%async_computation.3 | async-start | bytes 557056 | tf_op jit(solution)/shard_map/reduce_scatter | solution.py:89
  21.2 42.2 %copy-start.4 = (s32[32,32]{1,0:T(8,128)S(1)}, s32[32,32]{1,0:T(8,128)}, u32[]{:S(2)}) copy-start(s32[32,32]{1,0:T(8,128)} %param.11) | copy-start | bytes 12292
  75.5 2.4 copy-start
  80.0 3.9 %copy-start.1 = (f32[32,4096]{1,0:T(8,128)S(1)}, f32[32,4096]{1,0:T(8,128)}, u32[]{:S(2)}) copy-start(f32[32,4096]{1,0:T(8,128)} %param.6) | copy-start | bytes 1572868
  84.5 0.8 copy-start.2
  88.3 82.7 %copy-start.5 = (u32[128]{0:T(128)S(1)}, u32[128]{0:T(128)}, u32[]{:S(2)}) copy-start(u32[128]{0:T(128)} %constant.109) | copy-start | bytes 1540
  93.3 135.9 %all-reduce.8.cloned.1.call-start = ((), (), s32[]{:S(2)}) async-start(), calls=%async_computation.5 | async-start | bytes 131072
  229.9 2.6 %collective-permute-start = (f32[3,128]{1,0:T(4,128)S(1)}, f32[3,128]{1,0:T(4,128)S(1)}, u32[]{:S(2)}, u32[]{:S(2)}) collective-permute-start(f32[3,128]{1,0:T(4,128)S(1)} %get-tuple-element.15), channel_id=1, source_target_pairs={{0,16},{16,32},{32,48},{48,64},{64,80},{80,96},{96,112},{1,17},{17... | collective-permute-start | bytes 4616 | tf_op jit(solution)/shard_map/ppermute | solution.py:24
  231.2 3.1 %collective-permute-start.1 = (f32[3,128]{1,0:T(4,128)S(1)}, f32[3,128]{1,0:T(4,128)S(1)}, u32[]{:S(2)}, u32[]{:S(2)}) collective-permute-start(f32[3,128]{1,0:T(4,128)S(1)} %get-tuple-element.16), channel_id=1, source_target_pairs={{16,0},{32,16},{48,32},{64,48},{80,64},{96,80},{112,96},{17,1},{33... | collective-permute-start | bytes 4616 | tf_op jit(solution)/shard_map/ppermute | solution.py:26
  234.3 4.7 %collective-permute-start.2 = (f32[14,3]{1,0:T(8,128)S(1)}, f32[14,3]{1,0:T(8,128)S(1)}, u32[]{:S(2)}, u32[]{:S(2)}) collective-permute-start(f32[14,3]{1,0:T(8,128)S(1)} %get-tuple-element.13), channel_id=1, source_target_pairs={{0,1},{1,2},{2,3},{3,4},{4,5},{5,6},{6,7},{7,8},{8,9},{9,10},{10,1... | collective-permute-start | bytes 512 | tf_op jit(solution)/shard_map/ppermute | solution.py:24
  237.7 5.5 %collective-permute-start.3 = (f32[14,3]{1,0:T(8,128)S(1)}, f32[14,3]{1,0:T(8,128)S(1)}, u32[]{:S(2)}, u32[]{:S(2)}) collective-permute-start(f32[14,3]{1,0:T(8,128)S(1)} %get-tuple-element.14), channel_id=1, source_target_pairs={{1,0},{2,1},{3,2},{4,3},{5,4},{6,5},{7,6},{8,7},{9,8},{10,9},{11,1... | collective-permute-start | bytes 512 | tf_op jit(solution)/shard_map/ppermute | solution.py:26
Sparse Core Ops, SparseCore 0:
  11.7 63.7 all-reduce.5
  171.1 58.0 all-reduce.7
Sparse Core Ops, SparseCore 1:
  21.0 75.1 reduce-scatter.4
  99.2 71.7 reduce-scatter.2
where the time goes:
time: 255 us; the launch traced here: 251 us
  waiting for transfers between devices  152 us (60%)
  blocking collectives  26.3 us (10%)
  matrix products  23.3 us (9%)
  other arithmetic  20.7 us (8%)
  between operations  16.4 us (6%)
  starting transfers between devices  7.4 us (3%)
  local copies, waits for them, and re-layouts  5.3 us (2%)
    reduce_scatter x1, waiting for transfers between devices, body(): lax.psum_scatter(grid_sum, 'tm', scatter_dimension=1, tiled=True)  74.8 us
    unnamed x5, waiting for transfers between devices  57 us
    psum x1, blocking collectives, body(): mode_gram, summed = lax.psum((gram_part, projected), 'det')  26.3 us
    psum x1, waiting for transfers between devices, body(): mode_gram, summed = lax.psum((gram_part, projected), 'det')  11.4 us
    sin x1, other arithmetic, body(): basis = jnp.concatenate([jnp.cos(angle), jnp.sin(angle)], axis=1)  9.07 us
    dot_general x1, matrix products, body(): lax.dot_general(onehot, run_weight, (((0,), (0,)), ((), ())), precision=hp)  7.47 us
    ppermute x2, waiting for transfers between devices, extended(): lax.ppermute(head, axis, [((i + 1) % count, i) for i in range(ends)])  5.94 us
  transfers between devices with their start and end apart: 8, of which 6 were waited for; matrix products, arithmetic and copies ran while one was open for 18% of the time, Pallas kernels for 0%

commit v1 on v0

v1 whole, which is shorter than its diff:
```python
import math

import jax
import jax.numpy as jnp
import numpy as np
from jax import lax
from jax.experimental import pallas as pl
from jax.experimental.pallas import tpu as pltpu
from jax.sharding import Mesh
from jax.sharding import PartitionSpec as P
import ml_dtypes

SEG = 4096
NMODE = 32
FKEEP = 128
RUN = 128
TROWS = 64
TCOLS = 128
RADIUS = 3
DETS = 32
CHUNK = 256
NCHUNK = SEG // CHUNK
NRUNS = DETS * SEG // RUN
NT = 16
NY = 4
OWN = 8
BROWS = 16
NBLK = NY * NT
ZROWS = (TROWS // OWN + 1) * NT
BF = jnp.bfloat16
F32 = jnp.float32


def split_np(a):
    hi = a.astype(np.float32).astype(ml_dtypes.bfloat16)
    lo = (a - hi.astype(np.float64)).astype(np.float32).astype(ml_dtypes.bfloat16)
    return hi, lo


def tables():
    j = np.arange(CHUNK)[:, None]
    k = np.arange(FKEEP)[None, :]
    phi = 2.0 * np.pi * (j * k % SEG) / SEG
    basis = np.concatenate([np.cos(phi), np.sin(phi)], axis=1)
    c = np.arange(NCHUNK)[:, None]
    theta = 2.0 * np.pi * (c * CHUNK * k % SEG) / SEG
    twiddle = np.concatenate([np.cos(theta), np.sin(theta)], axis=1).astype(np.float32)
    scale = np.where(np.arange(FKEEP) == 0, 1.0 / SEG, 2.0 / SEG)
    synth = basis.T * np.concatenate([scale, scale])[:, None]
    return split_np(basis), split_np(synth), twiddle


def beam_taps():
    values = [math.exp(-(m * m) / 4.5) for m in range(-RADIUS, RADIUS + 1)]
    total = sum(values)
    return [v / total for v in values]


def split(a):
    hi = a.astype(BF)
    return hi, (a - hi.astype(F32)).astype(BF)


def mm(a, b):
    return jnp.dot(a, b, preferred_element_type=F32)


def mm0(a, b):
    return lax.dot_general(
        a, b, (((0,), (0,)), ((), ())), precision=lax.Precision.HIGHEST,
        preferred_element_type=F32,
    )


def column(row, n):
    full = jnp.broadcast_to(row, (n, row.shape[1]))
    same = lax.broadcasted_iota(jnp.int32, full.shape, 0) == lax.broadcasted_iota(
        jnp.int32, full.shape, 1
    )
    return jnp.sum(jnp.where(same, full, 0.0), axis=1, keepdims=True)


def analysis_kernel(x_ref, t_ref, v_ref, eh_ref, el_ref, tw_ref, out_ref):
    w = column(v_ref[...].astype(F32), DETS)
    x = jnp.concatenate(
        [x_ref[:, c * CHUNK : (c + 1) * CHUNK] for c in range(NCHUNK)], axis=0
    )
    hi, lo = split(x)
    y = mm(hi, eh_ref[...]) + mm(lo, eh_ref[...]) + mm(hi, el_ref[...])
    re = jnp.zeros((DETS, FKEEP), F32)
    im = jnp.zeros((DETS, FKEEP), F32)
    for c in range(NCHUNK):
        yc = y[c * DETS : (c + 1) * DETS, :FKEEP]
        ys = y[c * DETS : (c + 1) * DETS, FKEEP:]
        cos = tw_ref[c : c + 1, :FKEEP]
        sin = tw_ref[c : c + 1, FKEEP:]
        re = re + (cos * yc - sin * ys)
        im = im + (sin * yc + cos * ys)
    t = t_ref[...]
    wt = t * w
    out_ref[:, 0:FKEEP] = mm0(wt, re)
    out_ref[:, FKEEP : 2 * FKEEP] = mm0(wt, im)
    gram = mm0(wt, t)
    out_ref[:, 2 * FKEEP :] = jnp.concatenate(
        [gram, jnp.zeros((NMODE, FKEEP - NMODE), F32)], axis=1
    )


def edge_col(lane):
    slot = lane >> 3
    return jnp.where(slot < 3, TCOLS - RADIUS + slot, slot - 3)


def index_kernel(
    core_ref, line_ref, zid_ref, cs_ref, ro_ref, v_ref,
    send_ref, keep_ref, zhot_ref, idx_ref, edge_ref, mask_ref, zh_ref,
):
    line = line_ref[...]
    for which, ref in ((1, send_ref), (0, keep_ref)):
        core = core_ref[0] ^ which
        l = lax.broadcasted_iota(jnp.int32, (NBLK * BROWS, 128), 0)
        i = l & (BROWS - 1)
        b = l >> 4
        row = (b >> 4) * (2 * OWN) + core * OWN - RADIUS + i
        ok = (i < OWN + 2 * RADIUS) & (row >= 0) & (row < TROWS)
        ident = jnp.where(ok, (b & (NT - 1)) * TROWS + row, -1)
        for q in range(NRUNS // 128):
            hot = ident == line[:, q * 128 : (q + 1) * 128]
            ref[:, q * 128 : (q + 1) * 128] = jnp.where(hot, 1.0, 0.0).astype(BF)
    zl = lax.broadcasted_iota(jnp.int32, (ZROWS, NRUNS), 0)
    zhot = jnp.where(zl == zid_ref[...], 1.0, 0.0).astype(BF)
    zhot_ref[...] = zhot
    w = column(v_ref[...].astype(F32), DETS)
    lane = lax.broadcasted_iota(jnp.int32, (DETS, 128), 1)
    ecol = edge_col(lane)
    hparts = []
    for c in range(SEG // RUN):
        sl = slice(c * DETS, (c + 1) * DETS)
        cs = jnp.broadcast_to(cs_ref[:, c : c + 1], (DETS, 128))
        ro = jnp.broadcast_to(ro_ref[:, c : c + 1], (DETS, 128))
        idx_ref[sl, :] = (lane - cs) & (TCOLS - 1)
        edge_ref[sl, :] = (ecol - cs) & (TCOLS - 1)
        here = ((ro + RADIUS) & (OWN - 1)) == (lane & (OWN - 1))
        mask_ref[sl, :] = jnp.where(here & (lane < 48), 1.0, 0.0)
        hparts.append(jnp.where(here & (lane >= 48) & (lane < 56), w, 0.0).astype(BF))
    zh_ref[...] = mm(zhot, jnp.concatenate(hparts, axis=0))


def solve(gram, rhs):
    n = gram.shape[0]
    a = jnp.concatenate([gram, rhs], axis=1)
    rows = lax.broadcasted_iota(jnp.int32, a.shape, 0)
    for k in range(n):
        pivot = a[k : k + 1, :]
        pivot = pivot / a[k : k + 1, k : k + 1]
        a = jnp.where(rows == k, pivot, a - a[:, k : k + 1] * pivot)
    return a[:, n:]


def shifted_tiles(z, by):
    zero = jnp.zeros((z.shape[0], 1, 128), F32)
    if by < 0:
        return jnp.concatenate([zero, z[:, :-1]], axis=1)
    return jnp.concatenate([z[:, 1:], zero], axis=1)


def clean_kernel(
    core_ref, p_ref, q_ref, t_ref, v_ref, x_ref, sh_ref, sl_ref, tw_ref,
    idx_ref, edge_ref, mask_ref, zhot_ref, zh_ref, send_hot_ref,
    clean_ref, send_ref, vals_ref, rows_ref,
):
    w = column(v_ref[...].astype(F32), DETS)
    p = p_ref[...] + q_ref[...]
    eye = lax.broadcasted_iota(jnp.int32, (NMODE, NMODE), 0) == lax.broadcasted_iota(
        jnp.int32, (NMODE, NMODE), 1
    )
    gram = p[:, 2 * FKEEP : 2 * FKEEP + NMODE] + jnp.where(eye, 0.05, 0.0)
    coef = solve(gram, t_ref[...].T)
    a = mm0(coef, p[:, :FKEEP])
    b = mm0(coef, p[:, FKEEP : 2 * FKEEP])
    parts = []
    for c in range(NCHUNK):
        cos = tw_ref[c : c + 1, :FKEEP]
        sin = tw_ref[c : c + 1, FKEEP:]
        parts.append(jnp.concatenate([a * cos + b * sin, b * cos - a * sin], axis=1))
    hi, lo = split(jnp.concatenate(parts, axis=0))
    low = mm(hi, sh_ref[...]) + mm(lo, sh_ref[...]) + mm(hi, sl_ref[...])
    runs = []
    for c in range(NCHUNK):
        part = w * (x_ref[:, c * CHUNK : (c + 1) * CHUNK] - low[c * DETS : (c + 1) * DETS, :])
        clean_ref[:, c * CHUNK : (c + 1) * CHUNK] = part
        runs.append(part[:, :RUN])
        runs.append(part[:, RUN:])
    run = jnp.concatenate(runs, axis=0)
    vals = jnp.concatenate(
        split(jnp.take_along_axis(run, idx_ref[...], axis=1, mode="promise_in_bounds")), axis=1
    )
    vals_ref[...] = vals
    evals = jnp.take_along_axis(run, edge_ref[...], axis=1, mode="promise_in_bounds")
    evals = jnp.concatenate(split(evals * mask_ref[...]), axis=1)
    z = mm(zhot_ref[...], evals)
    z = (z[:, :128] + z[:, 128:] + zh_ref[...]).reshape(ZROWS // NT, NT, 128)
    left = shifted_tiles(z, -1)
    right = shifted_tiles(z, 1)
    lane = lax.broadcasted_iota(jnp.int32, z.shape, 2)
    left_hits = left
    right_hits = jnp.concatenate([jnp.zeros(z.shape[:2] + (8,), F32), right[:, :, :-8]], axis=2)
    near = jnp.where(
        lane < 24, left, jnp.where(lane < 48, right, jnp.where(lane < 56, left_hits, right_hits))
    )
    near = jnp.where(lane < 64, near, 0.0)
    mine = jnp.where((lane >= 48) & (lane < 56), z, 0.0)
    nd = TROWS // OWN

    def both(v):
        return v[:nd] + jnp.concatenate([jnp.zeros((nd, NT, 64), F32), v[1:, :, :64]], axis=2)

    rows14 = both(near)
    rows15 = both(mine)
    core = core_ref[0]

    def pick(v, which):
        return jnp.concatenate(
            [jnp.where(which == 1, v[2 * y + 1], v[2 * y]) for y in range(NY)], axis=0
        )

    rows_ref[0:NBLK, :] = pick(rows14, core)
    rows_ref[NBLK : 2 * NBLK, :] = pick(rows15, core)
    s = mm(send_hot_ref[...], vals)
    send_ref[...] = s[:, :128] + s[:, 128:]
    send_ref[pl.ds(14, NBLK, stride=BROWS), :] = pick(rows14, core ^ 1)
    send_ref[pl.ds(15, NBLK, stride=BROWS), :] = pick(rows15, core ^ 1)


def keep_kernel(hot_ref, vals_ref, rows_ref, keep_ref):
    s = mm(hot_ref[...], vals_ref[...])
    keep_ref[...] = s[:, :128] + s[:, 128:]
    keep_ref[pl.ds(14, NBLK, stride=BROWS), :] = rows_ref[0:NBLK, :]
    keep_ref[pl.ds(15, NBLK, stride=BROWS), :] = rows_ref[NBLK : 2 * NBLK, :]


def beam_kernel(blocks_ref, out_ref):
    total = blocks_ref[0:BROWS, :]
    for b in range(1, NBLK):
        total = total + blocks_ref[b * BROWS : (b + 1) * BROWS, :]
    near = jnp.broadcast_to(total[14:15, :], (BROWS, 128))
    mine = jnp.broadcast_to(total[15:16, :], (BROWS, 128))
    i = lax.broadcasted_iota(jnp.int32, (BROWS, 128), 0)
    lane = lax.broadcasted_iota(jnp.int32, (BROWS, 128), 1)
    spot = jnp.where(i < OWN, i, 64 + i - OWN)

    def take(src, slot):
        return jnp.sum(jnp.where(lane == spot + 8 * slot, src, 0.0), axis=1, keepdims=True)

    left_hits = take(near, 6) + 1.0
    right_hits = take(near, 7) + 1.0
    hits = take(mine, 6) + 1.0
    valid = i < OWN + 2 * RADIUS
    binned = jnp.where(valid, total / hits, 0.0)
    left = [take(near, m) / left_hits for m in range(RADIUS)]
    right = [take(near, RADIUS + m) / right_hits for m in range(RADIUS)]
    taps = beam_taps()
    smooth = taps[RADIUS] * binned
    for m in range(1, RADIUS + 1):
        moved = pltpu.roll(binned, m, 1)
        for q in range(m):
            moved = jnp.where(lane == q, left[RADIUS - m + q], moved)
        smooth = smooth + taps[RADIUS - m] * moved
        moved = pltpu.roll(binned, TCOLS - m, 1)
        for q in range(m):
            moved = jnp.where(lane == TCOLS - m + q, right[q], moved)
        smooth = smooth + taps[RADIUS + m] * moved
    out = taps[0] * smooth[0:OWN, :]
    for m in range(1, 2 * RADIUS + 1):
        out = out + taps[m] * smooth[m : m + OWN, :]
    out_ref[...] = out


VMEM = pl.BlockSpec(memory_space=pltpu.VMEM)
SMEM = pl.BlockSpec(memory_space=pltpu.SMEM)


def call(kernel, shapes, specs, name, flops, *args):
    nbytes = sum(math.prod(s.shape) * 4 for s in shapes) + sum(a.size * 4 for a in args)
    return pl.pallas_call(
        kernel,
        out_shape=shapes,
        in_specs=specs,
        out_specs=[VMEM] * len(shapes),
        name=name,
        compiler_params=pltpu.CompilerParams(vmem_limit_bytes=48 << 20),
        cost_estimate=pl.CostEstimate(flops=flops, bytes_accessed=nbytes, transcendentals=0),
    )(*args)


def sds(shape, dtype=F32):
    return jax.ShapeDtypeStruct(shape, dtype)


def body(timestreams, templates, validity, tile_index, row_offset, col_start):
    (eh, el), (sh, sl), tw = tables()
    eh, el, sh, sl, tw = (jnp.asarray(v) for v in (eh, el, sh, sl, tw))
    core = lax.axis_index("core").reshape(1)
    v_row = validity.reshape(1, DETS)
    (part,) = call(
        analysis_kernel, [sds((NMODE, 3 * FKEEP))], [VMEM] * 6, "analysis", 400_000_000,
        timestreams, templates, v_row, eh, el, tw,
    )
    part = part + lax.ppermute(part, "core", [(0, 1), (1, 0)])
    part = part + lax.ppermute(part, "y", [(k, k ^ 1) for k in range(NY)])
    other = lax.ppermute(part, "y", [(k, k ^ 2) for k in range(NY)])
    line = (tile_index * TROWS + row_offset).T.reshape(1, NRUNS)
    zid = (((row_offset + RADIUS) >> 3) * NT + tile_index).T.reshape(1, NRUNS)
    big = (NBLK * BROWS, NRUNS)
    send_hot, keep_hot, zhot, idx, edge, mask, zh = call(
        index_kernel,
        [
            sds(big, BF), sds(big, BF), sds((ZROWS, NRUNS), BF),
            sds((NRUNS, 128), jnp.int32), sds((NRUNS, 128), jnp.int32),
            sds((NRUNS, 128)), sds((ZROWS, 128)),
        ],
        [SMEM] + [VMEM] * 5, "index", 100_000_000,
        core, line, zid, col_start, row_offset, v_row,
    )
    cleaned, send, vals, rows = call(
        clean_kernel,
        [
            sds((DETS, SEG)), sds((NBLK * BROWS, 128)),
            sds((NRUNS, 256), BF), sds((2 * NBLK, 128)),
        ],
        [SMEM] + [VMEM] * 14, "clean", 1_000_000_000,
        core, part, other, templates, v_row, timestreams, sh, sl, tw,
        idx, edge, mask, zhot, zh, send_hot,
    )
    got = lax.ppermute(send, "core", [(0, 1), (1, 0)])
    (keep,) = call(
        keep_kernel, [sds((NBLK * BROWS, 128))], [VMEM] * 3, "keep", 500_000_000,
        keep_hot, vals, rows,
    )
    blocks = lax.all_to_all(keep + got, ("y", "z", "x"), 0, 0, tiled=True)
    (beamed,) = call(
        beam_kernel, [sds((OWN, TCOLS))], [VMEM], "beam", 1_000_000, blocks
    )
    return (cleaned, beamed)


def solution(mesh):
    fine = Mesh(mesh.devices.reshape(NY, 2, 4, 4), ("y", "core", "z", "x"))
    det, tm = ("y", "core"), ("z", "x")
    in_specs = (P(det, tm), P(det, None), P(det), P(det, tm), P(det, tm), P(det, tm))
    out_specs = (P(det, tm), P(det, tm))
    return jax.shard_map(body, mesh=fine, in_specs=in_specs, out_specs=out_specs, check_vma=False)
```

time: 255 us -> 52.1 us (0.20); the launches traced: 251 us -> 51.5 us
  waiting for transfers between devices: 152 us -> 4.84 us
  matrix products: 23.3 us -> 0 us
  other arithmetic: 20.7 us -> 0.81 us
  between operations: 16.4 us -> 0.75 us
  Pallas kernels: 0 us -> 9.72 us
  blocking collectives: 26.3 us -> 22.8 us
    reduce_scatter x2 -> x0, waiting for transfers between devices: 77.6 us -> none  [the longest x1 74.8 us: body(): lax.psum_scatter(grid_sum, 'tm', scatter_dimension=1, tiled=True)]
    unnamed x5 -> x0, waiting for transfers between devices: 57 us -> none
    psum x1 -> x0, blocking collectives: 26.3 us -> none  [body(): mode_gram, summed = lax.psum((gram_part, projected), 'det')]
    all_to_all x0 -> x1, blocking collectives: none -> 22.8 us  [body(): blocks = lax.all_to_all(keep + got, ('y', 'z', 'x'), 0, 0, tiled=True)]
    dot_general x7 -> x0, matrix products: 20.9 us -> none  [the longest x1 7.47 us: body(): lax.dot_general(onehot, run_weight, (((0,), (0,)), ((), ())), precision=hp)]
    psum x1 -> x0, waiting for transfers between devices: 11.4 us -> none  [body(): mode_gram, summed = lax.psum((gram_part, projected), 'det')]
    pallas_call x0 -> x5, Pallas kernels: none -> 9.72 us  [call(): pl.pallas_call(kernel, out_shape=shapes, in_specs=specs, out_specs=[VMEM]...]
    sin x1 -> x0, other arithmetic: 9.07 us -> none  [body(): basis = jnp.concatenate([jnp.cos(angle), jnp.sin(angle)], axis=1)]
  transfers between devices with their start and end apart: 8 -> 4, of which waited for: 6 -> 3; matrix products, arithmetic and copies ran while one was open for 18% -> 2% of each run, Pallas kernels for 0% -> 6%
where the time goes in v1:
time: 52.1 us; the launch traced here: 51.5 us
  blocking collectives  22.8 us (44%)
  Pallas kernels  9.72 us (19%)
  local copies, waits for them, and re-layouts  7.36 us (14%)
  starting transfers between devices  5.19 us (10%)
  waiting for transfers between devices  4.84 us (9%)
  other arithmetic  0.81 us (2%)
  between operations  0.75 us (1%)
    all_to_all x1, blocking collectives, body(): blocks = lax.all_to_all(keep + got, ('y', 'z', 'x'), 0, 0, tiled=True)  22.8 us
    pallas_call x5, Pallas kernels, call(): pl.pallas_call(kernel, out_shape=shapes, in_specs=specs, out_specs=[VMEM]...  9.72 us
    unnamed x28, local copies, waits for them, and re-layouts  7.05 us
    ppermute x1, starting transfers between devices, body(): other = lax.ppermute(part, 'y', [(k, k ^ 2) for k in range(NY)])  3.35 us
    ppermute x1, waiting for transfers between devices, body(): part = part + lax.ppermute(part, 'y', [(k, k ^ 1) for k in range(NY)])  2.44 us
    ppermute x1, starting transfers between devices, body(): part = part + lax.ppermute(part, 'y', [(k, k ^ 1) for k in range(NY)])  1.73 us
    ppermute x1, waiting for transfers between devices, body(): part = part + lax.ppermute(part, 'core', [(0, 1), (1, 0)])  1.22 us
    ppermute x1, waiting for transfers between devices, body(): got = lax.ppermute(send, 'core', [(0, 1), (1, 0)])  1.18 us
  transfers between devices with their start and end apart: 4, of which 3 were waited for; matrix products, arithmetic and copies ran while one was open for 2% of the time, Pallas kernels for 6%

profile of v1, /device:TPU:0, one launch (start us, length us, event | category | flops | bytes accessed | tf_op | source)
XLA Modules:
  0.0 51.5 jit_solution(4319232921336013327)
XLA Ops:
  0.6 1.0 %copy-done = f32[32,4096]{1,0:T(8,128)S(1)} copy-done((f32[32,4096]{1,0:T(8,128)S(1)}, f32[32,4096]{1,0:T(8,128)}, u32[]{:S(2)}) %copy-start) | copy-done | bytes 524312
  1.7 0.7 %copy-done.4 = f32[32,32]{1,0:T(8,128)S(1)} copy-done((f32[32,32]{1,0:T(8,128)S(1)}, f32[32,32]{1,0:T(8,128)}, u32[]{:S(2)}) %copy-start.4) | copy-done | bytes 4120
  2.4 0.7 %copy-done.6 = f32[16,256]{1,0:T(8,128)S(1)} copy-done((f32[16,256]{1,0:T(8,128)S(1)}, f32[16,256]{1,0:T(8,128)}, u32[]{:S(2)}) %copy-start.6) | copy-done | bytes 16408
  3.1 0.7 %copy-done.9 = s32[32]{0:T(128)S(1)} copy-done((s32[32]{0:T(128)S(1)}, s32[32]{0:T(128)}, u32[]{:S(2)}) %copy-start.9) | copy-done | bytes 152
  3.8 0.9 %copy-done.12 = bf16[256,256]{1,0:T(8,128)(2,1)S(1)} copy-done((bf16[256,256]{1,0:T(8,128)(2,1)S(1)}, bf16[256,256]{1,0:T(8,128)(2,1)}, u32[]{:S(2)}) %copy-start.12) | copy-done | bytes 131096
  4.7 0.9 %copy-done.13 = bf16[256,256]{1,0:T(8,128)(2,1)S(1)} copy-done((bf16[256,256]{1,0:T(8,128)(2,1)S(1)}, bf16[256,256]{1,0:T(8,128)(2,1)}, u32[]{:S(2)}) %copy-start.13) | copy-done | bytes 131096
  5.6 0.7 %analysis.1 = f32[32,384]{1,0:T(8,128)S(1)} custom-call(f32[32,4096]{1,0:T(8,128)S(1)} %copy-done, f32[32,32]{1,0:T(8,128)S(1)} %copy-done.4, s32[1,32]{1,0:T(1,128)S(1)} %bitcast.9, bf16[256,256]{1,0:T(8,128)(2,1)S(1)} %copy-done.13, bf16[256,256]{1,0:T(8,128)(2,1)S(1)} %copy-done.12, f32[16,256]{1,0:T(8,128)S(1)} %copy-done.6), custom_call_target="tpu_custom_call" | custom-call | flops 400000000 | bytes 1118336 | tf_op jit(solution)/shard_map/analysis/pallas_call | solution.py:285
  6.3 1.2 %collective-permute-done = f32[32,384]{1,0:T(8,128)S(1)} collective-permute-done((f32[32,384]{1,0:T(8,128)S(1)}, f32[32,384]{1,0:T(8,128)S(1)}, u32[]{:S(2)}, u32[]{:S(2)}) %collective-permute-start) | collective-permute-done | bytes 49184 | tf_op jit(solution)/shard_map/ppermute | solution.py:309
  7.5 1.7 %collective-permute-start.1 = (f32[32,384]{1,0:T(8,128)S(1)}, f32[32,384]{1,0:T(8,128)S(1)}, u32[]{:S(2)}, u32[]{:S(2)}) collective-permute-start(f32[32,384]{1,0:T(8,128)S(1)} %add.18), channel_id=1, source_target_pairs={{0,32},{32,0},{64,96},{96,64},{1,33},{33,1},{65,97},{97,65},{2,34}... | collective-permute-start | bytes 147464 | tf_op jit(solution)/shard_map/ppermute | solution.py:310
  9.3 2.4 %collective-permute-done.1 = f32[32,384]{1,0:T(8,128)S(1)} collective-permute-done((f32[32,384]{1,0:T(8,128)S(1)}, f32[32,384]{1,0:T(8,128)S(1)}, u32[]{:S(2)}, u32[]{:S(2)}) %collective-permute-start.1) | collective-permute-done | bytes 49184 | tf_op jit(solution)/shard_map/ppermute | solution.py:310
  11.7 3.3 %collective-permute-start.2 = (f32[32,384]{1,0:T(8,128)S(1)}, f32[32,384]{1,0:T(8,128)S(1)}, u32[]{:S(2)}, u32[]{:S(2)}) collective-permute-start(f32[32,384]{1,0:T(8,128)S(1)} %add.19.p_ref), channel_id=1, source_target_pairs={{0,64},{32,96},{64,0},{96,32},{1,65},{33,97},{65,1},{97,33},{2,66}... | collective-permute-start | bytes 147464 | tf_op jit(solution)/shard_map/ppermute | solution.py:311
  15.1 0.7 %add_bitcast_fusion = (s32[32,32]{0,1:T(8,128)S(1)}, s32[32,32]{0,1:T(8,128)S(1)}) fusion(s32[32,32]{1,0:T(8,128)} %param.14, s32[32,32]{1,0:T(8,128)} %ro_ref.1), kind=kLoop, calls=%fused_computation | loop fusion | flops 6144 | bytes 16384 | tf_op jit(solution)/shard_map/transpose | solution.py:313
  15.9 0.1 reshape.21.zid_ref
  16.0 0.1 reshape.20.line_ref
  16.1 0.7 %copy-done.8 = s32[32,32]{1,0:T(8,128)S(1)} copy-done((s32[32,32]{1,0:T(8,128)S(1)}, s32[32,32]{1,0:T(8,128)}, u32[]{:S(2)}) %copy-start.8) | copy-done | bytes 4120
  16.8 0.7 %copy-done.10 = s32[32]{0:T(128)S(1)} copy-done((s32[32]{0:T(128)S(1)}, s32[32]{0:T(128)}, u32[]{:S(2)}) %copy-start.10) | copy-done | bytes 152
  17.5 0.7 %copy-done.11 = s32[32,32]{1,0:T(8,128)S(1)} copy-done((s32[32,32]{1,0:T(8,128)S(1)}, s32[32,32]{1,0:T(8,128)}, u32[]{:S(2)}) %copy-start.11) | copy-done | bytes 4120
  18.2 2.6 %index.1 = (bf16[1024,1024]{1,0:T(8,128)(2,1)S(1)}, bf16[1024,1024]{1,0:T(8,128)(2,1)S(1)}, bf16[144,1024]{1,0:T(8,128)(2,1)S(1)}, s32[1024,128]{1,0:T(8,128)S(1...) custom-call(s32[1]{0:T(128)} %bitcast.core_ref, s32[1,1024]{1,0:T(1,128)S(1)} %reshape.20.line_ref, ...), custom_call_target="tpu_custom_call" | custom-call | flops 100000000 | bytes 10641540 | tf_op jit(solution)/shard_map/index/pallas_call | solution.py:285
  20.9 4.9 %clean.1 = (f32[32,4096]{1,0:T(8,128)}, f32[1024,128]{1,0:T(8,128)S(1)}, bf16[1024,256]{1,0:T(8,128)(2,1)S(1)}, f32[128,128]{1,0:T(8,128)S(1)}) custom-call(s32[1]{0:T(128)} %bitcast.core_ref, f32[32,384]{1,0:T(8,128)S(1)} %add.19.p_ref, f32[32,384]{1,0:T(8,128)S(1)} %collective-permute-done.2.q_ref, f32[32,32]{1,0:T(8,128)S(1)} %copy-done.5, ...), custom_call_target="tpu_custom_call" | custom-call | flops 1000000000 | bytes 9760900 | tf_op jit(solution)/shard_map/clean/pallas_call | solution.py:285
  25.8 0.1 collective-permute-start.3
  25.9 0.7 %keep.1 = f32[1024,128]{1,0:T(8,128)S(1)} custom-call(bf16[1024,1024]{1,0:T(8,128)(2,1)S(1)} %get-tuple-element.20.hot_ref, bf16[1024,256]{1,0:T(8,128)(2,1)S(1)} %get-tuple-element.21.vals_ref, f32[128,128]{1,0:T(8,128)S(1)} %get-tuple-element.22.rows_ref), custom_call_target="tpu_custom_call" | custom-call | flops 500000000 | bytes 5832704 | tf_op jit(solution)/shard_map/keep/pallas_call | solution.py:285
  26.6 1.2 %collective-permute-done.3 = f32[1024,128]{1,0:T(8,128)S(1)} collective-permute-done((f32[1024,128]{1,0:T(8,128)S(1)}, f32[1024,128]{1,0:T(8,128)S(1)}, u32[]{:S(2)}, u32[]{:S(2)}) %collective-permute-start.3) | collective-permute-done | bytes 524320 | tf_op jit(solution)/shard_map/ppermute | solution.py:335
  27.8 22.8 %all_to_all.11 = f32[64,16,128]{2,1,0:T(8,128)S(1)} all-to-all(f32[64,16,128]{2,1,0:T(8,128)S(1)} %bitcast.12), channel_id=1, replica_groups=mesh['y'=4,'core'=2,'z'=4,'x'=4] {'y','z','x'}, dimensions={0} | all-to-all | bytes 1048576 | tf_op jit(solution)/shard_map/all_to_all | solution.py:340
  50.7 0.8 %beam.1 = f32[8,128]{1,0:T(8,128)} custom-call(f32[1024,128]{1,0:T(8,128)S(1)} %bitcast.8), custom_call_target="tpu_custom_call" | custom-call | flops 1000000 | bytes 528384 | tf_op jit(solution)/shard_map/beam/pallas_call | solution.py:285
  (26 shorter events, 0.3 us)
Async XLA Ops:
  0.6 1.0 %copy-start = (f32[32,4096]{1,0:T(8,128)S(1)}, f32[32,4096]{1,0:T(8,128)}, u32[]{:S(2)}) copy-start(f32[32,4096]{1,0:T(8,128)} %x_ref.3) | copy-start | bytes 1572868
  1.7 0.7 %copy-start.4 = (f32[32,32]{1,0:T(8,128)S(1)}, f32[32,32]{1,0:T(8,128)}, u32[]{:S(2)}) copy-start(f32[32,32]{1,0:T(8,128)} %t_ref.3) | copy-start | bytes 12292
  2.4 0.7 %copy-start.6 = (f32[16,256]{1,0:T(8,128)S(1)}, f32[16,256]{1,0:T(8,128)}, u32[]{:S(2)}) copy-start(f32[16,256]{1,0:T(8,128)} %constant.26.clone.tw_ref) | copy-start | bytes 49156
  3.1 0.7 %copy-start.9 = (s32[32]{0:T(128)S(1)}, s32[32]{0:T(128)}, u32[]{:S(2)}) copy-start(s32[32]{0:T(128)} %param.13) | copy-start | bytes 388
  3.8 0.9 %copy-start.12 = (bf16[256,256]{1,0:T(8,128)(2,1)S(1)}, bf16[256,256]{1,0:T(8,128)(2,1)}, u32[]{:S(2)}) copy-start(bf16[256,256]{1,0:T(8,128)(2,1)} %constant.23.clone.el_ref) | copy-start | bytes 393220
  4.7 0.9 %copy-start.13 = (bf16[256,256]{1,0:T(8,128)(2,1)S(1)}, bf16[256,256]{1,0:T(8,128)(2,1)}, u32[]{:S(2)}) copy-start(bf16[256,256]{1,0:T(8,128)(2,1)} %constant.22.clone.eh_ref) | copy-start | bytes 393220
  5.6 15.3 %copy-start.1 = (f32[32,4096]{1,0:T(8,128)S(1)}, f32[32,4096]{1,0:T(8,128)}, u32[]{:S(2)}) copy-start(f32[32,4096]{1,0:T(8,128)} %x_ref.3) | copy-start | bytes 1572868
  5.6 15.3 %copy-start.2 = (bf16[256,256]{1,0:T(8,128)(2,1)S(1)}, bf16[256,256]{1,0:T(8,128)(2,1)}, u32[]{:S(2)}) copy-start(bf16[256,256]{1,0:T(8,128)(2,1)} %constant.25.clone.sl_ref) | copy-start | bytes 393220
  5.6 15.3 %copy-start.3 = (bf16[256,256]{1,0:T(8,128)(2,1)S(1)}, bf16[256,256]{1,0:T(8,128)(2,1)}, u32[]{:S(2)}) copy-start(bf16[256,256]{1,0:T(8,128)(2,1)} %constant.24.clone.sh_ref) | copy-start | bytes 393220
  5.6 15.3 %copy-start.5 = (f32[32,32]{1,0:T(8,128)S(1)}, f32[32,32]{1,0:T(8,128)}, u32[]{:S(2)}) copy-start(f32[32,32]{1,0:T(8,128)} %t_ref.3) | copy-start | bytes 12292
  5.6 15.3 %copy-start.7 = (f32[16,256]{1,0:T(8,128)S(1)}, f32[16,256]{1,0:T(8,128)}, u32[]{:S(2)}) copy-start(f32[16,256]{1,0:T(8,128)} %constant.26.clone.tw_ref) | copy-start | bytes 49156
  6.3 1.3 %collective-permute-start = (f32[32,384]{1,0:T(8,128)S(1)}, f32[32,384]{1,0:T(8,128)S(1)}, u32[]{:S(2)}, u32[]{:S(2)}) collective-permute-start(f32[32,384]{1,0:T(8,128)S(1)} %analysis.1), channel_id=1, source_target_pairs={{0,16},{16,0},{1,17},{17,1},{2,18},{18,2},{3,19},{19,3},{4,20},{20... | collective-permute-start | bytes 147464 | tf_op jit(solution)/shard_map/ppermute | solution.py:309
  7.5 4.2 %collective-permute-start.1 = (f32[32,384]{1,0:T(8,128)S(1)}, f32[32,384]{1,0:T(8,128)S(1)}, u32[]{:S(2)}, u32[]{:S(2)}) collective-permute-start(f32[32,384]{1,0:T(8,128)S(1)} %add.18), channel_id=1, source_target_pairs={{0,32},{32,0},{64,96},{96,64},{1,33},{33,1},{65,97},{97,65},{2,34}... | collective-permute-start | bytes 147464 | tf_op jit(solution)/shard_map/ppermute | solution.py:310
  11.7 9.1 %collective-permute-start.2 = (f32[32,384]{1,0:T(8,128)S(1)}, f32[32,384]{1,0:T(8,128)S(1)}, u32[]{:S(2)}, u32[]{:S(2)}) collective-permute-start(f32[32,384]{1,0:T(8,128)S(1)} %add.19.p_ref), channel_id=1, source_target_pairs={{0,64},{32,96},{64,0},{96,32},{1,65},{33,97},{65,1},{97,33},{2,66}... | collective-permute-start | bytes 147464 | tf_op jit(solution)/shard_map/ppermute | solution.py:311
  16.1 0.7 %copy-start.8 = (s32[32,32]{1,0:T(8,128)S(1)}, s32[32,32]{1,0:T(8,128)}, u32[]{:S(2)}) copy-start(s32[32,32]{1,0:T(8,128)} %ro_ref.1) | copy-start | bytes 12292
  16.8 0.7 %copy-start.10 = (s32[32]{0:T(128)S(1)}, s32[32]{0:T(128)}, u32[]{:S(2)}) copy-start(s32[32]{0:T(128)} %param.13) | copy-start | bytes 388
  17.5 0.7 %copy-start.11 = (s32[32,32]{1,0:T(8,128)S(1)}, s32[32,32]{1,0:T(8,128)}, u32[]{:S(2)}) copy-start(s32[32,32]{1,0:T(8,128)} %cs_ref.1) | copy-start | bytes 12292
  25.8 2.0 %collective-permute-start.3 = (f32[1024,128]{1,0:T(8,128)S(1)}, f32[1024,128]{1,0:T(8,128)S(1)}, u32[]{:S(2)}, u32[]{:S(2)}) collective-permute-start(f32[1024,128]{1,0:T(8,128)S(1)} %get-tuple-element.23), channel_id=1, source_target_pairs={{0,16},{16,0},{1,17},{17,1},{2,18},{18,2},{3,19},{19,3},{4,20},{20... | collective-permute-start | bytes 1572872 | tf_op jit(solution)/shard_map/ppermute | solution.py:335

commit v2 on v1

--- a/solution.py
+++ b/solution.py
@@ -47,7 +47,7 @@
     twiddle = np.concatenate([np.cos(theta), np.sin(theta)], axis=1).astype(np.float32)
     scale = np.where(np.arange(FKEEP) == 0, 1.0 / SEG, 2.0 / SEG)
     synth = basis.T * np.concatenate([scale, scale])[:, None]
-    return split_np(basis), split_np(synth), twiddle
+    return np.concatenate(split_np(basis)), np.concatenate(split_np(synth)), twiddle
 
 
 def beam_taps():
@@ -80,13 +80,42 @@
     return jnp.sum(jnp.where(same, full, 0.0), axis=1, keepdims=True)
 
 
-def analysis_kernel(x_ref, t_ref, v_ref, eh_ref, el_ref, tw_ref, out_ref):
+def analysis_kernel(
+    x_hbm, t_hbm, v_hbm, basis_hbm, synth_hbm, tw_hbm,
+    out_ref, x_ref, synth_ref, tw_ref, tt_ref, w_ref,
+    t_ref, v_ref, basis_ref, sems,
+):
+    copies = [
+        pltpu.make_async_copy(src, dst, sems.at[n])
+        for n, (src, dst) in enumerate(
+            (
+                (x_hbm, x_ref), (basis_hbm, basis_ref), (t_hbm, t_ref),
+                (v_hbm, v_ref), (tw_hbm, tw_ref), (synth_hbm, synth_ref),
+            )
+        )
+    ]
+    for copy in copies:
+        copy.start()
+    copies[2].wait()
+    copies[3].wait()
     w = column(v_ref[...].astype(F32), DETS)
+    t = t_ref[...]
+    wt = t * w
+    w_ref[...] = jnp.broadcast_to(w, (DETS, 128))
+    tt_ref[...] = t.T
+    gram = mm0(wt, t)
+    out_ref[:, 2 * FKEEP :] = jnp.concatenate(
+        [gram, jnp.zeros((NMODE, FKEEP - NMODE), F32)], axis=1
+    )
+    copies[0].wait()
+    copies[1].wait()
     x = jnp.concatenate(
         [x_ref[:, c * CHUNK : (c + 1) * CHUNK] for c in range(NCHUNK)], axis=0
     )
     hi, lo = split(x)
-    y = mm(hi, eh_ref[...]) + mm(lo, eh_ref[...]) + mm(hi, el_ref[...])
+    eh = basis_ref[:CHUNK, :]
+    y = mm(hi, eh) + mm(lo, eh) + mm(hi, basis_ref[CHUNK:, :])
+    copies[4].wait()
     re = jnp.zeros((DETS, FKEEP), F32)
     im = jnp.zeros((DETS, FKEEP), F32)
     for c in range(NCHUNK):
@@ -96,14 +125,9 @@
         sin = tw_ref[c : c + 1, FKEEP:]
         re = re + (cos * yc - sin * ys)
         im = im + (sin * yc + cos * ys)
-    t = t_ref[...]
-    wt = t * w
     out_ref[:, 0:FKEEP] = mm0(wt, re)
     out_ref[:, FKEEP : 2 * FKEEP] = mm0(wt, im)
-    gram = mm0(wt, t)
-    out_ref[:, 2 * FKEEP :] = jnp.concatenate(
-        [gram, jnp.zeros((NMODE, FKEEP - NMODE), F32)], axis=1
-    )
+    copies[5].wait()
 
 
 def edge_col(lane):
@@ -111,26 +135,56 @@
     return jnp.where(slot < 3, TCOLS - RADIUS + slot, slot - 3)
 
 
-def index_kernel(
-    core_ref, line_ref, zid_ref, cs_ref, ro_ref, v_ref,
-    send_ref, keep_ref, zhot_ref, idx_ref, edge_ref, mask_ref, zh_ref,
+def ids_of_blocks(core):
+    l = lax.broadcasted_iota(jnp.int32, (NBLK * BROWS, 128), 0)
+    i = l & (BROWS - 1)
+    b = l >> 4
+    row = (b >> 4) * (2 * OWN) + core * OWN - RADIUS + i
+    ok = (i < OWN + 2 * RADIUS) & (row >= 0) & (row < TROWS)
+    return jnp.where(ok, (b & (NT - 1)) * TROWS + row, -1)
+
+
+def run_row(ids):
+    flat = ids.astype(F32).T
+    parts = [flat[c : c + 1, :] for c in range(SEG // RUN)]
+    return jnp.concatenate(parts, axis=1).astype(jnp.int32)
+
+
+def fill_hot(ref, ids, line):
+    for q in range(NRUNS // 128):
+        sl = slice(q * 128, (q + 1) * 128)
+        ref[:, sl] = jnp.where(ids == line[:, sl], 1.0, 0.0).astype(BF)
+
+
+def first_index_kernel(
+    core_ref, ti_hbm, ro_hbm, cs_hbm,
+    send_ref, line_ref, zid_ref, ro_ref, cs_ref, ti_ref, sems,
 ):
-    line = line_ref[...]
-    for which, ref in ((1, send_ref), (0, keep_ref)):
-        core = core_ref[0] ^ which
-        l = lax.broadcasted_iota(jnp.int32, (NBLK * BROWS, 128), 0)
-        i = l & (BROWS - 1)
-        b = l >> 4
-        row = (b >> 4) * (2 * OWN) + core * OWN - RADIUS + i
-        ok = (i < OWN + 2 * RADIUS) & (row >= 0) & (row < TROWS)
-        ident = jnp.where(ok, (b & (NT - 1)) * TROWS + row, -1)
-        for q in range(NRUNS // 128):
-            hot = ident == line[:, q * 128 : (q + 1) * 128]
-            ref[:, q * 128 : (q + 1) * 128] = jnp.where(hot, 1.0, 0.0).astype(BF)
+    copies = [
+        pltpu.make_async_copy(src, dst, sems.at[n])
+        for n, (src, dst) in enumerate(((ti_hbm, ti_ref), (ro_hbm, ro_ref), (cs_hbm, cs_ref)))
+    ]
+    for copy in copies:
+        copy.start()
+    ids = ids_of_blocks(core_ref[0] ^ 1)
+    for copy in copies:
+        copy.wait()
+    ti = ti_ref[...]
+    ro = ro_ref[...]
+    line = run_row(ti * TROWS + ro)
+    line_ref[...] = line
+    zid_ref[...] = run_row(((ro + RADIUS) >> 3) * NT + ti)
+    fill_hot(send_ref, ids, line)
+
+
+def second_index_kernel(
+    core_ref, line_ref, zid_ref, ro_ref, cs_ref, w_ref,
+    keep_ref, zhot_ref, idx_ref, edge_ref, mask_ref, zh_ref,
+):
     zl = lax.broadcasted_iota(jnp.int32, (ZROWS, NRUNS), 0)
     zhot = jnp.where(zl == zid_ref[...], 1.0, 0.0).astype(BF)
     zhot_ref[...] = zhot
-    w = column(v_ref[...].astype(F32), DETS)
+    w = w_ref[...]
     lane = lax.broadcasted_iota(jnp.int32, (DETS, 128), 1)
     ecol = edge_col(lane)
     hparts = []
@@ -144,6 +198,7 @@
         mask_ref[sl, :] = jnp.where(here & (lane < 48), 1.0, 0.0)
         hparts.append(jnp.where(here & (lane >= 48) & (lane < 56), w, 0.0).astype(BF))
     zh_ref[...] = mm(zhot, jnp.concatenate(hparts, axis=0))
+    fill_hot(keep_ref, ids_of_blocks(core_ref[0]), line_ref[...])
 
 
 def solve(gram, rhs):
@@ -165,17 +220,18 @@
 
 
 def clean_kernel(
-    core_ref, p_ref, q_ref, t_ref, v_ref, x_ref, sh_ref, sl_ref, tw_ref,
+    core_ref, p_ref, q_ref, tt_ref, w_ref, x_ref, synth_ref, tw_ref,
     idx_ref, edge_ref, mask_ref, zhot_ref, zh_ref, send_hot_ref,
     clean_ref, send_ref, vals_ref, rows_ref,
 ):
-    w = column(v_ref[...].astype(F32), DETS)
+    w = w_ref[...]
+    w = jnp.concatenate([w, w], axis=1)
     p = p_ref[...] + q_ref[...]
     eye = lax.broadcasted_iota(jnp.int32, (NMODE, NMODE), 0) == lax.broadcasted_iota(
         jnp.int32, (NMODE, NMODE), 1
     )
     gram = p[:, 2 * FKEEP : 2 * FKEEP + NMODE] + jnp.where(eye, 0.05, 0.0)
-    coef = solve(gram, t_ref[...].T)
+    coef = solve(gram, tt_ref[...])
     a = mm0(coef, p[:, :FKEEP])
     b = mm0(coef, p[:, FKEEP : 2 * FKEEP])
     parts = []
@@ -184,7 +240,8 @@
         sin = tw_ref[c : c + 1, FKEEP:]
         parts.append(jnp.concatenate([a * cos + b * sin, b * cos - a * sin], axis=1))
     hi, lo = split(jnp.concatenate(parts, axis=0))
-    low = mm(hi, sh_ref[...]) + mm(lo, sh_ref[...]) + mm(hi, sl_ref[...])
+    sh = synth_ref[:CHUNK, :]
+    low = mm(hi, sh) + mm(lo, sh) + mm(hi, synth_ref[CHUNK:, :])
     runs = []
     for c in range(NCHUNK):
         part = w * (x_ref[:, c * CHUNK : (c + 1) * CHUNK] - low[c * DETS : (c + 1) * DETS, :])
@@ -232,11 +289,14 @@
     send_ref[pl.ds(15, NBLK, stride=BROWS), :] = pick(rows15, core ^ 1)
 
 
-def keep_kernel(hot_ref, vals_ref, rows_ref, keep_ref):
+def keep_kernel(hot_ref, vals_ref, rows_ref, clean_ref, keep_ref, out_hbm, sem):
+    copy = pltpu.make_async_copy(clean_ref, out_hbm, sem)
+    copy.start()
     s = mm(hot_ref[...], vals_ref[...])
     keep_ref[...] = s[:, :128] + s[:, 128:]
     keep_ref[pl.ds(14, NBLK, stride=BROWS), :] = rows_ref[0:NBLK, :]
     keep_ref[pl.ds(15, NBLK, stride=BROWS), :] = rows_ref[NBLK : 2 * NBLK, :]
+    copy.wait()
 
 
 def beam_kernel(blocks_ref, out_ref):
@@ -278,17 +338,23 @@
 
 VMEM = pl.BlockSpec(memory_space=pltpu.VMEM)
 SMEM = pl.BlockSpec(memory_space=pltpu.SMEM)
-
-
-def call(kernel, shapes, specs, name, flops, *args):
-    nbytes = sum(math.prod(s.shape) * 4 for s in shapes) + sum(a.size * 4 for a in args)
+HBM = pl.BlockSpec(memory_space=pltpu.HBM)
+
+
+def call(kernel, outs, specs, name, flops, *args, out_specs=None, scratch=()):
+    args = [
+        pltpu.with_memory_space_constraint(a, pltpu.HBM) if spec is HBM else a
+        for a, spec in zip(args, specs)
+    ]
+    nbytes = sum(math.prod(s.shape) * 4 for s in outs) + sum(a.size * 4 for a in args)
     return pl.pallas_call(
         kernel,
-        out_shape=shapes,
+        out_shape=outs,
         in_specs=specs,
-        out_specs=[VMEM] * len(shapes),
+        out_specs=out_specs or [VMEM] * len(outs),
+        scratch_shapes=list(scratch),
         name=name,
-        compiler_params=pltpu.CompilerParams(vmem_limit_bytes=48 << 20),
+        compiler_params=pltpu.CompilerParams(vmem_limit_bytes=40 << 20),
         cost_estimate=pl.CostEstimate(flops=flops, bytes_accessed=nbytes, transcendentals=0),
     )(*args)
 
@@ -297,30 +363,54 @@
     return jax.ShapeDtypeStruct(shape, dtype)
 
 
+I32 = jnp.int32
+
+
 def body(timestreams, templates, validity, tile_index, row_offset, col_start):
-    (eh, el), (sh, sl), tw = tables()
-    eh, el, sh, sl, tw = (jnp.asarray(v) for v in (eh, el, sh, sl, tw))
+    basis, synth, tw = tables()
     core = lax.axis_index("core").reshape(1)
-    v_row = validity.reshape(1, DETS)
-    (part,) = call(
-        analysis_kernel, [sds((NMODE, 3 * FKEEP))], [VMEM] * 6, "analysis", 400_000_000,
-        timestreams, templates, v_row, eh, el, tw,
+    part, x, synth, tw, tt, w = call(
+        analysis_kernel,
+        [
+            sds((NMODE, 3 * FKEEP)), sds((DETS, SEG)), sds((2 * CHUNK, 2 * FKEEP), BF),
+            sds((NCHUNK, 2 * FKEEP)), sds((NMODE, DETS)), sds((DETS, 128)),
+        ],
+        [HBM] * 6, "analysis", 400_000_000,
+        timestreams, templates, validity.reshape(1, DETS),
+        jnp.asarray(basis), jnp.asarray(synth), jnp.asarray(tw),
+        scratch=[
+            pltpu.VMEM((DETS, NMODE), F32), pltpu.VMEM((1, DETS), I32),
+            pltpu.VMEM((2 * CHUNK, 2 * FKEEP), BF), pltpu.SemaphoreType.DMA((6,)),
+        ],
     )
     part = part + lax.ppermute(part, "core", [(0, 1), (1, 0)])
-    part = part + lax.ppermute(part, "y", [(k, k ^ 1) for k in range(NY)])
+    tile_index, row_offset, col_start, part = lax.optimization_barrier(
+        (tile_index, row_offset, col_start, part)
+    )
+    other = lax.ppermute(part, "y", [(k, k ^ 1) for k in range(NY)])
+    big = (NBLK * BROWS, NRUNS)
+    send_hot, line, zid, ro, cs = call(
+        first_index_kernel,
+        [
+            sds(big, BF), sds((1, NRUNS), I32), sds((1, NRUNS), I32),
+            sds((DETS, SEG // RUN), I32), sds((DETS, SEG // RUN), I32),
+        ],
+        [SMEM] + [HBM] * 3, "index1", 100_000_000,
+        core, tile_index, row_offset, col_start,
+        scratch=[pltpu.VMEM((DETS, SEG // RUN), I32), pltpu.SemaphoreType.DMA((3,))],
+    )
+    part = part + other
+    part, line = lax.optimization_barrier((part, line))
     other = lax.ppermute(part, "y", [(k, k ^ 2) for k in range(NY)])
-    line = (tile_index * TROWS + row_offset).T.reshape(1, NRUNS)
-    zid = (((row_offset + RADIUS) >> 3) * NT + tile_index).T.reshape(1, NRUNS)
-    big = (NBLK * BROWS, NRUNS)
-    send_hot, keep_hot, zhot, idx, edge, mask, zh = call(
-        index_kernel,
+    keep_hot, zhot, idx, edge, mask, zh = call(
+        second_index_kernel,
         [
-            sds(big, BF), sds(big, BF), sds((ZROWS, NRUNS), BF),
-            sds((NRUNS, 128), jnp.int32), sds((NRUNS, 128), jnp.int32),
+            sds(big, BF), sds((ZROWS, NRUNS), BF),
+            sds((NRUNS, 128), I32), sds((NRUNS, 128), I32),
             sds((NRUNS, 128)), sds((ZROWS, 128)),
         ],
-        [SMEM] + [VMEM] * 5, "index", 100_000_000,
-        core, line, zid, col_start, row_offset, v_row,
+        [SMEM] + [VMEM] * 5, "index2", 100_000_000,
+        core, line, zid, ro, cs, w,
     )
     cleaned, send, vals, rows = call(
         clean_kernel,
@@ -328,14 +418,14 @@
             sds((DETS, SEG)), sds((NBLK * BROWS, 128)),
             sds((NRUNS, 256), BF), sds((2 * NBLK, 128)),
         ],
-        [SMEM] + [VMEM] * 14, "clean", 1_000_000_000,
-        core, part, other, templates, v_row, timestreams, sh, sl, tw,
-        idx, edge, mask, zhot, zh, send_hot,
+        [SMEM] + [VMEM] * 13, "clean", 1_000_000_000,
+        core, part, other, tt, w, x, synth, tw, idx, edge, mask, zhot, zh, send_hot,
     )
     got = lax.ppermute(send, "core", [(0, 1), (1, 0)])
-    (keep,) = call(
-        keep_kernel, [sds((NBLK * BROWS, 128))], [VMEM] * 3, "keep", 500_000_000,
-        keep_hot, vals, rows,
+    keep, cleaned = call(
+        keep_kernel, [sds((NBLK * BROWS, 128)), sds((DETS, SEG))], [VMEM] * 4, "keep",
+        500_000_000, keep_hot, vals, rows, cleaned,
+        out_specs=[VMEM, HBM], scratch=[pltpu.SemaphoreType.DMA],
     )
     blocks = lax.all_to_all(keep + got, ("y", "z", "x"), 0, 0, tiled=True)
     (beamed,) = call(

time: 52.1 us -> 46.8 us (0.90)
  local copies, waits for them, and re-layouts: 7.36 us -> 0 us
  blocking collectives: 22.8 us -> 25 us
  Pallas kernels: 9.72 us -> 11.8 us
  waiting for transfers between devices: 4.84 us -> 3.61 us
  other arithmetic: 0.81 us -> 0.09 us
    unnamed x28 -> x0, local copies, waits for them, and re-layouts: 7.05 us -> none
    all_to_all x1, blocking collectives: 22.8 us -> 25 us  [body(): blocks = lax.all_to_all(keep + got, ('y', 'z', 'x'), 0, 0, tiled=True)]
    pallas_call x5 -> x6, Pallas kernels: 9.72 us -> 11.8 us  [call(): pl.pallas_call(kernel, out_shape=outs, in_specs=specs, out_specs=out_spec...]
    ppermute x1, waiting for transfers between devices: 2.44 us -> 0.63 us  [body(): other = lax.ppermute(part, 'y', [(k, k ^ 1) for k in range(NY)])]
    transpose x1 -> x0, other arithmetic: 0.74 us -> none  [body(): zid = ((row_offset + RADIUS >> 3) * NT + tile_index).T.reshape(1, NRUNS)]
    ppermute x1, waiting for transfers between devices: 0.01 us -> 0.69 us  [body(): other = lax.ppermute(part, 'y', [(k, k ^ 2) for k in range(NY)])]
  transfers between devices with their start and end apart: 4 -> 4, of which waited for: 3 -> 4; matrix products, arithmetic and copies ran while one was open for 2% -> 0% of each run, Pallas kernels for 6% -> 9%
where the time goes in v2:
time: 46.8 us; the launch traced here: 46.5 us
  blocking collectives  25 us (53%)
  Pallas kernels  11.8 us (25%)
  starting transfers between devices  5.27 us (11%)
  waiting for transfers between devices  3.61 us (8%)
  between operations  0.69 us (1%)
    all_to_all x1, blocking collectives, body(): blocks = lax.all_to_all(keep + got, ('y', 'z', 'x'), 0, 0, tiled=True)  25 us
    pallas_call x6, Pallas kernels, call(): pl.pallas_call(kernel, out_shape=outs, in_specs=specs, out_specs=out_spec...  11.8 us
    ppermute x1, starting transfers between devices, body(): other = lax.ppermute(part, 'y', [(k, k ^ 2) for k in range(NY)])  3.36 us
    ppermute x1, starting transfers between devices, body(): other = lax.ppermute(part, 'y', [(k, k ^ 1) for k in range(NY)])  1.74 us
    ppermute x1, waiting for transfers between devices, body(): part = part + lax.ppermute(part, 'core', [(0, 1), (1, 0)])  1.22 us
    ppermute x1, waiting for transfers between devices, body(): got = lax.ppermute(send, 'core', [(0, 1), (1, 0)])  1.08 us
  transfers between devices with their start and end apart: 4, of which 4 were waited for; matrix products, arithmetic and copies ran while one was open for 0% of the time, Pallas kernels for 9%

profile of v2, /device:TPU:0, one launch (start us, length us, event | category | flops | bytes accessed | tf_op | source)
XLA Modules:
  0.0 46.5 jit_solution(15439697151401223003)
XLA Ops:
  0.6 2.0 %analysis.1 = (f32[32,384]{1,0:T(8,128)S(1)}, f32[32,4096]{1,0:T(8,128)S(1)}, bf16[512,256]{1,0:T(8,128)(2,1)S(1)}, f32[16,256]{1,0:T(8,128)S(1)}, f32[32,32]{1,0:T(8,128)S(1)}, /*index=5*/f32[32,128]{1,0:T(8,128)S(1)}) custom-call(f32[32,4096]{1,0:T(8,128)} %x_hbm.1, f32[32,32]{1,0:T(8,128)} %t_hbm.1, s32[1,32]{1,0:T(1,128)} %bitcast.6, ...), custom_call_target="tpu_custom_call" | custom-call | flops 400000000 | bytes 2728064 | tf_op jit(solution)/shard_map/analysis/pallas_call | solution.py:350
  2.6 0.1 collective-permute-start
  2.7 1.2 %collective-permute-done = f32[32,384]{1,0:T(8,128)S(1)} collective-permute-done((f32[32,384]{1,0:T(8,128)S(1)}, f32[32,384]{1,0:T(8,128)S(1)}, u32[]{:S(2)}, u32[]{:S(2)}) %collective-permute-start) | collective-permute-done | bytes 49184 | tf_op jit(solution)/shard_map/ppermute | solution.py:386
  4.0 1.7 %collective-permute-start.1 = (f32[32,384]{1,0:T(8,128)S(1)}, f32[32,384]{1,0:T(8,128)S(1)}, u32[]{:S(2)}, u32[]{:S(2)}) collective-permute-start(f32[32,384]{1,0:T(8,128)S(1)} %add.9), channel_id=1, source_target_pairs={{0,32},{32,0},{64,96},{96,64},{1,33},{33,1},{65,97},{97,65},{2,34}... | collective-permute-start | bytes 147464 | tf_op jit(solution)/shard_map/ppermute | solution.py:390
  5.7 1.8 %index1.1 = (bf16[1024,1024]{1,0:T(8,128)(2,1)S(1)}, s32[1,1024]{1,0:T(1,128)S(1)}, s32[1,1024]{1,0:T(1,128)S(1)}, s32[32,32]{1,0:T(8,128)S(1)}, s32[32,32]{1,0:T(8,128)S(1)}) custom-call(s32[1]{0:T(128)} %bitcast.core_ref, s32[32,32]{1,0:T(8,128)} %ti_hbm, s32[32,32]{1,0:T(8,128)} %ro_hbm, s32[32,32]{1,0:T(8,128)} %cs_hbm), custom_call_target="tpu_custom_call" | custom-call | flops 100000000 | bytes 4222980 | tf_op jit(solution)/shard_map/index1/pallas_call | solution.py:350
  7.5 0.6 %collective-permute-done.1 = f32[32,384]{1,0:T(8,128)S(1)} collective-permute-done((f32[32,384]{1,0:T(8,128)S(1)}, f32[32,384]{1,0:T(8,128)S(1)}, u32[]{:S(2)}, u32[]{:S(2)}) %collective-permute-start.1) | collective-permute-done | bytes 49184 | tf_op jit(solution)/shard_map/ppermute | solution.py:390
  8.2 3.4 %collective-permute-start.2 = (f32[32,384]{1,0:T(8,128)S(1)}, f32[32,384]{1,0:T(8,128)S(1)}, u32[]{:S(2)}, u32[]{:S(2)}) collective-permute-start(f32[32,384]{1,0:T(8,128)S(1)} %add.10.p_ref), channel_id=1, source_target_pairs={{0,64},{32,96},{64,0},{96,32},{1,65},{33,97},{65,1},{97,33},{2,66}... | collective-permute-start | bytes 147464 | tf_op jit(solution)/shard_map/ppermute | solution.py:404
  11.5 1.6 %index2.1 = (bf16[1024,1024]{1,0:T(8,128)(2,1)S(1)}, bf16[144,1024]{1,0:T(8,128)(2,1)S(1)}, s32[1024,128]{1,0:T(8,128)S(1)}, s32[1024,128]{1,0:T(8,128)S(1)}, f3...) custom-call(s32[1]{0:T(128)} %bitcast.core_ref, s32[1,1024]{1,0:T(1,128)S(1)} %get-tuple-element.37.line_ref, ...), custom_call_target="tpu_custom_call" | custom-call | flops 100000000 | bytes 6463492 | tf_op jit(solution)/shard_map/index2/pallas_call | solution.py:350
  13.1 0.7 %collective-permute-done.2.q_ref = f32[32,384]{1,0:T(8,128)S(1)} collective-permute-done((f32[32,384]{1,0:T(8,128)S(1)}, f32[32,384]{1,0:T(8,128)S(1)}, u32[]{:S(2)}, u32[]{:S(2)}) %collective-permute-start.2) | collective-permute-done | bytes 49184 | tf_op jit(solution)/shard_map/ppermute | solution.py:404
  13.8 4.7 %clean.1 = (f32[32,4096]{1,0:T(8,128)S(1)}, f32[1024,128]{1,0:T(8,128)S(1)}, bf16[1024,256]{1,0:T(8,128)(2,1)S(1)}, f32[128,128]{1,0:T(8,128)S(1)}) custom-call(s32[1]{0:T(128)} %bitcast.core_ref, f32[32,384]{1,0:T(8,128)S(1)} %add.10.p_ref, f32[32,384]{1,0:T(8,128)S(1)} %collective-permute-done.2.q_ref, f32[32,32]{1,0:T(8,128)S(1)} %get-tuple-element.44.tt_ref, ...), custom_call_target="tpu_custom_call" | custom-call | flops 1000000000 | bytes 9777156 | tf_op jit(solution)/shard_map/clean/pallas_call | solution.py:350
  18.6 0.1 collective-permute-start.3
  18.7 0.8 %keep.1 = (f32[1024,128]{1,0:T(8,128)S(1)}, f32[32,4096]{1,0:T(8,128)}) custom-call(bf16[1024,1024]{1,0:T(8,128)(2,1)S(1)} %get-tuple-element.42.hot_ref, bf16[1024,256]{1,0:T(8,128)(2,1)S(1)} %get-tuple-element.54.vals_ref, f32[128,128]{1,0:T(8,128)S(1)} %get-tuple-element.55.rows_ref, f32[32,4096]{1,0:T(8,128)S(1)} %get-tuple-element.56.clean_ref), custom_call_target="tpu_custom_call" | custom-call | flops 500000000 | bytes 6881280 | tf_op jit(solution)/shard_map/keep/pallas_call | solution.py:350
  19.5 1.1 %collective-permute-done.3 = f32[1024,128]{1,0:T(8,128)S(1)} collective-permute-done((f32[1024,128]{1,0:T(8,128)S(1)}, f32[1024,128]{1,0:T(8,128)S(1)}, u32[]{:S(2)}, u32[]{:S(2)}) %collective-permute-start.3) | collective-permute-done | bytes 524320 | tf_op jit(solution)/shard_map/ppermute | solution.py:424
  20.6 0.1 add.11
  20.6 25.0 %all_to_all.11 = f32[64,16,128]{2,1,0:T(8,128)S(1)} all-to-all(f32[64,16,128]{2,1,0:T(8,128)S(1)} %bitcast.5), channel_id=1, replica_groups=mesh['y'=4,'core'=2,'z'=4,'x'=4] {'y','z','x'}, dimensions={0} | all-to-all | bytes 1048576 | tf_op jit(solution)/shard_map/all_to_all | solution.py:430
  45.7 0.8 %beam.1 = f32[8,128]{1,0:T(8,128)} custom-call(f32[1024,128]{1,0:T(8,128)S(1)} %bitcast.4), custom_call_target="tpu_custom_call" | custom-call | flops 1000000 | bytes 528384 | tf_op jit(solution)/shard_map/beam/pallas_call | solution.py:350
  (2 shorter events, 0.0 us)
Async XLA Ops:
  2.6 1.3 %collective-permute-start = (f32[32,384]{1,0:T(8,128)S(1)}, f32[32,384]{1,0:T(8,128)S(1)}, u32[]{:S(2)}, u32[]{:S(2)}) collective-permute-start(f32[32,384]{1,0:T(8,128)S(1)} %get-tuple-element.31), channel_id=1, source_target_pairs={{0,16},{16,0},{1,17},{17,1},{2,18},{18,2},{3,19},{19,3},{4,20},{20... | collective-permute-start | bytes 147464 | tf_op jit(solution)/shard_map/ppermute | solution.py:386
  4.0 4.2 %collective-permute-start.1 = (f32[32,384]{1,0:T(8,128)S(1)}, f32[32,384]{1,0:T(8,128)S(1)}, u32[]{:S(2)}, u32[]{:S(2)}) collective-permute-start(f32[32,384]{1,0:T(8,128)S(1)} %add.9), channel_id=1, source_target_pairs={{0,32},{32,0},{64,96},{96,64},{1,33},{33,1},{65,97},{97,65},{2,34}... | collective-permute-start | bytes 147464 | tf_op jit(solution)/shard_map/ppermute | solution.py:390
  8.2 5.7 %collective-permute-start.2 = (f32[32,384]{1,0:T(8,128)S(1)}, f32[32,384]{1,0:T(8,128)S(1)}, u32[]{:S(2)}, u32[]{:S(2)}) collective-permute-start(f32[32,384]{1,0:T(8,128)S(1)} %add.10.p_ref), channel_id=1, source_target_pairs={{0,64},{32,96},{64,0},{96,32},{1,65},{33,97},{65,1},{97,33},{2,66}... | collective-permute-start | bytes 147464 | tf_op jit(solution)/shard_map/ppermute | solution.py:404
  18.6 2.0 %collective-permute-start.3 = (f32[1024,128]{1,0:T(8,128)S(1)}, f32[1024,128]{1,0:T(8,128)S(1)}, u32[]{:S(2)}, u32[]{:S(2)}) collective-permute-start(f32[1024,128]{1,0:T(8,128)S(1)} %get-tuple-element.59), channel_id=1, source_target_pairs={{0,16},{16,0},{1,17},{17,1},{2,18},{18,2},{3,19},{19,3},{4,20},{20... | collective-permute-start | bytes 1572872 | tf_op jit(solution)/shard_map/ppermute | solution.py:424

commit v3 on v2

--- a/solution.py
+++ b/solution.py
@@ -69,6 +69,15 @@
     return lax.dot_general(
         a, b, (((0,), (0,)), ((), ())), precision=lax.Precision.HIGHEST,
         preferred_element_type=F32,
+    )
+
+
+def mm0_split(a, b):
+    ah, al = split(a)
+    bh, bl = split(b)
+    return lax.dot_general(
+        jnp.concatenate([ah, al, ah], axis=0), jnp.concatenate([bh, bh, bl], axis=0),
+        (((0,), (0,)), ((), ())), preferred_element_type=F32,
     )
 
 
@@ -125,8 +134,7 @@
         sin = tw_ref[c : c + 1, FKEEP:]
         re = re + (cos * yc - sin * ys)
         im = im + (sin * yc + cos * ys)
-    out_ref[:, 0:FKEEP] = mm0(wt, re)
-    out_ref[:, FKEEP : 2 * FKEEP] = mm0(wt, im)
+    out_ref[:, : 2 * FKEEP] = mm0_split(wt, jnp.concatenate([re, im], axis=1))
     copies[5].wait()
 
 
@@ -201,15 +209,55 @@
     fill_hot(keep_ref, ids_of_blocks(core_ref[0]), line_ref[...])
 
 
+def lanes_of(v, k):
+    return jnp.broadcast_to(v[:, k : k + 1], (8, 128))
+
+
+def row_of(v, r):
+    return jnp.broadcast_to(v[r : r + 1, :], (8, 128))
+
+
 def solve(gram, rhs):
     n = gram.shape[0]
-    a = jnp.concatenate([gram, rhs], axis=1)
-    rows = lax.broadcasted_iota(jnp.int32, a.shape, 0)
-    for k in range(n):
-        pivot = a[k : k + 1, :]
-        pivot = pivot / a[k : k + 1, k : k + 1]
-        a = jnp.where(rows == k, pivot, a - a[:, k : k + 1] * pivot)
-    return a[:, n:]
+    eye = lax.broadcasted_iota(jnp.int32, gram.shape, 0) == lax.broadcasted_iota(
+        jnp.int32, gram.shape, 1
+    )
+    diag = jnp.where(eye, gram, 0.0)
+    down = lax.rsqrt(jnp.sum(diag, axis=1, keepdims=True))
+    along = lax.rsqrt(jnp.sum(diag, axis=0, keepdims=True))
+    full = jnp.concatenate(
+        [gram * down * along, rhs * down, jnp.zeros((n, 128 - 2 * n), F32)], axis=1
+    )
+    a = [full[8 * i : 8 * i + 8, :] for i in range(n // 8)]
+    sub = lax.broadcasted_iota(jnp.int32, (8, 128), 0)
+    for k in range(0, n, 4):
+        here, r = k // 8, k % 8
+        c = [[lanes_of(v, k + j) for v in a] for j in range(4)]
+        p = [[row_of(c[j][here], r + i) for j in range(4)] for i in range(4)]
+        rows = [row_of(a[here], r + i) for i in range(4)]
+        i1 = 1.0 / (p[0][0] * p[1][1] - p[0][1] * p[0][1])
+        e00, e01, e11 = p[1][1] * i1, -p[0][1] * i1, p[0][0] * i1
+        w00 = e00 * p[0][2] + e01 * p[1][2]
+        w01 = e00 * p[0][3] + e01 * p[1][3]
+        w10 = e01 * p[0][2] + e11 * p[1][2]
+        w11 = e01 * p[0][3] + e11 * p[1][3]
+        s00 = p[2][2] - (p[0][2] * w00 + p[1][2] * w10)
+        s01 = p[2][3] - (p[0][2] * w01 + p[1][2] * w11)
+        s11 = p[3][3] - (p[0][3] * w01 + p[1][3] * w11)
+        i2 = 1.0 / (s00 * s11 - s01 * s01)
+        y0 = e00 * rows[0] + e01 * rows[1]
+        y1 = e01 * rows[0] + e11 * rows[1]
+        q2 = rows[2] - (p[0][2] * y0 + p[1][2] * y1)
+        q3 = rows[3] - (p[0][3] * y0 + p[1][3] * y1)
+        n2 = (s11 * q2 - s01 * q3) * i2
+        n3 = (s00 * q3 - s01 * q2) * i2
+        n0 = y0 - (w00 * n2 + w01 * n3)
+        n1 = y1 - (w10 * n2 + w11 * n3)
+        for i in range(n // 8):
+            a[i] = a[i] - ((c[0][i] * n0 + c[1][i] * n1) + (c[2][i] * n2 + c[3][i] * n3))
+        for j, new in enumerate((n0, n1, n2, n3)):
+            a[here] = jnp.where(sub == r + j, new, a[here])
+    return jnp.concatenate(a, axis=0)[:, n : 2 * n] * down
 
 
 def shifted_tiles(z, by):
@@ -232,8 +280,9 @@
     )
     gram = p[:, 2 * FKEEP : 2 * FKEEP + NMODE] + jnp.where(eye, 0.05, 0.0)
     coef = solve(gram, tt_ref[...])
-    a = mm0(coef, p[:, :FKEEP])
-    b = mm0(coef, p[:, FKEEP : 2 * FKEEP])
+    ab = mm0_split(coef, p[:, : 2 * FKEEP])
+    a = ab[:, :FKEEP]
+    b = ab[:, FKEEP:]
     parts = []
     for c in range(NCHUNK):
         cos = tw_ref[c : c + 1, :FKEEP]
@@ -300,9 +349,10 @@
 
 
 def beam_kernel(blocks_ref, out_ref):
-    total = blocks_ref[0:BROWS, :]
-    for b in range(1, NBLK):
-        total = total + blocks_ref[b * BROWS : (b + 1) * BROWS, :]
+    sums = [blocks_ref[b * BROWS : (b + 1) * BROWS, :] for b in range(4)]
+    for b in range(4, NBLK):
+        sums[b % 4] = sums[b % 4] + blocks_ref[b * BROWS : (b + 1) * BROWS, :]
+    total = (sums[0] + sums[1]) + (sums[2] + sums[3])
     near = jnp.broadcast_to(total[14:15, :], (BROWS, 128))
     mine = jnp.broadcast_to(total[15:16, :], (BROWS, 128))
     i = lax.broadcasted_iota(jnp.int32, (BROWS, 128), 0)
@@ -401,7 +451,7 @@
     )
     part = part + other
     part, line = lax.optimization_barrier((part, line))
-    other = lax.ppermute(part, "y", [(k, k ^ 2) for k in range(NY)])
+    other = lax.ppermute(part, "y", [(k, k ^ 3) for k in range(NY)])
     keep_hot, zhot, idx, edge, mask, zh = call(
         second_index_kernel,
         [

time: 46.8 us -> 45 us (0.962)
  Pallas kernels: 11.8 us -> 10.5 us
    pallas_call x6, Pallas kernels: 11.8 us -> 10.5 us  [call(): pl.pallas_call(kernel, out_shape=outs, in_specs=specs, out_specs=out_spec...]
where the time goes in v3:
time: 45 us; the launch traced here: 44.8 us
  blocking collectives  24.9 us (55%)
  Pallas kernels  10.5 us (23%)
  starting transfers between devices  5.1 us (11%)
  waiting for transfers between devices  3.48 us (8%)
  between operations  0.69 us (2%)
    all_to_all x1, blocking collectives, body(): blocks = lax.all_to_all(keep + got, ('y', 'z', 'x'), 0, 0, tiled=True)  24.9 us
    pallas_call x6, Pallas kernels, call(): pl.pallas_call(kernel, out_shape=outs, in_specs=specs, out_specs=out_spec...  10.5 us
    ppermute x1, starting transfers between devices, body(): other = lax.ppermute(part, 'y', [(k, k ^ 3) for k in range(NY)])  3.18 us
    ppermute x1, starting transfers between devices, body(): other = lax.ppermute(part, 'y', [(k, k ^ 1) for k in range(NY)])  1.75 us
    ppermute x1, waiting for transfers between devices, body(): part = part + lax.ppermute(part, 'core', [(0, 1), (1, 0)])  1.22 us
    ppermute x1, waiting for transfers between devices, body(): got = lax.ppermute(send, 'core', [(0, 1), (1, 0)])  1.08 us
  transfers between devices with their start and end apart: 4, of which 4 were waited for; matrix products, arithmetic and copies ran while one was open for 0% of the time, Pallas kernels for 9%

profile of v3, /device:TPU:0, one launch (start us, length us, event | category | flops | bytes accessed | tf_op | source)
XLA Modules:
  0.0 44.8 jit_solution(14134876947053862875)
XLA Ops:
  0.6 1.9 %analysis.1 = (f32[32,384]{1,0:T(8,128)S(1)}, f32[32,4096]{1,0:T(8,128)S(1)}, bf16[512,256]{1,0:T(8,128)(2,1)S(1)}, f32[16,256]{1,0:T(8,128)S(1)}, f32[32,32]{1,0:T(8,128)S(1)}, /*index=5*/f32[32,128]{1,0:T(8,128)S(1)}) custom-call(f32[32,4096]{1,0:T(8,128)} %x_hbm.1, f32[32,32]{1,0:T(8,128)} %t_hbm.1, s32[1,32]{1,0:T(1,128)} %bitcast.6, ...), custom_call_target="tpu_custom_call" | custom-call | flops 400000000 | bytes 2728064 | tf_op jit(solution)/shard_map/analysis/pallas_call | solution.py:400
  2.6 0.1 collective-permute-start
  2.7 1.2 %collective-permute-done = f32[32,384]{1,0:T(8,128)S(1)} collective-permute-done((f32[32,384]{1,0:T(8,128)S(1)}, f32[32,384]{1,0:T(8,128)S(1)}, u32[]{:S(2)}, u32[]{:S(2)}) %collective-permute-start) | collective-permute-done | bytes 49184 | tf_op jit(solution)/shard_map/ppermute | solution.py:436
  3.9 1.7 %collective-permute-start.1 = (f32[32,384]{1,0:T(8,128)S(1)}, f32[32,384]{1,0:T(8,128)S(1)}, u32[]{:S(2)}, u32[]{:S(2)}) collective-permute-start(f32[32,384]{1,0:T(8,128)S(1)} %add.9), channel_id=1, source_target_pairs={{0,32},{32,0},{64,96},{96,64},{1,33},{33,1},{65,97},{97,65},{2,34}... | collective-permute-start | bytes 147464 | tf_op jit(solution)/shard_map/ppermute | solution.py:440
  5.6 1.8 %index1.1 = (bf16[1024,1024]{1,0:T(8,128)(2,1)S(1)}, s32[1,1024]{1,0:T(1,128)S(1)}, s32[1,1024]{1,0:T(1,128)S(1)}, s32[32,32]{1,0:T(8,128)S(1)}, s32[32,32]{1,0:T(8,128)S(1)}) custom-call(s32[1]{0:T(128)} %bitcast.core_ref, s32[32,32]{1,0:T(8,128)} %ti_hbm, s32[32,32]{1,0:T(8,128)} %ro_hbm, s32[32,32]{1,0:T(8,128)} %cs_hbm), custom_call_target="tpu_custom_call" | custom-call | flops 100000000 | bytes 4222980 | tf_op jit(solution)/shard_map/index1/pallas_call | solution.py:400
  7.4 0.6 %collective-permute-done.1 = f32[32,384]{1,0:T(8,128)S(1)} collective-permute-done((f32[32,384]{1,0:T(8,128)S(1)}, f32[32,384]{1,0:T(8,128)S(1)}, u32[]{:S(2)}, u32[]{:S(2)}) %collective-permute-start.1) | collective-permute-done | bytes 49184 | tf_op jit(solution)/shard_map/ppermute | solution.py:440
  8.1 3.2 %collective-permute-start.2 = (f32[32,384]{1,0:T(8,128)S(1)}, f32[32,384]{1,0:T(8,128)S(1)}, u32[]{:S(2)}, u32[]{:S(2)}) collective-permute-start(f32[32,384]{1,0:T(8,128)S(1)} %add.10.p_ref), channel_id=1, source_target_pairs={{0,96},{32,64},{64,32},{96,0},{1,97},{33,65},{65,33},{97,1},{2,98}... | collective-permute-start | bytes 147464 | tf_op jit(solution)/shard_map/ppermute | solution.py:454
  11.3 1.6 %index2.1 = (bf16[1024,1024]{1,0:T(8,128)(2,1)S(1)}, bf16[144,1024]{1,0:T(8,128)(2,1)S(1)}, s32[1024,128]{1,0:T(8,128)S(1)}, s32[1024,128]{1,0:T(8,128)S(1)}, f3...) custom-call(s32[1]{0:T(128)} %bitcast.core_ref, s32[1,1024]{1,0:T(1,128)S(1)} %get-tuple-element.37.line_ref, ...), custom_call_target="tpu_custom_call" | custom-call | flops 100000000 | bytes 6463492 | tf_op jit(solution)/shard_map/index2/pallas_call | solution.py:400
  12.9 0.6 %collective-permute-done.2.q_ref = f32[32,384]{1,0:T(8,128)S(1)} collective-permute-done((f32[32,384]{1,0:T(8,128)S(1)}, f32[32,384]{1,0:T(8,128)S(1)}, u32[]{:S(2)}, u32[]{:S(2)}) %collective-permute-start.2) | collective-permute-done | bytes 49184 | tf_op jit(solution)/shard_map/ppermute | solution.py:454
  13.5 3.6 %clean.1 = (f32[32,4096]{1,0:T(8,128)S(1)}, f32[1024,128]{1,0:T(8,128)S(1)}, bf16[1024,256]{1,0:T(8,128)(2,1)S(1)}, f32[128,128]{1,0:T(8,128)S(1)}) custom-call(s32[1]{0:T(128)} %bitcast.core_ref, f32[32,384]{1,0:T(8,128)S(1)} %add.10.p_ref, f32[32,384]{1,0:T(8,128)S(1)} %collective-permute-done.2.q_ref, f32[32,32]{1,0:T(8,128)S(1)} %get-tuple-element.44.tt_ref, ...), custom_call_target="tpu_custom_call" | custom-call | flops 1000000000 | bytes 9777156 | tf_op jit(solution)/shard_map/clean/pallas_call | solution.py:400
  17.0 0.1 collective-permute-start.3
  17.1 0.8 %keep.1 = (f32[1024,128]{1,0:T(8,128)S(1)}, f32[32,4096]{1,0:T(8,128)}) custom-call(bf16[1024,1024]{1,0:T(8,128)(2,1)S(1)} %get-tuple-element.42.hot_ref, bf16[1024,256]{1,0:T(8,128)(2,1)S(1)} %get-tuple-element.54.vals_ref, f32[128,128]{1,0:T(8,128)S(1)} %get-tuple-element.55.rows_ref, f32[32,4096]{1,0:T(8,128)S(1)} %get-tuple-element.56.clean_ref), custom_call_target="tpu_custom_call" | custom-call | flops 500000000 | bytes 6881280 | tf_op jit(solution)/shard_map/keep/pallas_call | solution.py:400
  17.9 1.1 %collective-permute-done.3 = f32[1024,128]{1,0:T(8,128)S(1)} collective-permute-done((f32[1024,128]{1,0:T(8,128)S(1)}, f32[1024,128]{1,0:T(8,128)S(1)}, u32[]{:S(2)}, u32[]{:S(2)}) %collective-permute-start.3) | collective-permute-done | bytes 524320 | tf_op jit(solution)/shard_map/ppermute | solution.py:474
  19.0 0.1 add.11
  19.1 24.9 %all_to_all.11 = f32[64,16,128]{2,1,0:T(8,128)S(1)} all-to-all(f32[64,16,128]{2,1,0:T(8,128)S(1)} %bitcast.5), channel_id=1, replica_groups=mesh['y'=4,'core'=2,'z'=4,'x'=4] {'y','z','x'}, dimensions={0} | all-to-all | bytes 1048576 | tf_op jit(solution)/shard_map/all_to_all | solution.py:480
  44.0 0.8 %beam.1 = f32[8,128]{1,0:T(8,128)} custom-call(f32[1024,128]{1,0:T(8,128)S(1)} %bitcast.4), custom_call_target="tpu_custom_call" | custom-call | flops 1000000 | bytes 528384 | tf_op jit(solution)/shard_map/beam/pallas_call | solution.py:400
  (2 shorter events, 0.0 us)
Async XLA Ops:
  2.6 1.3 %collective-permute-start = (f32[32,384]{1,0:T(8,128)S(1)}, f32[32,384]{1,0:T(8,128)S(1)}, u32[]{:S(2)}, u32[]{:S(2)}) collective-permute-start(f32[32,384]{1,0:T(8,128)S(1)} %get-tuple-element.31), channel_id=1, source_target_pairs={{0,16},{16,0},{1,17},{17,1},{2,18},{18,2},{3,19},{19,3},{4,20},{20... | collective-permute-start | bytes 147464 | tf_op jit(solution)/shard_map/ppermute | solution.py:436
  3.9 4.2 %collective-permute-start.1 = (f32[32,384]{1,0:T(8,128)S(1)}, f32[32,384]{1,0:T(8,128)S(1)}, u32[]{:S(2)}, u32[]{:S(2)}) collective-permute-start(f32[32,384]{1,0:T(8,128)S(1)} %add.9), channel_id=1, source_target_pairs={{0,32},{32,0},{64,96},{96,64},{1,33},{33,1},{65,97},{97,65},{2,34}... | collective-permute-start | bytes 147464 | tf_op jit(solution)/shard_map/ppermute | solution.py:440
  8.1 5.4 %collective-permute-start.2 = (f32[32,384]{1,0:T(8,128)S(1)}, f32[32,384]{1,0:T(8,128)S(1)}, u32[]{:S(2)}, u32[]{:S(2)}) collective-permute-start(f32[32,384]{1,0:T(8,128)S(1)} %add.10.p_ref), channel_id=1, source_target_pairs={{0,96},{32,64},{64,32},{96,0},{1,97},{33,65},{65,33},{97,1},{2,98}... | collective-permute-start | bytes 147464 | tf_op jit(solution)/shard_map/ppermute | solution.py:454
  17.0 2.0 %collective-permute-start.3 = (f32[1024,128]{1,0:T(8,128)S(1)}, f32[1024,128]{1,0:T(8,128)S(1)}, u32[]{:S(2)}, u32[]{:S(2)}) collective-permute-start(f32[1024,128]{1,0:T(8,128)S(1)} %get-tuple-element.59), channel_id=1, source_target_pairs={{0,16},{16,0},{1,17},{17,1},{2,18},{18,2},{3,19},{19,3},{4,20},{20... | collective-permute-start | bytes 1572872 | tf_op jit(solution)/shard_map/ppermute | solution.py:474

commit v4 on v3

--- a/solution.py
+++ b/solution.py
@@ -20,6 +20,7 @@
 DETS = 32
 CHUNK = 256
 NCHUNK = SEG // CHUNK
+XPIECE = 1024
 NRUNS = DETS * SEG // RUN
 NT = 16
 NY = 4
@@ -94,19 +95,23 @@
     out_ref, x_ref, synth_ref, tw_ref, tt_ref, w_ref,
     t_ref, v_ref, basis_ref, sems,
 ):
+    pieces = [
+        (x_hbm.at[:, pl.ds(n * XPIECE, XPIECE)], x_ref.at[:, pl.ds(n * XPIECE, XPIECE)])
+        for n in range(SEG // XPIECE)
+    ]
     copies = [
         pltpu.make_async_copy(src, dst, sems.at[n])
         for n, (src, dst) in enumerate(
-            (
-                (x_hbm, x_ref), (basis_hbm, basis_ref), (t_hbm, t_ref),
-                (v_hbm, v_ref), (tw_hbm, tw_ref), (synth_hbm, synth_ref),
-            )
+            [
+                (t_hbm, t_ref), (v_hbm, v_ref), (basis_hbm, basis_ref), *pieces,
+                (tw_hbm, tw_ref), (synth_hbm, synth_ref),
+            ]
         )
     ]
     for copy in copies:
         copy.start()
-    copies[2].wait()
-    copies[3].wait()
+    copies[0].wait()
+    copies[1].wait()
     w = column(v_ref[...].astype(F32), DETS)
     t = t_ref[...]
     wt = t * w
@@ -116,26 +121,31 @@
     out_ref[:, 2 * FKEEP :] = jnp.concatenate(
         [gram, jnp.zeros((NMODE, FKEEP - NMODE), F32)], axis=1
     )
-    copies[0].wait()
-    copies[1].wait()
-    x = jnp.concatenate(
-        [x_ref[:, c * CHUNK : (c + 1) * CHUNK] for c in range(NCHUNK)], axis=0
-    )
-    hi, lo = split(x)
+    copies[2].wait()
     eh = basis_ref[:CHUNK, :]
-    y = mm(hi, eh) + mm(lo, eh) + mm(hi, basis_ref[CHUNK:, :])
-    copies[4].wait()
+    el = basis_ref[CHUNK:, :]
+    ys = []
+    per = XPIECE // CHUNK
+    for n in range(SEG // XPIECE):
+        copies[3 + n].wait()
+        x = jnp.concatenate(
+            [x_ref[:, c * CHUNK : (c + 1) * CHUNK] for c in range(n * per, (n + 1) * per)], axis=0
+        )
+        hi, lo = split(x)
+        ys.append(mm(hi, eh) + mm(lo, eh) + mm(hi, el))
+    copies[-2].wait()
     re = jnp.zeros((DETS, FKEEP), F32)
     im = jnp.zeros((DETS, FKEEP), F32)
     for c in range(NCHUNK):
-        yc = y[c * DETS : (c + 1) * DETS, :FKEEP]
-        ys = y[c * DETS : (c + 1) * DETS, FKEEP:]
+        sl = slice(c % per * DETS, (c % per + 1) * DETS)
+        yc = ys[c // per][sl, :FKEEP]
+        yi = ys[c // per][sl, FKEEP:]
         cos = tw_ref[c : c + 1, :FKEEP]
         sin = tw_ref[c : c + 1, FKEEP:]
-        re = re + (cos * yc - sin * ys)
-        im = im + (sin * yc + cos * ys)
+        re = re + (cos * yc - sin * yi)
+        im = im + (sin * yc + cos * yi)
     out_ref[:, : 2 * FKEEP] = mm0_split(wt, jnp.concatenate([re, im], axis=1))
-    copies[5].wait()
+    copies[-1].wait()
 
 
 def edge_col(lane):
@@ -268,13 +278,13 @@
 
 
 def clean_kernel(
-    core_ref, p_ref, q_ref, tt_ref, w_ref, x_ref, synth_ref, tw_ref,
+    core_ref, p_ref, q_ref, r_ref, s_ref, tt_ref, w_ref, x_ref, synth_ref, tw_ref,
     idx_ref, edge_ref, mask_ref, zhot_ref, zh_ref, send_hot_ref,
     clean_ref, send_ref, vals_ref, rows_ref,
 ):
     w = w_ref[...]
     w = jnp.concatenate([w, w], axis=1)
-    p = p_ref[...] + q_ref[...]
+    p = (p_ref[...] + q_ref[...]) + (r_ref[...] + s_ref[...])
     eye = lax.broadcasted_iota(jnp.int32, (NMODE, NMODE), 0) == lax.broadcasted_iota(
         jnp.int32, (NMODE, NMODE), 1
     )
@@ -430,14 +440,14 @@
         jnp.asarray(basis), jnp.asarray(synth), jnp.asarray(tw),
         scratch=[
             pltpu.VMEM((DETS, NMODE), F32), pltpu.VMEM((1, DETS), I32),
-            pltpu.VMEM((2 * CHUNK, 2 * FKEEP), BF), pltpu.SemaphoreType.DMA((6,)),
+            pltpu.VMEM((2 * CHUNK, 2 * FKEEP), BF), pltpu.SemaphoreType.DMA((5 + SEG // XPIECE,)),
         ],
     )
     part = part + lax.ppermute(part, "core", [(0, 1), (1, 0)])
     tile_index, row_offset, col_start, part = lax.optimization_barrier(
         (tile_index, row_offset, col_start, part)
     )
-    other = lax.ppermute(part, "y", [(k, k ^ 1) for k in range(NY)])
+    others = [lax.ppermute(part, "y", [(k, k ^ m) for k in range(NY)]) for m in (2, 3, 1)]
     big = (NBLK * BROWS, NRUNS)
     send_hot, line, zid, ro, cs = call(
         first_index_kernel,
@@ -449,9 +459,6 @@
         core, tile_index, row_offset, col_start,
         scratch=[pltpu.VMEM((DETS, SEG // RUN), I32), pltpu.SemaphoreType.DMA((3,))],
     )
-    part = part + other
-    part, line = lax.optimization_barrier((part, line))
-    other = lax.ppermute(part, "y", [(k, k ^ 3) for k in range(NY)])
     keep_hot, zhot, idx, edge, mask, zh = call(
         second_index_kernel,
         [
@@ -468,8 +475,8 @@
             sds((DETS, SEG)), sds((NBLK * BROWS, 128)),
             sds((NRUNS, 256), BF), sds((2 * NBLK, 128)),
         ],
-        [SMEM] + [VMEM] * 13, "clean", 1_000_000_000,
-        core, part, other, tt, w, x, synth, tw, idx, edge, mask, zhot, zh, send_hot,
+        [SMEM] + [VMEM] * 15, "clean", 1_000_000_000,
+        core, part, *others, tt, w, x, synth, tw, idx, edge, mask, zhot, zh, send_hot,
     )
     got = lax.ppermute(send, "core", [(0, 1), (1, 0)])
     keep, cleaned = call(

time: 45 us -> 44.4 us (0.987)
  starting transfers between devices: 5.1 us -> 4.58 us
    ppermute x2 -> x3, starting transfers between devices: 4.93 us -> 4.41 us  [body(): lax.ppermute(part, 'y', [(k, k ^ m) for k in range(NY)])]
    ppermute x2 -> x3, waiting for transfers between devices: 1.19 us -> 0.8 us  [body(): lax.ppermute(part, 'y', [(k, k ^ m) for k in range(NY)])]
  transfers between devices with their start and end apart: 4 -> 5, of which waited for: 4 -> 3; matrix products, arithmetic and copies ran while one was open for 0% -> 0% of each run, Pallas kernels for 9% -> 10%
where the time goes in v4:
time: 44.4 us; the launch traced here: 44 us
  blocking collectives  24.6 us (55%)
  Pallas kernels  10.9 us (25%)
  starting transfers between devices  4.58 us (10%)
  waiting for transfers between devices  3.1 us (7%)
  between operations  0.69 us (2%)
    all_to_all x1, blocking collectives, body(): blocks = lax.all_to_all(keep + got, ('y', 'z', 'x'), 0, 0, tiled=True)  24.6 us
    pallas_call x6, Pallas kernels, call(): pl.pallas_call(kernel, out_shape=outs, in_specs=specs, out_specs=out_spec...  10.9 us
    ppermute x3, starting transfers between devices, body(): lax.ppermute(part, 'y', [(k, k ^ m) for k in range(NY)])  4.41 us
    ppermute x1, waiting for transfers between devices, body(): part = part + lax.ppermute(part, 'core', [(0, 1), (1, 0)])  1.22 us
    ppermute x1, waiting for transfers between devices, body(): got = lax.ppermute(send, 'core', [(0, 1), (1, 0)])  1.08 us
  transfers between devices with their start and end apart: 5, of which 3 were waited for; matrix products, arithmetic and copies ran while one was open for 0% of the time, Pallas kernels for 10%

profile of v4, /device:TPU:0, one launch (start us, length us, event | category | flops | bytes accessed | tf_op | source)
XLA Modules:
  0.0 44.0 jit_solution(15189145555470970463)
XLA Ops:
  0.6 2.3 %analysis.1 = (f32[32,384]{1,0:T(8,128)S(1)}, f32[32,4096]{1,0:T(8,128)S(1)}, bf16[512,256]{1,0:T(8,128)(2,1)S(1)}, f32[16,256]{1,0:T(8,128)S(1)}, f32[32,32]{1,0:T(8,128)S(1)}, /*index=5*/f32[32,128]{1,0:T(8,128)S(1)}) custom-call(f32[32,4096]{1,0:T(8,128)} %x_hbm.1, f32[32,32]{1,0:T(8,128)} %t_hbm.1, s32[1,32]{1,0:T(1,128)} %bitcast.6, ...), custom_call_target="tpu_custom_call" | custom-call | flops 400000000 | bytes 2728064 | tf_op jit(solution)/shard_map/analysis/pallas_call | solution.py:410
  3.0 0.1 collective-permute-start
  3.1 1.2 %collective-permute-done = f32[32,384]{1,0:T(8,128)S(1)} collective-permute-done((f32[32,384]{1,0:T(8,128)S(1)}, f32[32,384]{1,0:T(8,128)S(1)}, u32[]{:S(2)}, u32[]{:S(2)}) %collective-permute-start) | collective-permute-done | bytes 49184 | tf_op jit(solution)/shard_map/ppermute | solution.py:446
  4.3 3.4 %collective-permute-start.1 = (f32[32,384]{1,0:T(8,128)S(1)}, f32[32,384]{1,0:T(8,128)S(1)}, u32[]{:S(2)}, u32[]{:S(2)}) collective-permute-start(f32[32,384]{1,0:T(8,128)S(1)} %add.6.p_ref), channel_id=1, source_target_pairs={{0,64},{32,96},{64,0},{96,32},{1,65},{33,97},{65,1},{97,33},{2,66}... | collective-permute-start | bytes 147464 | tf_op jit(solution)/shard_map/ppermute | solution.py:450
  7.6 1.1 %collective-permute-start.2 = (f32[32,384]{1,0:T(8,128)S(1)}, f32[32,384]{1,0:T(8,128)S(1)}, u32[]{:S(2)}, u32[]{:S(2)}) collective-permute-start(f32[32,384]{1,0:T(8,128)S(1)} %add.6.p_ref), channel_id=1, source_target_pairs={{0,96},{32,64},{64,32},{96,0},{1,97},{33,65},{65,33},{97,1},{2,98}... | collective-permute-start | bytes 147464 | tf_op jit(solution)/shard_map/ppermute | solution.py:450
  8.7 0.0 collective-permute-start.3
  8.7 1.8 %index1.1 = (bf16[1024,1024]{1,0:T(8,128)(2,1)S(1)}, s32[1,1024]{1,0:T(1,128)S(1)}, s32[1,1024]{1,0:T(1,128)S(1)}, s32[32,32]{1,0:T(8,128)S(1)}, s32[32,32]{1,0:T(8,128)S(1)}) custom-call(s32[1]{0:T(128)} %bitcast.core_ref, s32[32,32]{1,0:T(8,128)} %ti_hbm, s32[32,32]{1,0:T(8,128)} %ro_hbm, s32[32,32]{1,0:T(8,128)} %cs_hbm), custom_call_target="tpu_custom_call" | custom-call | flops 100000000 | bytes 4222980 | tf_op jit(solution)/shard_map/index1/pallas_call | solution.py:410
  10.5 1.6 %index2.1 = (bf16[1024,1024]{1,0:T(8,128)(2,1)S(1)}, bf16[144,1024]{1,0:T(8,128)(2,1)S(1)}, s32[1024,128]{1,0:T(8,128)S(1)}, s32[1024,128]{1,0:T(8,128)S(1)}, f3...) custom-call(s32[1]{0:T(128)} %bitcast.core_ref, s32[1,1024]{1,0:T(1,128)S(1)} %get-tuple-element.33.line_ref, ...), custom_call_target="tpu_custom_call" | custom-call | flops 100000000 | bytes 6463492 | tf_op jit(solution)/shard_map/index2/pallas_call | solution.py:410
  12.1 0.0 collective-permute-done.1.q_ref
  12.1 0.8 %collective-permute-done.2.r_ref = f32[32,384]{1,0:T(8,128)S(1)} collective-permute-done((f32[32,384]{1,0:T(8,128)S(1)}, f32[32,384]{1,0:T(8,128)S(1)}, u32[]{:S(2)}, u32[]{:S(2)}) %collective-permute-start.2) | collective-permute-done | bytes 49184 | tf_op jit(solution)/shard_map/ppermute | solution.py:450
  12.9 0.0 collective-permute-done.3.s_ref
  12.9 3.6 %clean.1 = (f32[32,4096]{1,0:T(8,128)S(1)}, f32[1024,128]{1,0:T(8,128)S(1)}, bf16[1024,256]{1,0:T(8,128)(2,1)S(1)}, f32[128,128]{1,0:T(8,128)S(1)}) custom-call(s32[1]{0:T(128)} %bitcast.core_ref, f32[32,384]{1,0:T(8,128)S(1)} %add.6.p_ref, f32[32,384]{1,0:T(8,128)S(1)} %collective-permute-done.1.q_ref, f32[32,384]{1,0:T(8,128)S(1)} %collective-permute-done.2.r_ref, ...), custom_call_target="tpu_custom_call" | custom-call | flops 1000000000 | bytes 9875460 | tf_op jit(solution)/shard_map/clean/pallas_call | solution.py:410
  16.5 0.1 collective-permute-start.4
  16.6 0.8 %keep.1 = (f32[1024,128]{1,0:T(8,128)S(1)}, f32[32,4096]{1,0:T(8,128)}) custom-call(bf16[1024,1024]{1,0:T(8,128)(2,1)S(1)} %get-tuple-element.38.hot_ref, bf16[1024,256]{1,0:T(8,128)(2,1)S(1)} %get-tuple-element.50.vals_ref, f32[128,128]{1,0:T(8,128)S(1)} %get-tuple-element.51.rows_ref, f32[32,4096]{1,0:T(8,128)S(1)} %get-tuple-element.52.clean_ref), custom_call_target="tpu_custom_call" | custom-call | flops 500000000 | bytes 6881280 | tf_op jit(solution)/shard_map/keep/pallas_call | solution.py:410
  17.4 1.1 %collective-permute-done.4 = f32[1024,128]{1,0:T(8,128)S(1)} collective-permute-done((f32[1024,128]{1,0:T(8,128)S(1)}, f32[1024,128]{1,0:T(8,128)S(1)}, u32[]{:S(2)}, u32[]{:S(2)}) %collective-permute-start.4) | collective-permute-done | bytes 524320 | tf_op jit(solution)/shard_map/ppermute | solution.py:481
  18.5 0.1 add.7
  18.6 24.6 %all_to_all.11 = f32[64,16,128]{2,1,0:T(8,128)S(1)} all-to-all(f32[64,16,128]{2,1,0:T(8,128)S(1)} %bitcast.5), channel_id=1, replica_groups=mesh['y'=4,'core'=2,'z'=4,'x'=4] {'y','z','x'}, dimensions={0} | all-to-all | bytes 1048576 | tf_op jit(solution)/shard_map/all_to_all | solution.py:487
  43.2 0.8 %beam.1 = f32[8,128]{1,0:T(8,128)} custom-call(f32[1024,128]{1,0:T(8,128)S(1)} %bitcast.4), custom_call_target="tpu_custom_call" | custom-call | flops 1000000 | bytes 528384 | tf_op jit(solution)/shard_map/beam/pallas_call | solution.py:410
  (1 shorter events, 0.0 us)
Async XLA Ops:
  3.0 1.3 %collective-permute-start = (f32[32,384]{1,0:T(8,128)S(1)}, f32[32,384]{1,0:T(8,128)S(1)}, u32[]{:S(2)}, u32[]{:S(2)}) collective-permute-start(f32[32,384]{1,0:T(8,128)S(1)} %get-tuple-element.29), channel_id=1, source_target_pairs={{0,16},{16,0},{1,17},{17,1},{2,18},{18,2},{3,19},{19,3},{4,20},{20... | collective-permute-start | bytes 147464 | tf_op jit(solution)/shard_map/ppermute | solution.py:446
  4.3 7.9 %collective-permute-start.1 = (f32[32,384]{1,0:T(8,128)S(1)}, f32[32,384]{1,0:T(8,128)S(1)}, u32[]{:S(2)}, u32[]{:S(2)}) collective-permute-start(f32[32,384]{1,0:T(8,128)S(1)} %add.6.p_ref), channel_id=1, source_target_pairs={{0,64},{32,96},{64,0},{96,32},{1,65},{33,97},{65,1},{97,33},{2,66}... | collective-permute-start | bytes 147464 | tf_op jit(solution)/shard_map/ppermute | solution.py:450
  7.6 5.3 %collective-permute-start.2 = (f32[32,384]{1,0:T(8,128)S(1)}, f32[32,384]{1,0:T(8,128)S(1)}, u32[]{:S(2)}, u32[]{:S(2)}) collective-permute-start(f32[32,384]{1,0:T(8,128)S(1)} %add.6.p_ref), channel_id=1, source_target_pairs={{0,96},{32,64},{64,32},{96,0},{1,97},{33,65},{65,33},{97,1},{2,98}... | collective-permute-start | bytes 147464 | tf_op jit(solution)/shard_map/ppermute | solution.py:450
  8.7 4.2 %collective-permute-start.3 = (f32[32,384]{1,0:T(8,128)S(1)}, f32[32,384]{1,0:T(8,128)S(1)}, u32[]{:S(2)}, u32[]{:S(2)}) collective-permute-start(f32[32,384]{1,0:T(8,128)S(1)} %add.6.p_ref), channel_id=1, source_target_pairs={{0,32},{32,0},{64,96},{96,64},{1,33},{33,1},{65,97},{97,65},{2,34}... | collective-permute-start | bytes 147464 | tf_op jit(solution)/shard_map/ppermute | solution.py:450
  16.5 2.0 %collective-permute-start.4 = (f32[1024,128]{1,0:T(8,128)S(1)}, f32[1024,128]{1,0:T(8,128)S(1)}, u32[]{:S(2)}, u32[]{:S(2)}) collective-permute-start(f32[1024,128]{1,0:T(8,128)S(1)} %get-tuple-element.55), channel_id=1, source_target_pairs={{0,16},{16,0},{1,17},{17,1},{2,18},{18,2},{3,19},{19,3},{4,20},{20... | collective-permute-start | bytes 1572872 | tf_op jit(solution)/shard_map/ppermute | solution.py:481

commit v5 on v4

--- a/solution.py
+++ b/solution.py
@@ -20,7 +20,7 @@
 DETS = 32
 CHUNK = 256
 NCHUNK = SEG // CHUNK
-XPIECE = 1024
+XPIECE = 4096
 NRUNS = DETS * SEG // RUN
 NT = 16
 NY = 4
@@ -90,10 +90,16 @@
     return jnp.sum(jnp.where(same, full, 0.0), axis=1, keepdims=True)
 
 
+def run_row(ids):
+    flat = ids.astype(F32).T
+    parts = [flat[c : c + 1, :] for c in range(SEG // RUN)]
+    return jnp.concatenate(parts, axis=1).astype(jnp.int32)
+
+
 def analysis_kernel(
-    x_hbm, t_hbm, v_hbm, basis_hbm, synth_hbm, tw_hbm,
-    out_ref, x_ref, synth_ref, tw_ref, tt_ref, w_ref,
-    t_ref, v_ref, basis_ref, sems,
+    x_hbm, t_hbm, v_hbm, ti_hbm, ro_hbm, cs_hbm, basis_hbm, synth_hbm, tw_hbm,
+    out_ref, x_ref, synth_ref, tw_ref, tt_ref, w_ref, ro_ref, cs_ref, line_ref, zid_ref,
+    t_ref, v_ref, ti_ref, basis_ref, sems,
 ):
     pieces = [
         (x_hbm.at[:, pl.ds(n * XPIECE, XPIECE)], x_ref.at[:, pl.ds(n * XPIECE, XPIECE)])
@@ -104,6 +110,7 @@
         for n, (src, dst) in enumerate(
             [
                 (t_hbm, t_ref), (v_hbm, v_ref), (basis_hbm, basis_ref), *pieces,
+                (ti_hbm, ti_ref), (ro_hbm, ro_ref), (cs_hbm, cs_ref),
                 (tw_hbm, tw_ref), (synth_hbm, synth_ref),
             ]
         )
@@ -121,6 +128,12 @@
     out_ref[:, 2 * FKEEP :] = jnp.concatenate(
         [gram, jnp.zeros((NMODE, FKEEP - NMODE), F32)], axis=1
     )
+    for copy in copies[-5:-2]:
+        copy.wait()
+    ti = ti_ref[...]
+    ro = ro_ref[...]
+    line_ref[...] = run_row(ti * TROWS + ro)
+    zid_ref[...] = run_row(((ro + RADIUS) >> 3) * NT + ti)
     copies[2].wait()
     eh = basis_ref[:CHUNK, :]
     el = basis_ref[CHUNK:, :]
@@ -162,37 +175,14 @@
     return jnp.where(ok, (b & (NT - 1)) * TROWS + row, -1)
 
 
-def run_row(ids):
-    flat = ids.astype(F32).T
-    parts = [flat[c : c + 1, :] for c in range(SEG // RUN)]
-    return jnp.concatenate(parts, axis=1).astype(jnp.int32)
-
-
 def fill_hot(ref, ids, line):
     for q in range(NRUNS // 128):
         sl = slice(q * 128, (q + 1) * 128)
         ref[:, sl] = jnp.where(ids == line[:, sl], 1.0, 0.0).astype(BF)
 
 
-def first_index_kernel(
-    core_ref, ti_hbm, ro_hbm, cs_hbm,
-    send_ref, line_ref, zid_ref, ro_ref, cs_ref, ti_ref, sems,
-):
-    copies = [
-        pltpu.make_async_copy(src, dst, sems.at[n])
-        for n, (src, dst) in enumerate(((ti_hbm, ti_ref), (ro_hbm, ro_ref), (cs_hbm, cs_ref)))
-    ]
-    for copy in copies:
-        copy.start()
-    ids = ids_of_blocks(core_ref[0] ^ 1)
-    for copy in copies:
-        copy.wait()
-    ti = ti_ref[...]
-    ro = ro_ref[...]
-    line = run_row(ti * TROWS + ro)
-    line_ref[...] = line
-    zid_ref[...] = run_row(((ro + RADIUS) >> 3) * NT + ti)
-    fill_hot(send_ref, ids, line)
+def first_index_kernel(core_ref, line_ref, send_ref):
+    fill_hot(send_ref, ids_of_blocks(core_ref[0] ^ 1), line_ref[...])
 
 
 def second_index_kernel(
@@ -429,36 +419,29 @@
 def body(timestreams, templates, validity, tile_index, row_offset, col_start):
     basis, synth, tw = tables()
     core = lax.axis_index("core").reshape(1)
-    part, x, synth, tw, tt, w = call(
+    small = (DETS, SEG // RUN)
+    big = (NBLK * BROWS, NRUNS)
+    part, x, synth, tw, tt, w, ro, cs, line, zid = call(
         analysis_kernel,
         [
             sds((NMODE, 3 * FKEEP)), sds((DETS, SEG)), sds((2 * CHUNK, 2 * FKEEP), BF),
             sds((NCHUNK, 2 * FKEEP)), sds((NMODE, DETS)), sds((DETS, 128)),
+            sds(small, I32), sds(small, I32), sds((1, NRUNS), I32), sds((1, NRUNS), I32),
         ],
-        [HBM] * 6, "analysis", 400_000_000,
-        timestreams, templates, validity.reshape(1, DETS),
+        [HBM] * 9, "analysis", 400_000_000,
+        timestreams, templates, validity.reshape(1, DETS), tile_index, row_offset, col_start,
         jnp.asarray(basis), jnp.asarray(synth), jnp.asarray(tw),
         scratch=[
-            pltpu.VMEM((DETS, NMODE), F32), pltpu.VMEM((1, DETS), I32),
-            pltpu.VMEM((2 * CHUNK, 2 * FKEEP), BF), pltpu.SemaphoreType.DMA((5 + SEG // XPIECE,)),
+            pltpu.VMEM((DETS, NMODE), F32), pltpu.VMEM((1, DETS), I32), pltpu.VMEM(small, I32),
+            pltpu.VMEM((2 * CHUNK, 2 * FKEEP), BF), pltpu.SemaphoreType.DMA((8 + SEG // XPIECE,)),
         ],
     )
-    part = part + lax.ppermute(part, "core", [(0, 1), (1, 0)])
-    tile_index, row_offset, col_start, part = lax.optimization_barrier(
-        (tile_index, row_offset, col_start, part)
-    )
+    other = lax.ppermute(part, "core", [(0, 1), (1, 0)])
+    (send_hot,) = call(
+        first_index_kernel, [sds(big, BF)], [SMEM, VMEM], "index1", 100_000_000, core, line
+    )
+    part, send_hot, line = lax.optimization_barrier((part + other, send_hot, line))
     others = [lax.ppermute(part, "y", [(k, k ^ m) for k in range(NY)]) for m in (2, 3, 1)]
-    big = (NBLK * BROWS, NRUNS)
-    send_hot, line, zid, ro, cs = call(
-        first_index_kernel,
-        [
-            sds(big, BF), sds((1, NRUNS), I32), sds((1, NRUNS), I32),
-            sds((DETS, SEG // RUN), I32), sds((DETS, SEG // RUN), I32),
-        ],
-        [SMEM] + [HBM] * 3, "index1", 100_000_000,
-        core, tile_index, row_offset, col_start,
-        scratch=[pltpu.VMEM((DETS, SEG // RUN), I32), pltpu.SemaphoreType.DMA((3,))],
-    )
     keep_hot, zhot, idx, edge, mask, zh = call(
         second_index_kernel,
         [

time: 44.4 us -> 43 us (0.968)
  Pallas kernels: 10.9 us -> 9.58 us
  waiting for transfers between devices: 3.1 us -> 4.05 us
  blocking collectives: 24.6 us -> 23.8 us
    ppermute x3, waiting for transfers between devices: 0.8 us -> 2.61 us  [body(): lax.ppermute(part, 'y', [(k, k ^ m) for k in range(NY)])]
    pallas_call x6, Pallas kernels: 10.9 us -> 9.58 us  [call(): pl.pallas_call(kernel, out_shape=outs, in_specs=specs, out_specs=out_spec...]
    ppermute x1, waiting for transfers between devices: 1.22 us -> 0.36 us  [body(): other = lax.ppermute(part, 'core', [(0, 1), (1, 0)])]
    all_to_all x1, blocking collectives: 24.6 us -> 23.8 us  [body(): blocks = lax.all_to_all(keep + got, ('y', 'z', 'x'), 0, 0, tiled=True)]
  transfers between devices with their start and end apart: 5 -> 5, of which waited for: 3 -> 3; matrix products, arithmetic and copies ran while one was open for 0% -> 0% of each run, Pallas kernels for 10% -> 8%
where the time goes in v5:
time: 43 us; the launch traced here: 42.8 us
  blocking collectives  23.8 us (55%)
  Pallas kernels  9.58 us (22%)
  starting transfers between devices  4.58 us (11%)
  waiting for transfers between devices  4.05 us (9%)
  between operations  0.7 us (2%)
    all_to_all x1, blocking collectives, body(): blocks = lax.all_to_all(keep + got, ('y', 'z', 'x'), 0, 0, tiled=True)  23.8 us
    pallas_call x6, Pallas kernels, call(): pl.pallas_call(kernel, out_shape=outs, in_specs=specs, out_specs=out_spec...  9.58 us
    ppermute x3, starting transfers between devices, body(): lax.ppermute(part, 'y', [(k, k ^ m) for k in range(NY)])  4.41 us
    ppermute x3, waiting for transfers between devices, body(): lax.ppermute(part, 'y', [(k, k ^ m) for k in range(NY)])  2.61 us
    ppermute x1, waiting for transfers between devices, body(): got = lax.ppermute(send, 'core', [(0, 1), (1, 0)])  1.08 us
  transfers between devices with their start and end apart: 5, of which 3 were waited for; matrix products, arithmetic and copies ran while one was open for 0% of the time, Pallas kernels for 8%

profile of v5, /device:TPU:0, one launch (start us, length us, event | category | flops | bytes accessed | tf_op | source)
XLA Modules:
  0.0 42.8 jit_solution(6915339338161530553)
XLA Ops:
  0.6 1.9 %analysis.1 = (f32[32,384]{1,0:T(8,128)S(1)}, f32[32,4096]{1,0:T(8,128)S(1)}, bf16[512,256]{1,0:T(8,128)(2,1)S(1)}, f32[16,256]{1,0:T(8,128)S(1)}, f32[32,32]{1,...) custom-call(f32[32,4096]{1,0:T(8,128)} %x_hbm.1, ...), custom_call_target="tpu_custom_call" | custom-call | flops 400000000 | bytes 2756736 | tf_op jit(solution)/shard_map/analysis/pallas_call | solution.py:400
  2.6 0.1 collective-permute-start
  2.7 0.8 %index1.1.send_hot_ref = bf16[1024,1024]{1,0:T(8,128)(2,1)S(1)} custom-call(s32[1]{0:T(128)} %bitcast.core_ref, s32[1,1024]{1,0:T(1,128)S(1)} %get-tuple-element.29.line_ref), custom_call_target="tpu_custom_call" | custom-call | flops 100000000 | bytes 4198404 | tf_op jit(solution)/shard_map/index1/pallas_call | solution.py:400
  3.5 0.4 collective-permute-done
  3.9 3.4 %collective-permute-start.1 = (f32[32,384]{1,0:T(8,128)S(1)}, f32[32,384]{1,0:T(8,128)S(1)}, u32[]{:S(2)}, u32[]{:S(2)}) collective-permute-start(f32[32,384]{1,0:T(8,128)S(1)} %add.6.p_ref), channel_id=1, source_target_pairs={{0,64},{32,96},{64,0},{96,32},{1,65},{33,97},{65,1},{97,33},{2,66}... | collective-permute-start | bytes 147464 | tf_op jit(solution)/shard_map/ppermute | solution.py:444
  7.3 1.1 %collective-permute-start.2 = (f32[32,384]{1,0:T(8,128)S(1)}, f32[32,384]{1,0:T(8,128)S(1)}, u32[]{:S(2)}, u32[]{:S(2)}) collective-permute-start(f32[32,384]{1,0:T(8,128)S(1)} %add.6.p_ref), channel_id=1, source_target_pairs={{0,96},{32,64},{64,32},{96,0},{1,97},{33,65},{65,33},{97,1},{2,98}... | collective-permute-start | bytes 147464 | tf_op jit(solution)/shard_map/ppermute | solution.py:444
  8.3 0.0 collective-permute-start.3
  8.3 1.6 %index2.1 = (bf16[1024,1024]{1,0:T(8,128)(2,1)S(1)}, bf16[144,1024]{1,0:T(8,128)(2,1)S(1)}, s32[1024,128]{1,0:T(8,128)S(1)}, s32[1024,128]{1,0:T(8,128)S(1)}, f3...) custom-call(s32[1]{0:T(128)} %bitcast.core_ref, s32[1,1024]{1,0:T(1,128)S(1)} %get-tuple-element.29.line_ref, ...), custom_call_target="tpu_custom_call" | custom-call | flops 100000000 | bytes 6463492 | tf_op jit(solution)/shard_map/index2/pallas_call | solution.py:400
  9.9 0.0 collective-permute-done.1.q_ref
  10.0 2.6 %collective-permute-done.2.r_ref = f32[32,384]{1,0:T(8,128)S(1)} collective-permute-done((f32[32,384]{1,0:T(8,128)S(1)}, f32[32,384]{1,0:T(8,128)S(1)}, u32[]{:S(2)}, u32[]{:S(2)}) %collective-permute-start.2) | collective-permute-done | bytes 49184 | tf_op jit(solution)/shard_map/ppermute | solution.py:444
  12.6 0.0 collective-permute-done.3.s_ref
  12.6 3.6 %clean.1 = (f32[32,4096]{1,0:T(8,128)S(1)}, f32[1024,128]{1,0:T(8,128)S(1)}, bf16[1024,256]{1,0:T(8,128)(2,1)S(1)}, f32[128,128]{1,0:T(8,128)S(1)}) custom-call(s32[1]{0:T(128)} %bitcast.core_ref, f32[32,384]{1,0:T(8,128)S(1)} %add.6.p_ref, f32[32,384]{1,0:T(8,128)S(1)} %collective-permute-done.1.q_ref, f32[32,384]{1,0:T(8,128)S(1)} %collective-permute-done.2.r_ref, ...), custom_call_target="tpu_custom_call" | custom-call | flops 1000000000 | bytes 9875460 | tf_op jit(solution)/shard_map/clean/pallas_call | solution.py:400
  16.1 0.1 collective-permute-start.4
  16.2 0.8 %keep.1 = (f32[1024,128]{1,0:T(8,128)S(1)}, f32[32,4096]{1,0:T(8,128)}) custom-call(bf16[1024,1024]{1,0:T(8,128)(2,1)S(1)} %get-tuple-element.34.hot_ref, bf16[1024,256]{1,0:T(8,128)(2,1)S(1)} %get-tuple-element.46.vals_ref, f32[128,128]{1,0:T(8,128)S(1)} %get-tuple-element.47.rows_ref, f32[32,4096]{1,0:T(8,128)S(1)} %get-tuple-element.48.clean_ref), custom_call_target="tpu_custom_call" | custom-call | flops 500000000 | bytes 6881280 | tf_op jit(solution)/shard_map/keep/pallas_call | solution.py:400
  17.0 1.1 %collective-permute-done.4 = f32[1024,128]{1,0:T(8,128)S(1)} collective-permute-done((f32[1024,128]{1,0:T(8,128)S(1)}, f32[1024,128]{1,0:T(8,128)S(1)}, u32[]{:S(2)}, u32[]{:S(2)}) %collective-permute-start.4) | collective-permute-done | bytes 524320 | tf_op jit(solution)/shard_map/ppermute | solution.py:464
  18.1 0.1 add.7
  18.2 23.8 %all_to_all.11 = f32[64,16,128]{2,1,0:T(8,128)S(1)} all-to-all(f32[64,16,128]{2,1,0:T(8,128)S(1)} %bitcast.5), channel_id=1, replica_groups=mesh['y'=4,'core'=2,'z'=4,'x'=4] {'y','z','x'}, dimensions={0} | all-to-all | bytes 1048576 | tf_op jit(solution)/shard_map/all_to_all | solution.py:470
  42.0 0.8 %beam.1 = f32[8,128]{1,0:T(8,128)} custom-call(f32[1024,128]{1,0:T(8,128)S(1)} %bitcast.4), custom_call_target="tpu_custom_call" | custom-call | flops 1000000 | bytes 528384 | tf_op jit(solution)/shard_map/beam/pallas_call | solution.py:400
  (1 shorter events, 0.0 us)
Async XLA Ops:
  2.6 1.3 %collective-permute-start = (f32[32,384]{1,0:T(8,128)S(1)}, f32[32,384]{1,0:T(8,128)S(1)}, u32[]{:S(2)}, u32[]{:S(2)}) collective-permute-start(f32[32,384]{1,0:T(8,128)S(1)} %get-tuple-element.27), channel_id=1, source_target_pairs={{0,16},{16,0},{1,17},{17,1},{2,18},{18,2},{3,19},{19,3},{4,20},{20... | collective-permute-start | bytes 147464 | tf_op jit(solution)/shard_map/ppermute | solution.py:439
  3.9 6.0 %collective-permute-start.1 = (f32[32,384]{1,0:T(8,128)S(1)}, f32[32,384]{1,0:T(8,128)S(1)}, u32[]{:S(2)}, u32[]{:S(2)}) collective-permute-start(f32[32,384]{1,0:T(8,128)S(1)} %add.6.p_ref), channel_id=1, source_target_pairs={{0,64},{32,96},{64,0},{96,32},{1,65},{33,97},{65,1},{97,33},{2,66}... | collective-permute-start | bytes 147464 | tf_op jit(solution)/shard_map/ppermute | solution.py:444
  7.3 5.3 %collective-permute-start.2 = (f32[32,384]{1,0:T(8,128)S(1)}, f32[32,384]{1,0:T(8,128)S(1)}, u32[]{:S(2)}, u32[]{:S(2)}) collective-permute-start(f32[32,384]{1,0:T(8,128)S(1)} %add.6.p_ref), channel_id=1, source_target_pairs={{0,96},{32,64},{64,32},{96,0},{1,97},{33,65},{65,33},{97,1},{2,98}... | collective-permute-start | bytes 147464 | tf_op jit(solution)/shard_map/ppermute | solution.py:444
  8.3 4.2 %collective-permute-start.3 = (f32[32,384]{1,0:T(8,128)S(1)}, f32[32,384]{1,0:T(8,128)S(1)}, u32[]{:S(2)}, u32[]{:S(2)}) collective-permute-start(f32[32,384]{1,0:T(8,128)S(1)} %add.6.p_ref), channel_id=1, source_target_pairs={{0,32},{32,0},{64,96},{96,64},{1,33},{33,1},{65,97},{97,65},{2,34}... | collective-permute-start | bytes 147464 | tf_op jit(solution)/shard_map/ppermute | solution.py:444
  16.1 2.0 %collective-permute-start.4 = (f32[1024,128]{1,0:T(8,128)S(1)}, f32[1024,128]{1,0:T(8,128)S(1)}, u32[]{:S(2)}, u32[]{:S(2)}) collective-permute-start(f32[1024,128]{1,0:T(8,128)S(1)} %get-tuple-element.51), channel_id=1, source_target_pairs={{0,16},{16,0},{1,17},{17,1},{2,18},{18,2},{3,19},{19,3},{4,20},{20... | collective-permute-start | bytes 1572872 | tf_op jit(solution)/shard_map/ppermute | solution.py:464

commit v6 on v5

--- a/solution.py
+++ b/solution.py
@@ -98,7 +98,7 @@
 
 def analysis_kernel(
     x_hbm, t_hbm, v_hbm, ti_hbm, ro_hbm, cs_hbm, basis_hbm, synth_hbm, tw_hbm,
-    out_ref, x_ref, synth_ref, tw_ref, tt_ref, w_ref, ro_ref, cs_ref, line_ref, zid_ref,
+    out_ref, x_ref, synth_ref, tw_ref, rhs_ref, w_ref, ro_ref, cs_ref, line_ref, zid_ref,
     t_ref, v_ref, ti_ref, basis_ref, sems,
 ):
     pieces = [
@@ -123,10 +123,11 @@
     t = t_ref[...]
     wt = t * w
     w_ref[...] = jnp.broadcast_to(w, (DETS, 128))
-    tt_ref[...] = t.T
+    zero = jnp.zeros((NMODE, 32), F32)
+    rhs_ref[...] = jnp.concatenate([zero, t.T, zero, zero], axis=1)
     gram = mm0(wt, t)
-    out_ref[:, 2 * FKEEP :] = jnp.concatenate(
-        [gram, jnp.zeros((NMODE, FKEEP - NMODE), F32)], axis=1
+    out_ref[2 * NMODE :, :] = jnp.concatenate(
+        [gram[8 * i : 8 * i + 8, :] for i in range(NMODE // 8)], axis=1
     )
     for copy in copies[-5:-2]:
         copy.wait()
@@ -157,7 +158,9 @@
         sin = tw_ref[c : c + 1, FKEEP:]
         re = re + (cos * yc - sin * yi)
         im = im + (sin * yc + cos * yi)
-    out_ref[:, : 2 * FKEEP] = mm0_split(wt, jnp.concatenate([re, im], axis=1))
+    both = mm0_split(wt, jnp.concatenate([re, im], axis=1))
+    out_ref[:NMODE, :] = both[:, :FKEEP]
+    out_ref[NMODE : 2 * NMODE, :] = both[:, FKEEP:]
     copies[-1].wait()
 
 
@@ -213,28 +216,24 @@
     return jnp.broadcast_to(v[:, k : k + 1], (8, 128))
 
 
-def row_of(v, r):
-    return jnp.broadcast_to(v[r : r + 1, :], (8, 128))
-
-
-def solve(gram, rhs):
-    n = gram.shape[0]
-    eye = lax.broadcasted_iota(jnp.int32, gram.shape, 0) == lax.broadcasted_iota(
-        jnp.int32, gram.shape, 1
-    )
-    diag = jnp.where(eye, gram, 0.0)
+def solve(packed, rhs):
+    n = NMODE
+    groups = range(n // 8)
+    full = jnp.concatenate(
+        [packed] + [pltpu.roll(packed, 128 - n * i, 1) for i in groups[1:]], axis=0
+    )
+    row = lax.broadcasted_iota(jnp.int32, (n, 128), 0)
+    lane = lax.broadcasted_iota(jnp.int32, (n, 128), 1)
+    full = jnp.where(lane < n, full, rhs) + jnp.where(lane == row, 0.05, 0.0)
+    diag = jnp.where(lane == row, full, 0.0)
     down = lax.rsqrt(jnp.sum(diag, axis=1, keepdims=True))
-    along = lax.rsqrt(jnp.sum(diag, axis=0, keepdims=True))
-    full = jnp.concatenate(
-        [gram * down * along, rhs * down, jnp.zeros((n, 128 - 2 * n), F32)], axis=1
-    )
-    a = [full[8 * i : 8 * i + 8, :] for i in range(n // 8)]
+    along = jnp.sum(jnp.where(lane < n, diag, 1.0 / n), axis=0, keepdims=True)
+    full = full * down * lax.rsqrt(along)
+    a = [full[8 * i : 8 * i + 8, :] for i in groups]
     sub = lax.broadcasted_iota(jnp.int32, (8, 128), 0)
-    for k in range(0, n, 4):
-        here, r = k // 8, k % 8
-        c = [[lanes_of(v, k + j) for v in a] for j in range(4)]
-        p = [[row_of(c[j][here], r + i) for j in range(4)] for i in range(4)]
-        rows = [row_of(a[here], r + i) for i in range(4)]
+    for q in range(8):
+        c = [[lanes_of(v, 8 * j + q) for v in a] for j in groups]
+        p = [[c[j][i] for j in groups] for i in groups]
         i1 = 1.0 / (p[0][0] * p[1][1] - p[0][1] * p[0][1])
         e00, e01, e11 = p[1][1] * i1, -p[0][1] * i1, p[0][0] * i1
         w00 = e00 * p[0][2] + e01 * p[1][2]
@@ -245,18 +244,23 @@
         s01 = p[2][3] - (p[0][2] * w01 + p[1][2] * w11)
         s11 = p[3][3] - (p[0][3] * w01 + p[1][3] * w11)
         i2 = 1.0 / (s00 * s11 - s01 * s01)
-        y0 = e00 * rows[0] + e01 * rows[1]
-        y1 = e01 * rows[0] + e11 * rows[1]
-        q2 = rows[2] - (p[0][2] * y0 + p[1][2] * y1)
-        q3 = rows[3] - (p[0][3] * y0 + p[1][3] * y1)
+        y0 = e00 * a[0] + e01 * a[1]
+        y1 = e01 * a[0] + e11 * a[1]
+        q2 = a[2] - (p[0][2] * y0 + p[1][2] * y1)
+        q3 = a[3] - (p[0][3] * y0 + p[1][3] * y1)
         n2 = (s11 * q2 - s01 * q3) * i2
         n3 = (s00 * q3 - s01 * q2) * i2
         n0 = y0 - (w00 * n2 + w01 * n3)
         n1 = y1 - (w10 * n2 + w11 * n3)
-        for i in range(n // 8):
-            a[i] = a[i] - ((c[0][i] * n0 + c[1][i] * n1) + (c[2][i] * n2 + c[3][i] * n3))
-        for j, new in enumerate((n0, n1, n2, n3)):
-            a[here] = jnp.where(sub == r + j, new, a[here])
+        new = [jnp.broadcast_to(v[q : q + 1, :], (8, 128)) for v in (n0, n1, n2, n3)]
+        a = [
+            jnp.where(
+                sub == q,
+                new[i],
+                a[i] - ((c[0][i] * new[0] + c[1][i] * new[1]) + (c[2][i] * new[2] + c[3][i] * new[3])),
+            )
+            for i in groups
+        ]
     return jnp.concatenate(a, axis=0)[:, n : 2 * n] * down
 
 
@@ -268,19 +272,15 @@
 
 
 def clean_kernel(
-    core_ref, p_ref, q_ref, r_ref, s_ref, tt_ref, w_ref, x_ref, synth_ref, tw_ref,
+    core_ref, p_ref, q_ref, r_ref, s_ref, rhs_ref, w_ref, x_ref, synth_ref, tw_ref,
     idx_ref, edge_ref, mask_ref, zhot_ref, zh_ref, send_hot_ref,
     clean_ref, send_ref, vals_ref, rows_ref,
 ):
     w = w_ref[...]
     w = jnp.concatenate([w, w], axis=1)
     p = (p_ref[...] + q_ref[...]) + (r_ref[...] + s_ref[...])
-    eye = lax.broadcasted_iota(jnp.int32, (NMODE, NMODE), 0) == lax.broadcasted_iota(
-        jnp.int32, (NMODE, NMODE), 1
-    )
-    gram = p[:, 2 * FKEEP : 2 * FKEEP + NMODE] + jnp.where(eye, 0.05, 0.0)
-    coef = solve(gram, tt_ref[...])
-    ab = mm0_split(coef, p[:, : 2 * FKEEP])
+    coef = solve(p[2 * NMODE :, :], rhs_ref[...])
+    ab = mm0_split(coef, jnp.concatenate([p[:NMODE, :], p[NMODE : 2 * NMODE, :]], axis=1))
     a = ab[:, :FKEEP]
     b = ab[:, FKEEP:]
     parts = []
@@ -421,11 +421,11 @@
     core = lax.axis_index("core").reshape(1)
     small = (DETS, SEG // RUN)
     big = (NBLK * BROWS, NRUNS)
-    part, x, synth, tw, tt, w, ro, cs, line, zid = call(
+    part, x, synth, tw, rhs, w, ro, cs, line, zid = call(
         analysis_kernel,
         [
-            sds((NMODE, 3 * FKEEP)), sds((DETS, SEG)), sds((2 * CHUNK, 2 * FKEEP), BF),
-            sds((NCHUNK, 2 * FKEEP)), sds((NMODE, DETS)), sds((DETS, 128)),
+            sds((2 * NMODE + 8, FKEEP)), sds((DETS, SEG)), sds((2 * CHUNK, 2 * FKEEP), BF),
+            sds((NCHUNK, 2 * FKEEP)), sds((NMODE, 128)), sds((DETS, 128)),
             sds(small, I32), sds(small, I32), sds((1, NRUNS), I32), sds((1, NRUNS), I32),
         ],
         [HBM] * 9, "analysis", 400_000_000,
@@ -459,7 +459,7 @@
             sds((NRUNS, 256), BF), sds((2 * NBLK, 128)),
         ],
         [SMEM] + [VMEM] * 15, "clean", 1_000_000_000,
-        core, part, *others, tt, w, x, synth, tw, idx, edge, mask, zhot, zh, send_hot,
+        core, part, *others, rhs, w, x, synth, tw, idx, edge, mask, zhot, zh, send_hot,
     )
     got = lax.ppermute(send, "core", [(0, 1), (1, 0)])
     keep, cleaned = call(

time: 43 us -> 42.2 us (0.981)
  Pallas kernels: 9.58 us -> 9.05 us
    pallas_call x6, Pallas kernels: 9.58 us -> 9.05 us  [call(): pl.pallas_call(kernel, out_shape=outs, in_specs=specs, out_specs=out_spec...]
where the time goes in v6:
time: 42.2 us; the launch traced here: 42 us
  blocking collectives  23.8 us (56%)
  Pallas kernels  9.05 us (21%)
  starting transfers between devices  4.51 us (11%)
  waiting for transfers between devices  3.91 us (9%)
  between operations  0.7 us (2%)
    all_to_all x1, blocking collectives, body(): blocks = lax.all_to_all(keep + got, ('y', 'z', 'x'), 0, 0, tiled=True)  23.8 us
    pallas_call x6, Pallas kernels, call(): pl.pallas_call(kernel, out_shape=outs, in_specs=specs, out_specs=out_spec...  9.05 us
    ppermute x3, starting transfers between devices, body(): lax.ppermute(part, 'y', [(k, k ^ m) for k in range(NY)])  4.33 us
    ppermute x3, waiting for transfers between devices, body(): lax.ppermute(part, 'y', [(k, k ^ m) for k in range(NY)])  2.49 us
    ppermute x1, waiting for transfers between devices, body(): got = lax.ppermute(send, 'core', [(0, 1), (1, 0)])  1.08 us
  transfers between devices with their start and end apart: 5, of which 3 were waited for; matrix products, arithmetic and copies ran while one was open for 0% of the time, Pallas kernels for 8%

profile of v6, /device:TPU:0, one launch (start us, length us, event | category | flops | bytes accessed | tf_op | source)
XLA Modules:
  0.0 42.0 jit_solution(827221636712927657)
XLA Ops:
  0.6 2.0 %analysis.1 = (f32[72,128]{1,0:T(8,128)S(1)}, f32[32,4096]{1,0:T(8,128)S(1)}, bf16[512,256]{1,0:T(8,128)(2,1)S(1)}, f32[16,256]{1,0:T(8,128)S(1)}, f32[32,128]{1...) custom-call(f32[32,4096]{1,0:T(8,128)} %x_hbm.1, ...), custom_call_target="tpu_custom_call" | custom-call | flops 400000000 | bytes 2756736 | tf_op jit(solution)/shard_map/analysis/pallas_call | solution.py:400
  2.6 0.1 collective-permute-start
  2.7 0.8 %index1.1.send_hot_ref = bf16[1024,1024]{1,0:T(8,128)(2,1)S(1)} custom-call(s32[1]{0:T(128)} %bitcast.core_ref, s32[1,1024]{1,0:T(1,128)S(1)} %get-tuple-element.29.line_ref), custom_call_target="tpu_custom_call" | custom-call | flops 100000000 | bytes 4198404 | tf_op jit(solution)/shard_map/index1/pallas_call | solution.py:400
  3.6 0.3 collective-permute-done
  3.9 3.3 %collective-permute-start.1 = (f32[72,128]{1,0:T(8,128)S(1)}, f32[72,128]{1,0:T(8,128)S(1)}, u32[]{:S(2)}, u32[]{:S(2)}) collective-permute-start(f32[72,128]{1,0:T(8,128)S(1)} %add.6.p_ref), channel_id=1, source_target_pairs={{0,64},{32,96},{64,0},{96,32},{1,65},{33,97},{65,1},{97,33},{2,66}... | collective-permute-start | bytes 110600 | tf_op jit(solution)/shard_map/ppermute | solution.py:444
  7.2 1.1 %collective-permute-start.2 = (f32[72,128]{1,0:T(8,128)S(1)}, f32[72,128]{1,0:T(8,128)S(1)}, u32[]{:S(2)}, u32[]{:S(2)}) collective-permute-start(f32[72,128]{1,0:T(8,128)S(1)} %add.6.p_ref), channel_id=1, source_target_pairs={{0,96},{32,64},{64,32},{96,0},{1,97},{33,65},{65,33},{97,1},{2,98}... | collective-permute-start | bytes 110600 | tf_op jit(solution)/shard_map/ppermute | solution.py:444
  8.3 0.0 collective-permute-start.3
  8.3 1.6 %index2.1 = (bf16[1024,1024]{1,0:T(8,128)(2,1)S(1)}, bf16[144,1024]{1,0:T(8,128)(2,1)S(1)}, s32[1024,128]{1,0:T(8,128)S(1)}, s32[1024,128]{1,0:T(8,128)S(1)}, f3...) custom-call(s32[1]{0:T(128)} %bitcast.core_ref, s32[1,1024]{1,0:T(1,128)S(1)} %get-tuple-element.29.line_ref, ...), custom_call_target="tpu_custom_call" | custom-call | flops 100000000 | bytes 6463492 | tf_op jit(solution)/shard_map/index2/pallas_call | solution.py:400
  9.9 0.0 collective-permute-done.1.q_ref
  9.9 2.5 %collective-permute-done.2.r_ref = f32[72,128]{1,0:T(8,128)S(1)} collective-permute-done((f32[72,128]{1,0:T(8,128)S(1)}, f32[72,128]{1,0:T(8,128)S(1)}, u32[]{:S(2)}, u32[]{:S(2)}) %collective-permute-start.2) | collective-permute-done | bytes 36896 | tf_op jit(solution)/shard_map/ppermute | solution.py:444
  12.4 0.0 collective-permute-done.3.s_ref
  12.4 3.0 %clean.1 = (f32[32,4096]{1,0:T(8,128)S(1)}, f32[1024,128]{1,0:T(8,128)S(1)}, bf16[1024,256]{1,0:T(8,128)(2,1)S(1)}, f32[128,128]{1,0:T(8,128)S(1)}) custom-call(s32[1]{0:T(128)} %bitcast.core_ref, f32[72,128]{1,0:T(8,128)S(1)} %add.6.p_ref, f32[72,128]{1,0:T(8,128)S(1)} %collective-permute-done.1.q_ref, f32[72,128]{1,0:T(8,128)S(1)} %collective-permute-done.2.r_ref, ...), custom_call_target="tpu_custom_call" | custom-call | flops 1000000000 | bytes 9838596 | tf_op jit(solution)/shard_map/clean/pallas_call | solution.py:400
  15.4 0.1 collective-permute-start.4
  15.5 0.8 %keep.1 = (f32[1024,128]{1,0:T(8,128)S(1)}, f32[32,4096]{1,0:T(8,128)}) custom-call(bf16[1024,1024]{1,0:T(8,128)(2,1)S(1)} %get-tuple-element.34.hot_ref, bf16[1024,256]{1,0:T(8,128)(2,1)S(1)} %get-tuple-element.46.vals_ref, f32[128,128]{1,0:T(8,128)S(1)} %get-tuple-element.47.rows_ref, f32[32,4096]{1,0:T(8,128)S(1)} %get-tuple-element.48.clean_ref), custom_call_target="tpu_custom_call" | custom-call | flops 500000000 | bytes 6881280 | tf_op jit(solution)/shard_map/keep/pallas_call | solution.py:400
  16.3 1.1 %collective-permute-done.4 = f32[1024,128]{1,0:T(8,128)S(1)} collective-permute-done((f32[1024,128]{1,0:T(8,128)S(1)}, f32[1024,128]{1,0:T(8,128)S(1)}, u32[]{:S(2)}, u32[]{:S(2)}) %collective-permute-start.4) | collective-permute-done | bytes 524320 | tf_op jit(solution)/shard_map/ppermute | solution.py:464
  17.4 0.1 add.7
  17.4 23.8 %all_to_all.11 = f32[64,16,128]{2,1,0:T(8,128)S(1)} all-to-all(f32[64,16,128]{2,1,0:T(8,128)S(1)} %bitcast.5), channel_id=1, replica_groups=mesh['y'=4,'core'=2,'z'=4,'x'=4] {'y','z','x'}, dimensions={0} | all-to-all | bytes 1048576 | tf_op jit(solution)/shard_map/all_to_all | solution.py:470
  41.2 0.8 %beam.1 = f32[8,128]{1,0:T(8,128)} custom-call(f32[1024,128]{1,0:T(8,128)S(1)} %bitcast.4), custom_call_target="tpu_custom_call" | custom-call | flops 1000000 | bytes 528384 | tf_op jit(solution)/shard_map/beam/pallas_call | solution.py:400
  (1 shorter events, 0.0 us)
Async XLA Ops:
  2.6 1.3 %collective-permute-start = (f32[72,128]{1,0:T(8,128)S(1)}, f32[72,128]{1,0:T(8,128)S(1)}, u32[]{:S(2)}, u32[]{:S(2)}) collective-permute-start(f32[72,128]{1,0:T(8,128)S(1)} %get-tuple-element.27), channel_id=1, source_target_pairs={{0,16},{16,0},{1,17},{17,1},{2,18},{18,2},{3,19},{19,3},{4,20},{20... | collective-permute-start | bytes 110600 | tf_op jit(solution)/shard_map/ppermute | solution.py:439
  3.9 6.0 %collective-permute-start.1 = (f32[72,128]{1,0:T(8,128)S(1)}, f32[72,128]{1,0:T(8,128)S(1)}, u32[]{:S(2)}, u32[]{:S(2)}) collective-permute-start(f32[72,128]{1,0:T(8,128)S(1)} %add.6.p_ref), channel_id=1, source_target_pairs={{0,64},{32,96},{64,0},{96,32},{1,65},{33,97},{65,1},{97,33},{2,66}... | collective-permute-start | bytes 110600 | tf_op jit(solution)/shard_map/ppermute | solution.py:444
  7.2 5.2 %collective-permute-start.2 = (f32[72,128]{1,0:T(8,128)S(1)}, f32[72,128]{1,0:T(8,128)S(1)}, u32[]{:S(2)}, u32[]{:S(2)}) collective-permute-start(f32[72,128]{1,0:T(8,128)S(1)} %add.6.p_ref), channel_id=1, source_target_pairs={{0,96},{32,64},{64,32},{96,0},{1,97},{33,65},{65,33},{97,1},{2,98}... | collective-permute-start | bytes 110600 | tf_op jit(solution)/shard_map/ppermute | solution.py:444
  8.3 4.1 %collective-permute-start.3 = (f32[72,128]{1,0:T(8,128)S(1)}, f32[72,128]{1,0:T(8,128)S(1)}, u32[]{:S(2)}, u32[]{:S(2)}) collective-permute-start(f32[72,128]{1,0:T(8,128)S(1)} %add.6.p_ref), channel_id=1, source_target_pairs={{0,32},{32,0},{64,96},{96,64},{1,33},{33,1},{65,97},{97,65},{2,34}... | collective-permute-start | bytes 110600 | tf_op jit(solution)/shard_map/ppermute | solution.py:444
  15.4 2.0 %collective-permute-start.4 = (f32[1024,128]{1,0:T(8,128)S(1)}, f32[1024,128]{1,0:T(8,128)S(1)}, u32[]{:S(2)}, u32[]{:S(2)}) collective-permute-start(f32[1024,128]{1,0:T(8,128)S(1)} %get-tuple-element.51), channel_id=1, source_target_pairs={{0,16},{16,0},{1,17},{17,1},{2,18},{18,2},{3,19},{19,3},{4,20},{20... | collective-permute-start | bytes 1572872 | tf_op jit(solution)/shard_map/ppermute | solution.py:464

commit v7 on v6

--- a/solution.py
+++ b/solution.py
@@ -98,8 +98,8 @@
 
 def analysis_kernel(
     x_hbm, t_hbm, v_hbm, ti_hbm, ro_hbm, cs_hbm, basis_hbm, synth_hbm, tw_hbm,
-    out_ref, x_ref, synth_ref, tw_ref, rhs_ref, w_ref, ro_ref, cs_ref, line_ref, zid_ref,
-    t_ref, v_ref, ti_ref, basis_ref, sems,
+    out_ref, x_ref, synth_ref, tw_ref, pack_ref, line_ref,
+    t_ref, v_ref, ti_ref, ro_ref, cs_ref, basis_ref, sems,
 ):
     pieces = [
         (x_hbm.at[:, pl.ds(n * XPIECE, XPIECE)], x_ref.at[:, pl.ds(n * XPIECE, XPIECE)])
@@ -122,19 +122,17 @@
     w = column(v_ref[...].astype(F32), DETS)
     t = t_ref[...]
     wt = t * w
-    w_ref[...] = jnp.broadcast_to(w, (DETS, 128))
-    zero = jnp.zeros((NMODE, 32), F32)
-    rhs_ref[...] = jnp.concatenate([zero, t.T, zero, zero], axis=1)
     gram = mm0(wt, t)
     out_ref[2 * NMODE :, :] = jnp.concatenate(
         [gram[8 * i : 8 * i + 8, :] for i in range(NMODE // 8)], axis=1
     )
     for copy in copies[-5:-2]:
         copy.wait()
-    ti = ti_ref[...]
-    ro = ro_ref[...]
-    line_ref[...] = run_row(ti * TROWS + ro)
-    zid_ref[...] = run_row(((ro + RADIUS) >> 3) * NT + ti)
+    line = ti_ref[...] * TROWS + ro_ref[...]
+    line_ref[...] = run_row(line)
+    pack_ref[...] = jnp.concatenate(
+        [t, line.astype(F32), cs_ref[...].astype(F32), jnp.broadcast_to(w, (DETS, 32))], axis=1
+    )
     copies[2].wait()
     eh = basis_ref[:CHUNK, :]
     el = basis_ref[CHUNK:, :]
@@ -184,32 +182,44 @@
         ref[:, sl] = jnp.where(ids == line[:, sl], 1.0, 0.0).astype(BF)
 
 
-def first_index_kernel(core_ref, line_ref, send_ref):
-    fill_hot(send_ref, ids_of_blocks(core_ref[0] ^ 1), line_ref[...])
+def first_index_kernel(core_ref, line_ref, hot_ref):
+    fill_hot(hot_ref, ids_of_blocks(core_ref[0]), line_ref[...])
 
 
 def second_index_kernel(
-    core_ref, line_ref, zid_ref, ro_ref, cs_ref, w_ref,
-    keep_ref, zhot_ref, idx_ref, edge_ref, mask_ref, zh_ref,
+    core_ref, line_ref, pack_ref, other_ref,
+    hot_ref, zhot_ref, idx_ref, edge_ref, mask_ref, zh_ref, rhs_ref, w_ref,
 ):
-    zl = lax.broadcasted_iota(jnp.int32, (ZROWS, NRUNS), 0)
-    zhot = jnp.where(zl == zid_ref[...], 1.0, 0.0).astype(BF)
+    packs = (pack_ref[...], other_ref[...])
+    lines = [pack[:, 32:64].astype(jnp.int32) for pack in packs]
+    rows = (line_ref[...], run_row(lines[1]))
+    fill_hot(hot_ref, ids_of_blocks(core_ref[0]), rows[1])
+    line = jnp.concatenate(rows, axis=1)
+    zid = (((line & (TROWS - 1)) + RADIUS) >> 3) * NT + (line >> 6)
+    zl = lax.broadcasted_iota(jnp.int32, (ZROWS, 2 * NRUNS), 0)
+    zhot = jnp.where(zl == zid, 1.0, 0.0).astype(BF)
     zhot_ref[...] = zhot
-    w = w_ref[...]
     lane = lax.broadcasted_iota(jnp.int32, (DETS, 128), 1)
     ecol = edge_col(lane)
     hparts = []
-    for c in range(SEG // RUN):
-        sl = slice(c * DETS, (c + 1) * DETS)
-        cs = jnp.broadcast_to(cs_ref[:, c : c + 1], (DETS, 128))
-        ro = jnp.broadcast_to(ro_ref[:, c : c + 1], (DETS, 128))
-        idx_ref[sl, :] = (lane - cs) & (TCOLS - 1)
-        edge_ref[sl, :] = (ecol - cs) & (TCOLS - 1)
-        here = ((ro + RADIUS) & (OWN - 1)) == (lane & (OWN - 1))
-        mask_ref[sl, :] = jnp.where(here & (lane < 48), 1.0, 0.0)
-        hparts.append(jnp.where(here & (lane >= 48) & (lane < 56), w, 0.0).astype(BF))
+    for n, pack in enumerate(packs):
+        w = jnp.broadcast_to(pack[:, 96:97], (DETS, 128))
+        w_ref[n * DETS : (n + 1) * DETS, :] = w
+        ro3 = (lines[n] & (TROWS - 1)) + RADIUS
+        css = pack[:, 64:96].astype(jnp.int32)
+        for c in range(SEG // RUN):
+            sl = slice(n * NRUNS + c * DETS, n * NRUNS + (c + 1) * DETS)
+            cs = jnp.broadcast_to(css[:, c : c + 1], (DETS, 128))
+            idx_ref[sl, :] = (lane - cs) & (TCOLS - 1)
+            edge_ref[sl, :] = (ecol - cs) & (TCOLS - 1)
+            here = ((jnp.broadcast_to(ro3[:, c : c + 1], (DETS, 128)) ^ lane) & (OWN - 1)) == 0
+            mask_ref[sl, :] = jnp.where(here & (lane < 48), 1.0, 0.0)
+            hparts.append(jnp.where(here & (lane >= 48) & (lane < 56), w, 0.0).astype(BF))
     zh_ref[...] = mm(zhot, jnp.concatenate(hparts, axis=0))
-    fill_hot(keep_ref, ids_of_blocks(core_ref[0]), line_ref[...])
+    zero = jnp.zeros((NMODE, 32), F32)
+    rhs_ref[...] = jnp.concatenate(
+        [zero, packs[0][:, :NMODE].T, packs[1][:, :NMODE].T, zero], axis=1
+    )
 
 
 def lanes_of(v, k):
@@ -261,7 +271,7 @@
             )
             for i in groups
         ]
-    return jnp.concatenate(a, axis=0)[:, n : 2 * n] * down
+    return jnp.concatenate(a, axis=0)[:, n : 3 * n] * down
 
 
 def shifted_tiles(z, by):
@@ -272,12 +282,10 @@
 
 
 def clean_kernel(
-    core_ref, p_ref, q_ref, r_ref, s_ref, rhs_ref, w_ref, x_ref, synth_ref, tw_ref,
-    idx_ref, edge_ref, mask_ref, zhot_ref, zh_ref, send_hot_ref,
-    clean_ref, send_ref, vals_ref, rows_ref,
+    core_ref, p_ref, q_ref, r_ref, s_ref, rhs_ref, w_ref, x_ref, other_ref, synth_ref, tw_ref,
+    idx_ref, edge_ref, mask_ref, zhot_ref, zh_ref, hot_ref, other_hot_ref,
+    blocks_ref, out_hbm, clean_ref, sem,
 ):
-    w = w_ref[...]
-    w = jnp.concatenate([w, w], axis=1)
     p = (p_ref[...] + q_ref[...]) + (r_ref[...] + s_ref[...])
     coef = solve(p[2 * NMODE :, :], rhs_ref[...])
     ab = mm0_split(coef, jnp.concatenate([p[:NMODE, :], p[NMODE : 2 * NMODE, :]], axis=1))
@@ -292,18 +300,26 @@
     sh = synth_ref[:CHUNK, :]
     low = mm(hi, sh) + mm(lo, sh) + mm(hi, synth_ref[CHUNK:, :])
     runs = []
-    for c in range(NCHUNK):
-        part = w * (x_ref[:, c * CHUNK : (c + 1) * CHUNK] - low[c * DETS : (c + 1) * DETS, :])
-        clean_ref[:, c * CHUNK : (c + 1) * CHUNK] = part
-        runs.append(part[:, :RUN])
-        runs.append(part[:, RUN:])
+    for n, source in enumerate((x_ref, other_ref)):
+        w = w_ref[n * DETS : (n + 1) * DETS, :]
+        w = jnp.concatenate([w, w], axis=1)
+        for c in range(NCHUNK):
+            at = 2 * DETS * c + DETS * n
+            part = w * (source[:, c * CHUNK : (c + 1) * CHUNK] - low[at : at + DETS, :])
+            if n == 0:
+                clean_ref[:, c * CHUNK : (c + 1) * CHUNK] = part
+            runs.append(part[:, :RUN])
+            runs.append(part[:, RUN:])
+    copy = pltpu.make_async_copy(clean_ref, out_hbm, sem)
+    copy.start()
     run = jnp.concatenate(runs, axis=0)
     vals = jnp.concatenate(
         split(jnp.take_along_axis(run, idx_ref[...], axis=1, mode="promise_in_bounds")), axis=1
     )
-    vals_ref[...] = vals
     evals = jnp.take_along_axis(run, edge_ref[...], axis=1, mode="promise_in_bounds")
     evals = jnp.concatenate(split(evals * mask_ref[...]), axis=1)
+    s = mm(hot_ref[...], vals[:NRUNS]) + mm(other_hot_ref[...], vals[NRUNS:])
+    blocks_ref[...] = s[:, :128] + s[:, 128:]
     z = mm(zhot_ref[...], evals)
     z = (z[:, :128] + z[:, 128:] + zh_ref[...]).reshape(ZROWS // NT, NT, 128)
     left = shifted_tiles(z, -1)
@@ -321,30 +337,12 @@
     def both(v):
         return v[:nd] + jnp.concatenate([jnp.zeros((nd, NT, 64), F32), v[1:, :, :64]], axis=2)
 
-    rows14 = both(near)
-    rows15 = both(mine)
     core = core_ref[0]
-
-    def pick(v, which):
-        return jnp.concatenate(
-            [jnp.where(which == 1, v[2 * y + 1], v[2 * y]) for y in range(NY)], axis=0
-        )
-
-    rows_ref[0:NBLK, :] = pick(rows14, core)
-    rows_ref[NBLK : 2 * NBLK, :] = pick(rows15, core)
-    s = mm(send_hot_ref[...], vals)
-    send_ref[...] = s[:, :128] + s[:, 128:]
-    send_ref[pl.ds(14, NBLK, stride=BROWS), :] = pick(rows14, core ^ 1)
-    send_ref[pl.ds(15, NBLK, stride=BROWS), :] = pick(rows15, core ^ 1)
-
-
-def keep_kernel(hot_ref, vals_ref, rows_ref, clean_ref, keep_ref, out_hbm, sem):
-    copy = pltpu.make_async_copy(clean_ref, out_hbm, sem)
-    copy.start()
-    s = mm(hot_ref[...], vals_ref[...])
-    keep_ref[...] = s[:, :128] + s[:, 128:]
-    keep_ref[pl.ds(14, NBLK, stride=BROWS), :] = rows_ref[0:NBLK, :]
-    keep_ref[pl.ds(15, NBLK, stride=BROWS), :] = rows_ref[NBLK : 2 * NBLK, :]
+    for row, values in ((14, both(near)), (15, both(mine))):
+        picked = [
+            jnp.where(core == 1, values[2 * y + 1], values[2 * y]) for y in range(NY)
+        ]
+        blocks_ref[pl.ds(row, NBLK, stride=BROWS), :] = jnp.concatenate(picked, axis=0)
     copy.wait()
 
 
@@ -421,53 +419,49 @@
     core = lax.axis_index("core").reshape(1)
     small = (DETS, SEG // RUN)
     big = (NBLK * BROWS, NRUNS)
-    part, x, synth, tw, rhs, w, ro, cs, line, zid = call(
+    swap = [(0, 1), (1, 0)]
+    mate_x = lax.ppermute(timestreams, "core", swap)
+    part, x, synth, tw, pack, line = call(
         analysis_kernel,
         [
             sds((2 * NMODE + 8, FKEEP)), sds((DETS, SEG)), sds((2 * CHUNK, 2 * FKEEP), BF),
-            sds((NCHUNK, 2 * FKEEP)), sds((NMODE, 128)), sds((DETS, 128)),
-            sds(small, I32), sds(small, I32), sds((1, NRUNS), I32), sds((1, NRUNS), I32),
+            sds((NCHUNK, 2 * FKEEP)), sds((DETS, 128)), sds((1, NRUNS), I32),
         ],
         [HBM] * 9, "analysis", 400_000_000,
         timestreams, templates, validity.reshape(1, DETS), tile_index, row_offset, col_start,
         jnp.asarray(basis), jnp.asarray(synth), jnp.asarray(tw),
         scratch=[
             pltpu.VMEM((DETS, NMODE), F32), pltpu.VMEM((1, DETS), I32), pltpu.VMEM(small, I32),
+            pltpu.VMEM(small, I32), pltpu.VMEM(small, I32),
             pltpu.VMEM((2 * CHUNK, 2 * FKEEP), BF), pltpu.SemaphoreType.DMA((8 + SEG // XPIECE,)),
         ],
     )
-    other = lax.ppermute(part, "core", [(0, 1), (1, 0)])
-    (send_hot,) = call(
+    mate = lax.ppermute(part, "core", swap)
+    (hot,) = call(
         first_index_kernel, [sds(big, BF)], [SMEM, VMEM], "index1", 100_000_000, core, line
     )
-    part, send_hot, line = lax.optimization_barrier((part + other, send_hot, line))
+    mate_pack = lax.ppermute(pack, "core", swap)
+    part, hot, line, mate_pack = lax.optimization_barrier((part + mate, hot, line, mate_pack))
     others = [lax.ppermute(part, "y", [(k, k ^ m) for k in range(NY)]) for m in (2, 3, 1)]
-    keep_hot, zhot, idx, edge, mask, zh = call(
+    twice = (2 * NRUNS, 128)
+    mate_hot, zhot, idx, edge, mask, zh, rhs, w = call(
         second_index_kernel,
         [
-            sds(big, BF), sds((ZROWS, NRUNS), BF),
-            sds((NRUNS, 128), I32), sds((NRUNS, 128), I32),
-            sds((NRUNS, 128)), sds((ZROWS, 128)),
+            sds(big, BF), sds((ZROWS, 2 * NRUNS), BF), sds(twice, I32), sds(twice, I32),
+            sds(twice), sds((ZROWS, 128)), sds((NMODE, 128)), sds((2 * DETS, 128)),
         ],
-        [SMEM] + [VMEM] * 5, "index2", 100_000_000,
-        core, line, zid, ro, cs, w,
-    )
-    cleaned, send, vals, rows = call(
+        [SMEM] + [VMEM] * 3, "index2", 100_000_000,
+        core, line, pack, mate_pack,
+    )
+    blocks, cleaned = call(
         clean_kernel,
-        [
-            sds((DETS, SEG)), sds((NBLK * BROWS, 128)),
-            sds((NRUNS, 256), BF), sds((2 * NBLK, 128)),
-        ],
-        [SMEM] + [VMEM] * 15, "clean", 1_000_000_000,
-        core, part, *others, rhs, w, x, synth, tw, idx, edge, mask, zhot, zh, send_hot,
-    )
-    got = lax.ppermute(send, "core", [(0, 1), (1, 0)])
-    keep, cleaned = call(
-        keep_kernel, [sds((NBLK * BROWS, 128)), sds((DETS, SEG))], [VMEM] * 4, "keep",
-        500_000_000, keep_hot, vals, rows, cleaned,
-        out_specs=[VMEM, HBM], scratch=[pltpu.SemaphoreType.DMA],
-    )
-    blocks = lax.all_to_all(keep + got, ("y", "z", "x"), 0, 0, tiled=True)
+        [sds((NBLK * BROWS, 128)), sds((DETS, SEG))],
+        [SMEM] + [VMEM] * 17, "clean", 2_000_000_000,
+        core, part, *others, rhs, w, x, mate_x, synth, tw, idx, edge, mask, zhot, zh, hot, mate_hot,
+        out_specs=[VMEM, HBM],
+        scratch=[pltpu.VMEM((DETS, SEG), F32), pltpu.SemaphoreType.DMA],
+    )
+    blocks = lax.all_to_all(blocks, ("y", "z", "x"), 0, 0, tiled=True)
     (beamed,) = call(
         beam_kernel, [sds((OWN, TCOLS))], [VMEM], "beam", 1_000_000, blocks
     )

time: 42.2 us -> 40.2 us (0.953)
  blocking collectives: 23.8 us -> 21.4 us
  waiting for transfers between devices: 3.91 us -> 2.84 us
  starting transfers between devices: 4.51 us -> 5.31 us
  Pallas kernels: 9.05 us -> 9.77 us
    all_to_all x1, blocking collectives: 23.8 us -> 21.4 us  [body(): blocks = lax.all_to_all(blocks, ('y', 'z', 'x'), 0, 0, tiled=True)]
    ppermute x2 -> x3, waiting for transfers between devices: 1.42 us -> 0.22 us  [the longest x1 0.22 us: body(): mate_pack = lax.ppermute(pack, 'core', swap)]
    pallas_call x6 -> x5, Pallas kernels: 9.05 us -> 9.77 us  [call(): pl.pallas_call(kernel, out_shape=outs, in_specs=specs, out_specs=out_spec...]
    ppermute x2 -> x3, starting transfers between devices: 0.17 us -> 0.75 us  [the longest x1 0.57 us: body(): mate = lax.ppermute(part, 'core', swap)]
  transfers between devices with their start and end apart: 5 -> 6, of which waited for: 3 -> 3; matrix products, arithmetic and copies ran while one was open for 0% -> 0% of each run, Pallas kernels for 8% -> 12%
where the time goes in v7:
time: 40.2 us; the launch traced here: 40 us
  blocking collectives  21.4 us (53%)
  Pallas kernels  9.77 us (24%)
  starting transfers between devices  5.31 us (13%)
  waiting for transfers between devices  2.84 us (7%)
  between operations  0.69 us (2%)
    all_to_all x1, blocking collectives, body(): blocks = lax.all_to_all(blocks, ('y', 'z', 'x'), 0, 0, tiled=True)  21.4 us
    pallas_call x5, Pallas kernels, call(): pl.pallas_call(kernel, out_shape=outs, in_specs=specs, out_specs=out_spec...  9.77 us
    ppermute x3, starting transfers between devices, body(): lax.ppermute(part, 'y', [(k, k ^ m) for k in range(NY)])  4.56 us
    ppermute x3, waiting for transfers between devices, body(): lax.ppermute(part, 'y', [(k, k ^ m) for k in range(NY)])  2.62 us
  transfers between devices with their start and end apart: 6, of which 3 were waited for; matrix products, arithmetic and copies ran while one was open for 0% of the time, Pallas kernels for 12%

profile of v7, /device:TPU:0, one launch (start us, length us, event | category | flops | bytes accessed | tf_op | source)
XLA Modules:
  0.0 40.0 jit_solution(2237744191913536844)
XLA Ops:
  0.6 0.1 collective-permute-start.5
  0.7 2.0 %analysis.1 = (f32[72,128]{1,0:T(8,128)S(1)}, f32[32,4096]{1,0:T(8,128)S(1)}, bf16[512,256]{1,0:T(8,128)(2,1)S(1)}, f32[16,256]{1,0:T(8,128)S(1)}, f32[32,128]{1,0:T(8,128)S(1)}, /*index=5*/s32[1,1024]{1,0:T(1,128)S(1)}) custom-call(f32[32,4096]{1,0:T(8,128)} %x_hbm.1, f32[32,32]{1,0:T(8,128)} %t_hbm.1, s32[1,32]{1,0:T(1,128)} %bitcast.6, s32[32,32]{1,0:T(8,128)} %ti_hbm.1, ...), custom_call_target="tpu_custom_call" | custom-call | flops 400000000 | bytes 2728064 | tf_op jit(solution)/shard_map/analysis/pallas_call | solution.py:398
  2.7 0.6 %collective-permute-start = (f32[72,128]{1,0:T(8,128)S(1)}, f32[72,128]{1,0:T(8,128)S(1)}, u32[]{:S(2)}, u32[]{:S(2)}) collective-permute-start(f32[72,128]{1,0:T(8,128)S(1)} %get-tuple-element.22), channel_id=1, source_target_pairs={{0,16},{16,0},{1,17},{17,1},{2,18},{18,2},{3,19},{19,3},{4,20},{20... | collective-permute-start | bytes 110600 | tf_op jit(solution)/shard_map/ppermute | solution.py:439
  3.3 0.1 collective-permute-start.1
  3.4 0.8 %index1.1.hot_ref = bf16[1024,1024]{1,0:T(8,128)(2,1)S(1)} custom-call(s32[1]{0:T(128)} %bitcast.core_ref, s32[1,1024]{1,0:T(1,128)S(1)} %get-tuple-element.26.line_ref), custom_call_target="tpu_custom_call" | custom-call | flops 100000000 | bytes 4198404 | tf_op jit(solution)/shard_map/index1/pallas_call | solution.py:398
  4.2 0.0 collective-permute-done
  4.3 0.2 collective-permute-done.1.other_ref
  4.5 1.7 %collective-permute-start.4 = (f32[72,128]{1,0:T(8,128)S(1)}, f32[72,128]{1,0:T(8,128)S(1)}, u32[]{:S(2)}, u32[]{:S(2)}) collective-permute-start(f32[72,128]{1,0:T(8,128)S(1)} %add.3.p_ref), channel_id=1, source_target_pairs={{0,32},{32,0},{64,96},{96,64},{1,33},{33,1},{65,97},{97,65},{2,34}... | collective-permute-start | bytes 110600 | tf_op jit(solution)/shard_map/ppermute | solution.py:445
  6.1 2.2 %collective-permute-start.3 = (f32[72,128]{1,0:T(8,128)S(1)}, f32[72,128]{1,0:T(8,128)S(1)}, u32[]{:S(2)}, u32[]{:S(2)}) collective-permute-start(f32[72,128]{1,0:T(8,128)S(1)} %add.3.p_ref), channel_id=1, source_target_pairs={{0,96},{32,64},{64,32},{96,0},{1,97},{33,65},{65,33},{97,1},{2,98}... | collective-permute-start | bytes 110600 | tf_op jit(solution)/shard_map/ppermute | solution.py:445
  8.3 0.7 %collective-permute-start.2 = (f32[72,128]{1,0:T(8,128)S(1)}, f32[72,128]{1,0:T(8,128)S(1)}, u32[]{:S(2)}, u32[]{:S(2)}) collective-permute-start(f32[72,128]{1,0:T(8,128)S(1)} %add.3.p_ref), channel_id=1, source_target_pairs={{0,64},{32,96},{64,0},{96,32},{1,65},{33,97},{65,1},{97,33},{2,66}... | collective-permute-start | bytes 110600 | tf_op jit(solution)/shard_map/ppermute | solution.py:445
  9.0 2.1 %index2.1 = (bf16[1024,1024]{1,0:T(8,128)(2,1)S(1)}, bf16[144,2048]{1,0:T(8,128)(2,1)S(1)}, s32[2048,128]{1,0:T(8,128)S(1)}, s32[2048,128]{1,0:T(8,128)S(1)}, f3...) custom-call(s32[1]{0:T(128)} %bitcast.core_ref, ...), custom_call_target="tpu_custom_call" | custom-call | flops 100000000 | bytes 8679428 | tf_op jit(solution)/shard_map/index2/pallas_call | solution.py:398
  11.2 0.0 collective-permute-done.4.s_ref
  11.2 0.1 collective-permute-done.3.r_ref
  11.3 2.5 %collective-permute-done.2.q_ref = f32[72,128]{1,0:T(8,128)S(1)} collective-permute-done((f32[72,128]{1,0:T(8,128)S(1)}, f32[72,128]{1,0:T(8,128)S(1)}, u32[]{:S(2)}, u32[]{:S(2)}) %collective-permute-start.2) | collective-permute-done | bytes 36896 | tf_op jit(solution)/shard_map/ppermute | solution.py:445
  13.8 0.0 collective-permute-done.5.other_ref
  13.8 4.0 %clean.1 = (f32[1024,128]{1,0:T(8,128)S(1)}, f32[32,4096]{1,0:T(8,128)}) custom-call(s32[1]{0:T(128)} %bitcast.core_ref, f32[72,128]{1,0:T(8,128)S(1)} %add.3.p_ref, f32[72,128]{1,0:T(8,128)S(1)} %collective-permute-done.2.q_ref, f32[72,128]{1,0:T(8,128)S(1)} %collective-permute-done.3.r_ref, f32[72,128]{1,0:T(8,128)S(1)} %collective-permute-done.4.s_ref, ...), custom_call_target="tpu_custom_call" | custom-call | flops 2000000000 | bytes 15622148 | tf_op jit(solution)/shard_map/clean/pallas_call | solution.py:398
  17.8 21.4 %all_to_all.11 = f32[64,16,128]{2,1,0:T(8,128)S(1)} all-to-all(f32[64,16,128]{2,1,0:T(8,128)S(1)} %bitcast.5), channel_id=1, replica_groups=mesh['y'=4,'core'=2,'z'=4,'x'=4] {'y','z','x'}, dimensions={0} | all-to-all | bytes 1048576 | tf_op jit(solution)/shard_map/all_to_all | solution.py:464
  39.2 0.8 %beam.1 = f32[8,128]{1,0:T(8,128)} custom-call(f32[1024,128]{1,0:T(8,128)S(1)} %bitcast.4), custom_call_target="tpu_custom_call" | custom-call | flops 1000000 | bytes 528384 | tf_op jit(solution)/shard_map/beam/pallas_call | solution.py:398
  (1 shorter events, 0.0 us)
Async XLA Ops:
  0.6 13.2 %collective-permute-start.5 = (f32[32,4096]{1,0:T(8,128)}, f32[32,4096]{1,0:T(8,128)S(1)}, u32[]{:S(2)}, u32[]{:S(2)}) collective-permute-start(f32[32,4096]{1,0:T(8,128)} %x_hbm.1), channel_id=1, source_target_pairs={{0,16},{16,0},{1,17},{17,1},{2,18},{18,2},{3,19},{19,3},{4,20},{20... | collective-permute-start | bytes 1572872 | tf_op jit(solution)/shard_map/ppermute | solution.py:423
  2.7 1.5 %collective-permute-start = (f32[72,128]{1,0:T(8,128)S(1)}, f32[72,128]{1,0:T(8,128)S(1)}, u32[]{:S(2)}, u32[]{:S(2)}) collective-permute-start(f32[72,128]{1,0:T(8,128)S(1)} %get-tuple-element.22), channel_id=1, source_target_pairs={{0,16},{16,0},{1,17},{17,1},{2,18},{18,2},{3,19},{19,3},{4,20},{20... | collective-permute-start | bytes 110600 | tf_op jit(solution)/shard_map/ppermute | solution.py:439
  3.3 1.2 %collective-permute-start.1 = (f32[32,128]{1,0:T(8,128)S(1)}, f32[32,128]{1,0:T(8,128)S(1)}, u32[]{:S(2)}, u32[]{:S(2)}) collective-permute-start(f32[32,128]{1,0:T(8,128)S(1)} %get-tuple-element.24.pack_ref), channel_id=1, source_target_pairs={{0,16},{16,0},{1,17},{17,1},{2,18},{18,2},{3,19},{19,3},{4,20},{20... | collective-permute-start | bytes 49160 | tf_op jit(solution)/shard_map/ppermute | solution.py:443
  4.5 6.7 %collective-permute-start.4 = (f32[72,128]{1,0:T(8,128)S(1)}, f32[72,128]{1,0:T(8,128)S(1)}, u32[]{:S(2)}, u32[]{:S(2)}) collective-permute-start(f32[72,128]{1,0:T(8,128)S(1)} %add.3.p_ref), channel_id=1, source_target_pairs={{0,32},{32,0},{64,96},{96,64},{1,33},{33,1},{65,97},{97,65},{2,34}... | collective-permute-start | bytes 110600 | tf_op jit(solution)/shard_map/ppermute | solution.py:445
  6.1 5.2 %collective-permute-start.3 = (f32[72,128]{1,0:T(8,128)S(1)}, f32[72,128]{1,0:T(8,128)S(1)}, u32[]{:S(2)}, u32[]{:S(2)}) collective-permute-start(f32[72,128]{1,0:T(8,128)S(1)} %add.3.p_ref), channel_id=1, source_target_pairs={{0,96},{32,64},{64,32},{96,0},{1,97},{33,65},{65,33},{97,1},{2,98}... | collective-permute-start | bytes 110600 | tf_op jit(solution)/shard_map/ppermute | solution.py:445
  8.3 5.5 %collective-permute-start.2 = (f32[72,128]{1,0:T(8,128)S(1)}, f32[72,128]{1,0:T(8,128)S(1)}, u32[]{:S(2)}, u32[]{:S(2)}) collective-permute-start(f32[72,128]{1,0:T(8,128)S(1)} %add.3.p_ref), channel_id=1, source_target_pairs={{0,64},{32,96},{64,0},{96,32},{1,65},{33,97},{65,1},{97,33},{2,66}... | collective-permute-start | bytes 110600 | tf_op jit(solution)/shard_map/ppermute | solution.py:445

commit v8 on v7

--- a/solution.py
+++ b/solution.py
@@ -91,14 +91,14 @@
 
 
 def run_row(ids):
-    flat = ids.astype(F32).T
+    flat = ids.T
     parts = [flat[c : c + 1, :] for c in range(SEG // RUN)]
     return jnp.concatenate(parts, axis=1).astype(jnp.int32)
 
 
 def analysis_kernel(
     x_hbm, t_hbm, v_hbm, ti_hbm, ro_hbm, cs_hbm, basis_hbm, synth_hbm, tw_hbm,
-    out_ref, x_ref, synth_ref, tw_ref, pack_ref, line_ref,
+    out_ref, x_ref, synth_ref, tw_ref, pack_ref,
     t_ref, v_ref, ti_ref, ro_ref, cs_ref, basis_ref, sems,
 ):
     pieces = [
@@ -129,7 +129,6 @@
     for copy in copies[-5:-2]:
         copy.wait()
     line = ti_ref[...] * TROWS + ro_ref[...]
-    line_ref[...] = run_row(line)
     pack_ref[...] = jnp.concatenate(
         [t, line.astype(F32), cs_ref[...].astype(F32), jnp.broadcast_to(w, (DETS, 32))], axis=1
     )
@@ -182,8 +181,10 @@
         ref[:, sl] = jnp.where(ids == line[:, sl], 1.0, 0.0).astype(BF)
 
 
-def first_index_kernel(core_ref, line_ref, hot_ref):
-    fill_hot(hot_ref, ids_of_blocks(core_ref[0]), line_ref[...])
+def first_index_kernel(core_ref, pack_ref, hot_ref, line_ref):
+    line = run_row(pack_ref[:, 32:64])
+    line_ref[...] = line
+    fill_hot(hot_ref, ids_of_blocks(core_ref[0]), line)
 
 
 def second_index_kernel(
@@ -192,7 +193,7 @@
 ):
     packs = (pack_ref[...], other_ref[...])
     lines = [pack[:, 32:64].astype(jnp.int32) for pack in packs]
-    rows = (line_ref[...], run_row(lines[1]))
+    rows = (line_ref[...], run_row(packs[1][:, 32:64]))
     fill_hot(hot_ref, ids_of_blocks(core_ref[0]), rows[1])
     line = jnp.concatenate(rows, axis=1)
     zid = (((line & (TROWS - 1)) + RADIUS) >> 3) * NT + (line >> 6)
@@ -421,11 +422,11 @@
     big = (NBLK * BROWS, NRUNS)
     swap = [(0, 1), (1, 0)]
     mate_x = lax.ppermute(timestreams, "core", swap)
-    part, x, synth, tw, pack, line = call(
+    part, x, synth, tw, pack = call(
         analysis_kernel,
         [
             sds((2 * NMODE + 8, FKEEP)), sds((DETS, SEG)), sds((2 * CHUNK, 2 * FKEEP), BF),
-            sds((NCHUNK, 2 * FKEEP)), sds((DETS, 128)), sds((1, NRUNS), I32),
+            sds((NCHUNK, 2 * FKEEP)), sds((DETS, 128)),
         ],
         [HBM] * 9, "analysis", 400_000_000,
         timestreams, templates, validity.reshape(1, DETS), tile_index, row_offset, col_start,
@@ -437,12 +438,15 @@
         ],
     )
     mate = lax.ppermute(part, "core", swap)
-    (hot,) = call(
-        first_index_kernel, [sds(big, BF)], [SMEM, VMEM], "index1", 100_000_000, core, line
+    hot, line = call(
+        first_index_kernel, [sds(big, BF), sds((1, NRUNS), I32)], [SMEM, VMEM], "index1",
+        100_000_000, core, pack,
     )
     mate_pack = lax.ppermute(pack, "core", swap)
     part, hot, line, mate_pack = lax.optimization_barrier((part + mate, hot, line, mate_pack))
-    others = [lax.ppermute(part, "y", [(k, k ^ m) for k in range(NY)]) for m in (2, 3, 1)]
+    others = [
+        lax.ppermute(part, "y", [(k, (k + m) % NY) for k in range(NY)]) for m in (1, 3, 2)
+    ]
     twice = (2 * NRUNS, 128)
     mate_hot, zhot, idx, edge, mask, zh, rhs, w = call(
         second_index_kernel,

time: 40.2 us -> 40.8 us (1.015)
  starting transfers between devices: 5.31 us -> 6.13 us
  waiting for transfers between devices: 2.84 us -> 2.07 us
  Pallas kernels: 9.77 us -> 10.2 us
    ppermute x3, starting transfers between devices: 4.56 us -> 5.38 us  [body(): lax.ppermute(part, 'y', [(k, (k + m) % NY) for k in range(NY)])]
    ppermute x3, waiting for transfers between devices: 2.62 us -> 2.06 us  [body(): lax.ppermute(part, 'y', [(k, (k + m) % NY) for k in range(NY)])]
    pallas_call x5, Pallas kernels: 9.77 us -> 10.2 us  [call(): pl.pallas_call(kernel, out_shape=outs, in_specs=specs, out_specs=out_spec...]
  transfers between devices with their start and end apart: 6 -> 6, of which waited for: 3 -> 1; matrix products, arithmetic and copies ran while one was open for 0% -> 0% of each run, Pallas kernels for 12% -> 13%
where the time goes in v8:
time: 40.8 us; the launch traced here: 40.6 us
  blocking collectives  21.5 us (53%)
  Pallas kernels  10.2 us (25%)
  starting transfers between devices  6.13 us (15%)
  waiting for transfers between devices  2.07 us (5%)
  between operations  0.71 us (2%)
    all_to_all x1, blocking collectives, body(): blocks = lax.all_to_all(blocks, ('y', 'z', 'x'), 0, 0, tiled=True)  21.5 us
    pallas_call x5, Pallas kernels, call(): pl.pallas_call(kernel, out_shape=outs, in_specs=specs, out_specs=out_spec...  10.2 us
    ppermute x3, starting transfers between devices, body(): lax.ppermute(part, 'y', [(k, (k + m) % NY) for k in range(NY)])  5.38 us
    ppermute x3, waiting for transfers between devices, body(): lax.ppermute(part, 'y', [(k, (k + m) % NY) for k in range(NY)])  2.06 us
  transfers between devices with their start and end apart: 6, of which 1 were waited for; matrix products, arithmetic and copies ran while one was open for 0% of the time, Pallas kernels for 13%

profile of v8, /device:TPU:0, one launch (start us, length us, event | category | flops | bytes accessed | tf_op | source)
XLA Modules:
  0.0 40.6 jit_solution(17126507910769565160)
XLA Ops:
  0.6 0.1 collective-permute-start.5
  0.7 1.9 %analysis.1 = (f32[72,128]{1,0:T(8,128)S(1)}, f32[32,4096]{1,0:T(8,128)S(1)}, bf16[512,256]{1,0:T(8,128)(2,1)S(1)}, f32[16,256]{1,0:T(8,128)S(1)}, f32[32,128]{1,0:T(8,128)S(1)}) custom-call(f32[32,4096]{1,0:T(8,128)} %x_hbm.1, f32[32,32]{1,0:T(8,128)} %t_hbm.1, s32[1,32]{1,0:T(1,128)} %bitcast.6, s32[32,32]{1,0:T(8,128)} %ti_hbm.1, s32[32,32]{1,0:T(8,128)} %ro_hbm.1, ...), custom_call_target="tpu_custom_call" | custom-call | flops 400000000 | bytes 2723968 | tf_op jit(solution)/shard_map/analysis/pallas_call | solution.py:399
  2.6 0.6 %collective-permute-start = (f32[72,128]{1,0:T(8,128)S(1)}, f32[72,128]{1,0:T(8,128)S(1)}, u32[]{:S(2)}, u32[]{:S(2)}) collective-permute-start(f32[72,128]{1,0:T(8,128)S(1)} %get-tuple-element.23), channel_id=1, source_target_pairs={{0,16},{16,0},{1,17},{17,1},{2,18},{18,2},{3,19},{19,3},{4,20},{20... | collective-permute-start | bytes 110600 | tf_op jit(solution)/shard_map/ppermute | solution.py:440
  3.2 0.1 collective-permute-start.1
  3.3 1.4 %index1.1 = (bf16[1024,1024]{1,0:T(8,128)(2,1)S(1)}, s32[1,1024]{1,0:T(1,128)S(1)}) custom-call(s32[1]{0:T(128)} %bitcast.core_ref, f32[32,128]{1,0:T(8,128)S(1)} %get-tuple-element.24.pack_ref), custom_call_target="tpu_custom_call" | custom-call | flops 100000000 | bytes 4214788 | tf_op jit(solution)/shard_map/index1/pallas_call | solution.py:399
  4.7 0.0 collective-permute-done
  4.7 0.0 collective-permute-done.1.other_ref
  4.7 3.4 %collective-permute-start.4 = (f32[72,128]{1,0:T(8,128)S(1)}, f32[72,128]{1,0:T(8,128)S(1)}, u32[]{:S(2)}, u32[]{:S(2)}) collective-permute-start(f32[72,128]{1,0:T(8,128)S(1)} %add.3.p_ref), channel_id=1, source_target_pairs={{0,64},{32,96},{64,0},{96,32},{1,65},{33,97},{65,1},{97,33},{2,66}... | collective-permute-start | bytes 110600 | tf_op jit(solution)/shard_map/ppermute | solution.py:448
  8.1 1.1 %collective-permute-start.3 = (f32[72,128]{1,0:T(8,128)S(1)}, f32[72,128]{1,0:T(8,128)S(1)}, u32[]{:S(2)}, u32[]{:S(2)}) collective-permute-start(f32[72,128]{1,0:T(8,128)S(1)} %add.3.p_ref), channel_id=1, source_target_pairs={{0,96},{32,0},{64,32},{96,64},{1,97},{33,1},{65,33},{97,65},{2,98}... | collective-permute-start | bytes 110600 | tf_op jit(solution)/shard_map/ppermute | solution.py:448
  9.1 1.0 %collective-permute-start.2 = (f32[72,128]{1,0:T(8,128)S(1)}, f32[72,128]{1,0:T(8,128)S(1)}, u32[]{:S(2)}, u32[]{:S(2)}) collective-permute-start(f32[72,128]{1,0:T(8,128)S(1)} %add.3.p_ref), channel_id=1, source_target_pairs={{0,32},{32,64},{64,96},{96,0},{1,33},{33,65},{65,97},{97,1},{2,34}... | collective-permute-start | bytes 110600 | tf_op jit(solution)/shard_map/ppermute | solution.py:448
  10.1 2.1 %index2.1 = (bf16[1024,1024]{1,0:T(8,128)(2,1)S(1)}, bf16[144,2048]{1,0:T(8,128)(2,1)S(1)}, s32[2048,128]{1,0:T(8,128)S(1)}, s32[2048,128]{1,0:T(8,128)S(1)}, f3...) custom-call(s32[1]{0:T(128)} %bitcast.core_ref, ...), custom_call_target="tpu_custom_call" | custom-call | flops 100000000 | bytes 8679428 | tf_op jit(solution)/shard_map/index2/pallas_call | solution.py:399
  12.2 0.0 collective-permute-done.4.s_ref
  12.2 0.0 collective-permute-done.3.r_ref
  12.2 2.1 %collective-permute-done.2.q_ref = f32[72,128]{1,0:T(8,128)S(1)} collective-permute-done((f32[72,128]{1,0:T(8,128)S(1)}, f32[72,128]{1,0:T(8,128)S(1)}, u32[]{:S(2)}, u32[]{:S(2)}) %collective-permute-start.2) | collective-permute-done | bytes 36896 | tf_op jit(solution)/shard_map/ppermute | solution.py:448
  14.3 0.0 collective-permute-done.5.other_ref
  14.3 4.0 %clean.1 = (f32[1024,128]{1,0:T(8,128)S(1)}, f32[32,4096]{1,0:T(8,128)}) custom-call(s32[1]{0:T(128)} %bitcast.core_ref, f32[72,128]{1,0:T(8,128)S(1)} %add.3.p_ref, f32[72,128]{1,0:T(8,128)S(1)} %collective-permute-done.2.q_ref, f32[72,128]{1,0:T(8,128)S(1)} %collective-permute-done.3.r_ref, f32[72,128]{1,0:T(8,128)S(1)} %collective-permute-done.4.s_ref, ...), custom_call_target="tpu_custom_call" | custom-call | flops 2000000000 | bytes 15622148 | tf_op jit(solution)/shard_map/clean/pallas_call | solution.py:399
  18.4 21.5 %all_to_all.11 = f32[64,16,128]{2,1,0:T(8,128)S(1)} all-to-all(f32[64,16,128]{2,1,0:T(8,128)S(1)} %bitcast.5), channel_id=1, replica_groups=mesh['y'=4,'core'=2,'z'=4,'x'=4] {'y','z','x'}, dimensions={0} | all-to-all | bytes 1048576 | tf_op jit(solution)/shard_map/all_to_all | solution.py:468
  39.8 0.8 %beam.1 = f32[8,128]{1,0:T(8,128)} custom-call(f32[1024,128]{1,0:T(8,128)S(1)} %bitcast.4), custom_call_target="tpu_custom_call" | custom-call | flops 1000000 | bytes 528384 | tf_op jit(solution)/shard_map/beam/pallas_call | solution.py:399
  (1 shorter events, 0.0 us)
Async XLA Ops:
  0.6 13.7 %collective-permute-start.5 = (f32[32,4096]{1,0:T(8,128)}, f32[32,4096]{1,0:T(8,128)S(1)}, u32[]{:S(2)}, u32[]{:S(2)}) collective-permute-start(f32[32,4096]{1,0:T(8,128)} %x_hbm.1), channel_id=1, source_target_pairs={{0,16},{16,0},{1,17},{17,1},{2,18},{18,2},{3,19},{19,3},{4,20},{20... | collective-permute-start | bytes 1572872 | tf_op jit(solution)/shard_map/ppermute | solution.py:424
  2.6 2.1 %collective-permute-start = (f32[72,128]{1,0:T(8,128)S(1)}, f32[72,128]{1,0:T(8,128)S(1)}, u32[]{:S(2)}, u32[]{:S(2)}) collective-permute-start(f32[72,128]{1,0:T(8,128)S(1)} %get-tuple-element.23), channel_id=1, source_target_pairs={{0,16},{16,0},{1,17},{17,1},{2,18},{18,2},{3,19},{19,3},{4,20},{20... | collective-permute-start | bytes 110600 | tf_op jit(solution)/shard_map/ppermute | solution.py:440
  3.2 1.5 %collective-permute-start.1 = (f32[32,128]{1,0:T(8,128)S(1)}, f32[32,128]{1,0:T(8,128)S(1)}, u32[]{:S(2)}, u32[]{:S(2)}) collective-permute-start(f32[32,128]{1,0:T(8,128)S(1)} %get-tuple-element.24.pack_ref), channel_id=1, source_target_pairs={{0,16},{16,0},{1,17},{17,1},{2,18},{18,2},{3,19},{19,3},{4,20},{20... | collective-permute-start | bytes 49160 | tf_op jit(solution)/shard_map/ppermute | solution.py:445
  4.7 7.5 %collective-permute-start.4 = (f32[72,128]{1,0:T(8,128)S(1)}, f32[72,128]{1,0:T(8,128)S(1)}, u32[]{:S(2)}, u32[]{:S(2)}) collective-permute-start(f32[72,128]{1,0:T(8,128)S(1)} %add.3.p_ref), channel_id=1, source_target_pairs={{0,64},{32,96},{64,0},{96,32},{1,65},{33,97},{65,1},{97,33},{2,66}... | collective-permute-start | bytes 110600 | tf_op jit(solution)/shard_map/ppermute | solution.py:448
  8.1 4.2 %collective-permute-start.3 = (f32[72,128]{1,0:T(8,128)S(1)}, f32[72,128]{1,0:T(8,128)S(1)}, u32[]{:S(2)}, u32[]{:S(2)}) collective-permute-start(f32[72,128]{1,0:T(8,128)S(1)} %add.3.p_ref), channel_id=1, source_target_pairs={{0,96},{32,0},{64,32},{96,64},{1,97},{33,1},{65,33},{97,65},{2,98}... | collective-permute-start | bytes 110600 | tf_op jit(solution)/shard_map/ppermute | solution.py:448
  9.1 5.2 %collective-permute-start.2 = (f32[72,128]{1,0:T(8,128)S(1)}, f32[72,128]{1,0:T(8,128)S(1)}, u32[]{:S(2)}, u32[]{:S(2)}) collective-permute-start(f32[72,128]{1,0:T(8,128)S(1)} %add.3.p_ref), channel_id=1, source_target_pairs={{0,32},{32,64},{64,96},{96,0},{1,33},{33,65},{65,97},{97,1},{2,34}... | collective-permute-start | bytes 110600 | tf_op jit(solution)/shard_map/ppermute | solution.py:448

commit v9 on v7

--- a/solution.py
+++ b/solution.py
@@ -20,7 +20,7 @@
 DETS = 32
 CHUNK = 256
 NCHUNK = SEG // CHUNK
-XPIECE = 4096
+WIDE = 1024
 NRUNS = DETS * SEG // RUN
 NT = 16
 NY = 4
@@ -30,6 +30,8 @@
 ZROWS = (TROWS // OWN + 1) * NT
 BF = jnp.bfloat16
 F32 = jnp.float32
+I32 = jnp.int32
+PART = 2 * NMODE + 8
 
 
 def split_np(a):
@@ -47,7 +49,9 @@
     theta = 2.0 * np.pi * (c * CHUNK * k % SEG) / SEG
     twiddle = np.concatenate([np.cos(theta), np.sin(theta)], axis=1).astype(np.float32)
     scale = np.where(np.arange(FKEEP) == 0, 1.0 / SEG, 2.0 / SEG)
-    synth = basis.T * np.concatenate([scale, scale])[:, None]
+    phi = 2.0 * np.pi * (np.arange(WIDE)[:, None] * k % SEG) / SEG
+    synth = np.concatenate([np.cos(phi), np.sin(phi)], axis=1).T
+    synth = synth * np.concatenate([scale, scale])[:, None]
     return np.concatenate(split_np(basis)), np.concatenate(split_np(synth)), twiddle
 
 
@@ -98,18 +102,14 @@
 
 def analysis_kernel(
     x_hbm, t_hbm, v_hbm, ti_hbm, ro_hbm, cs_hbm, basis_hbm, synth_hbm, tw_hbm,
-    out_ref, x_ref, synth_ref, tw_ref, pack_ref, line_ref,
+    out_ref, x_ref, synth_ref, tw_ref, line_ref,
     t_ref, v_ref, ti_ref, ro_ref, cs_ref, basis_ref, sems,
 ):
-    pieces = [
-        (x_hbm.at[:, pl.ds(n * XPIECE, XPIECE)], x_ref.at[:, pl.ds(n * XPIECE, XPIECE)])
-        for n in range(SEG // XPIECE)
-    ]
     copies = [
         pltpu.make_async_copy(src, dst, sems.at[n])
         for n, (src, dst) in enumerate(
             [
-                (t_hbm, t_ref), (v_hbm, v_ref), (basis_hbm, basis_ref), *pieces,
+                (t_hbm, t_ref), (v_hbm, v_ref), (basis_hbm, basis_ref), (x_hbm, x_ref),
                 (ti_hbm, ti_ref), (ro_hbm, ro_ref), (cs_hbm, cs_ref),
                 (tw_hbm, tw_ref), (synth_hbm, synth_ref),
             ]
@@ -123,35 +123,33 @@
     t = t_ref[...]
     wt = t * w
     gram = mm0(wt, t)
-    out_ref[2 * NMODE :, :] = jnp.concatenate(
+    out_ref[2 * NMODE : PART, :] = jnp.concatenate(
         [gram[8 * i : 8 * i + 8, :] for i in range(NMODE // 8)], axis=1
     )
     for copy in copies[-5:-2]:
         copy.wait()
     line = ti_ref[...] * TROWS + ro_ref[...]
     line_ref[...] = run_row(line)
-    pack_ref[...] = jnp.concatenate(
+    out_ref[PART:, :] = jnp.concatenate(
         [t, line.astype(F32), cs_ref[...].astype(F32), jnp.broadcast_to(w, (DETS, 32))], axis=1
     )
     copies[2].wait()
     eh = basis_ref[:CHUNK, :]
     el = basis_ref[CHUNK:, :]
-    ys = []
-    per = XPIECE // CHUNK
-    for n in range(SEG // XPIECE):
-        copies[3 + n].wait()
-        x = jnp.concatenate(
-            [x_ref[:, c * CHUNK : (c + 1) * CHUNK] for c in range(n * per, (n + 1) * per)], axis=0
-        )
-        hi, lo = split(x)
-        ys.append(mm(hi, eh) + mm(lo, eh) + mm(hi, el))
+    copies[3].wait()
+    wide = jnp.broadcast_to(w, (DETS, CHUNK))
+    x = jnp.concatenate(
+        [wide * x_ref[:, c * CHUNK : (c + 1) * CHUNK] for c in range(NCHUNK)], axis=0
+    )
+    hi, lo = split(x)
+    y = mm(hi, eh) + mm(lo, eh) + mm(hi, el)
     copies[-2].wait()
     re = jnp.zeros((DETS, FKEEP), F32)
     im = jnp.zeros((DETS, FKEEP), F32)
     for c in range(NCHUNK):
-        sl = slice(c % per * DETS, (c % per + 1) * DETS)
-        yc = ys[c // per][sl, :FKEEP]
-        yi = ys[c // per][sl, FKEEP:]
+        sl = slice(c * DETS, (c + 1) * DETS)
+        yc = y[sl, :FKEEP]
+        yi = y[sl, FKEEP:]
         cos = tw_ref[c : c + 1, :FKEEP]
         sin = tw_ref[c : c + 1, FKEEP:]
         re = re + (cos * yc - sin * yi)
@@ -186,36 +184,47 @@
     fill_hot(hot_ref, ids_of_blocks(core_ref[0]), line_ref[...])
 
 
+def shifted_tiles(z, by):
+    zero = jnp.zeros((z.shape[0], 1, 128), F32)
+    if by < 0:
+        return jnp.concatenate([zero, z[:, :-1]], axis=1)
+    return jnp.concatenate([z[:, 1:], zero], axis=1)
+
+
 def second_index_kernel(
-    core_ref, line_ref, pack_ref, other_ref,
-    hot_ref, zhot_ref, idx_ref, edge_ref, mask_ref, zh_ref, rhs_ref, w_ref,
+    core_ref, line_ref, mine_ref, other_ref, hot_ref, idx_ref, hits_ref, rhs_ref, w_ref
 ):
-    packs = (pack_ref[...], other_ref[...])
+    core = core_ref[0]
+    packs = (mine_ref[PART:, :], other_ref[PART:, :])
     lines = [pack[:, 32:64].astype(jnp.int32) for pack in packs]
     rows = (line_ref[...], run_row(lines[1]))
-    fill_hot(hot_ref, ids_of_blocks(core_ref[0]), rows[1])
+    fill_hot(hot_ref, ids_of_blocks(core), rows[1])
     line = jnp.concatenate(rows, axis=1)
     zid = (((line & (TROWS - 1)) + RADIUS) >> 3) * NT + (line >> 6)
     zl = lax.broadcasted_iota(jnp.int32, (ZROWS, 2 * NRUNS), 0)
     zhot = jnp.where(zl == zid, 1.0, 0.0).astype(BF)
-    zhot_ref[...] = zhot
     lane = lax.broadcasted_iota(jnp.int32, (DETS, 128), 1)
-    ecol = edge_col(lane)
     hparts = []
     for n, pack in enumerate(packs):
         w = jnp.broadcast_to(pack[:, 96:97], (DETS, 128))
         w_ref[n * DETS : (n + 1) * DETS, :] = w
-        ro3 = (lines[n] & (TROWS - 1)) + RADIUS
+        spot = ((lines[n] + RADIUS) & (OWN - 1)) + 48
         css = pack[:, 64:96].astype(jnp.int32)
         for c in range(SEG // RUN):
             sl = slice(n * NRUNS + c * DETS, n * NRUNS + (c + 1) * DETS)
             cs = jnp.broadcast_to(css[:, c : c + 1], (DETS, 128))
             idx_ref[sl, :] = (lane - cs) & (TCOLS - 1)
-            edge_ref[sl, :] = (ecol - cs) & (TCOLS - 1)
-            here = ((jnp.broadcast_to(ro3[:, c : c + 1], (DETS, 128)) ^ lane) & (OWN - 1)) == 0
-            mask_ref[sl, :] = jnp.where(here & (lane < 48), 1.0, 0.0)
-            hparts.append(jnp.where(here & (lane >= 48) & (lane < 56), w, 0.0).astype(BF))
-    zh_ref[...] = mm(zhot, jnp.concatenate(hparts, axis=0))
+            here = jnp.broadcast_to(spot[:, c : c + 1], (DETS, 128)) == lane
+            hparts.append(jnp.where(here, w, 0.0).astype(BF))
+    z = mm(zhot, jnp.concatenate(hparts, axis=0)).reshape(ZROWS // NT, NT, 128)
+    right = shifted_tiles(z, 1)
+    right = jnp.concatenate([jnp.zeros(z.shape[:2] + (8,), F32), right[:, :, :-8]], axis=2)
+    nd = TROWS // OWN
+    for n, v in enumerate((shifted_tiles(z, -1) + right, z)):
+        moved = jnp.concatenate([jnp.zeros((nd, NT, 64), F32), v[1:, :, :64]], axis=2)
+        v = v[:nd] + moved
+        picked = [jnp.where(core == 1, v[2 * y + 1], v[2 * y]) for y in range(NY)]
+        hits_ref[n * NBLK : (n + 1) * NBLK, :] = jnp.concatenate(picked, axis=0)
     zero = jnp.zeros((NMODE, 32), F32)
     rhs_ref[...] = jnp.concatenate(
         [zero, packs[0][:, :NMODE].T, packs[1][:, :NMODE].T, zero], axis=1
@@ -274,16 +283,20 @@
     return jnp.concatenate(a, axis=0)[:, n : 3 * n] * down
 
 
-def shifted_tiles(z, by):
-    zero = jnp.zeros((z.shape[0], 1, 128), F32)
-    if by < 0:
-        return jnp.concatenate([zero, z[:, :-1]], axis=1)
-    return jnp.concatenate([z[:, 1:], zero], axis=1)
+def edge_rows(s):
+    lane = lax.broadcasted_iota(jnp.int32, s.shape, 1)
+    moved = jnp.take_along_axis(s, edge_col(lane & 63), axis=1, mode="promise_in_bounds")
+    moved = moved.reshape(NBLK, 2, 8, 128)
+    sub = lax.broadcasted_iota(jnp.int32, (NBLK, 8, 128), 1)
+    lane = lax.broadcasted_iota(jnp.int32, (NBLK, 8, 128), 2)
+    moved = jnp.where(lane < 64, moved[:, 0], moved[:, 1])
+    here = ((lane & 7) == sub) & ((lane & 63) < 48)
+    return jnp.sum(jnp.where(here, moved, 0.0), axis=1)
 
 
 def clean_kernel(
-    core_ref, p_ref, q_ref, r_ref, s_ref, rhs_ref, w_ref, x_ref, other_ref, synth_ref, tw_ref,
-    idx_ref, edge_ref, mask_ref, zhot_ref, zh_ref, hot_ref, other_hot_ref,
+    p_ref, q_ref, r_ref, s_ref, rhs_ref, w_ref, x_ref, other_ref, synth_ref, tw_ref,
+    idx_ref, hits_ref, hot_ref, other_hot_ref,
     blocks_ref, out_hbm, clean_ref, sem,
 ):
     p = (p_ref[...] + q_ref[...]) + (r_ref[...] + s_ref[...])
@@ -292,57 +305,42 @@
     a = ab[:, :FKEEP]
     b = ab[:, FKEEP:]
     parts = []
-    for c in range(NCHUNK):
-        cos = tw_ref[c : c + 1, :FKEEP]
-        sin = tw_ref[c : c + 1, FKEEP:]
+    for c in range(SEG // WIDE):
+        at = c * WIDE // CHUNK
+        cos = tw_ref[at : at + 1, :FKEEP]
+        sin = tw_ref[at : at + 1, FKEEP:]
         parts.append(jnp.concatenate([a * cos + b * sin, b * cos - a * sin], axis=1))
     hi, lo = split(jnp.concatenate(parts, axis=0))
-    sh = synth_ref[:CHUNK, :]
-    low = mm(hi, sh) + mm(lo, sh) + mm(hi, synth_ref[CHUNK:, :])
+    sh = synth_ref[: 2 * FKEEP, :]
+    low = mm(hi, sh) + mm(lo, sh) + mm(hi, synth_ref[2 * FKEEP :, :])
     runs = []
     for n, source in enumerate((x_ref, other_ref)):
         w = w_ref[n * DETS : (n + 1) * DETS, :]
-        w = jnp.concatenate([w, w], axis=1)
-        for c in range(NCHUNK):
-            at = 2 * DETS * c + DETS * n
-            part = w * (source[:, c * CHUNK : (c + 1) * CHUNK] - low[at : at + DETS, :])
+        for r in range(SEG // RUN):
+            at = 2 * DETS * (r * RUN // WIDE) + DETS * n
+            col = r * RUN % WIDE
+            part = w * (source[:, r * RUN : (r + 1) * RUN] - low[at : at + DETS, col : col + RUN])
             if n == 0:
-                clean_ref[:, c * CHUNK : (c + 1) * CHUNK] = part
-            runs.append(part[:, :RUN])
-            runs.append(part[:, RUN:])
+                clean_ref[:, r * RUN : (r + 1) * RUN] = part
+            runs.append(part)
     copy = pltpu.make_async_copy(clean_ref, out_hbm, sem)
     copy.start()
     run = jnp.concatenate(runs, axis=0)
     vals = jnp.concatenate(
         split(jnp.take_along_axis(run, idx_ref[...], axis=1, mode="promise_in_bounds")), axis=1
     )
-    evals = jnp.take_along_axis(run, edge_ref[...], axis=1, mode="promise_in_bounds")
-    evals = jnp.concatenate(split(evals * mask_ref[...]), axis=1)
     s = mm(hot_ref[...], vals[:NRUNS]) + mm(other_hot_ref[...], vals[NRUNS:])
-    blocks_ref[...] = s[:, :128] + s[:, 128:]
-    z = mm(zhot_ref[...], evals)
-    z = (z[:, :128] + z[:, 128:] + zh_ref[...]).reshape(ZROWS // NT, NT, 128)
-    left = shifted_tiles(z, -1)
-    right = shifted_tiles(z, 1)
-    lane = lax.broadcasted_iota(jnp.int32, z.shape, 2)
-    left_hits = left
-    right_hits = jnp.concatenate([jnp.zeros(z.shape[:2] + (8,), F32), right[:, :, :-8]], axis=2)
-    near = jnp.where(
-        lane < 24, left, jnp.where(lane < 48, right, jnp.where(lane < 56, left_hits, right_hits))
-    )
-    near = jnp.where(lane < 64, near, 0.0)
-    mine = jnp.where((lane >= 48) & (lane < 56), z, 0.0)
-    nd = TROWS // OWN
-
-    def both(v):
-        return v[:nd] + jnp.concatenate([jnp.zeros((nd, NT, 64), F32), v[1:, :, :64]], axis=2)
-
-    core = core_ref[0]
-    for row, values in ((14, both(near)), (15, both(mine))):
-        picked = [
-            jnp.where(core == 1, values[2 * y + 1], values[2 * y]) for y in range(NY)
-        ]
-        blocks_ref[pl.ds(row, NBLK, stride=BROWS), :] = jnp.concatenate(picked, axis=0)
+    s = s[:, :128] + s[:, 128:]
+    blocks_ref[...] = s
+    edges = edge_rows(s)
+    tile = lax.broadcasted_iota(jnp.int32, edges.shape, 0) & (NT - 1)
+    slot = (lax.broadcasted_iota(jnp.int32, edges.shape, 1) & 63) >> 3
+    zero = jnp.zeros((1, 128), F32)
+    left = jnp.where(tile == 0, 0.0, jnp.concatenate([zero, edges[:-1]], axis=0))
+    right = jnp.where(tile == NT - 1, 0.0, jnp.concatenate([edges[1:], zero], axis=0))
+    near = jnp.where(slot < RADIUS, left, right) + hits_ref[:NBLK, :]
+    blocks_ref[pl.ds(14, NBLK, stride=BROWS), :] = near
+    blocks_ref[pl.ds(15, NBLK, stride=BROWS), :] = hits_ref[NBLK:, :]
     copy.wait()
 
 
@@ -411,9 +409,6 @@
     return jax.ShapeDtypeStruct(shape, dtype)
 
 
-I32 = jnp.int32
-
-
 def body(timestreams, templates, validity, tile_index, row_offset, col_start):
     basis, synth, tw = tables()
     core = lax.axis_index("core").reshape(1)
@@ -421,11 +416,11 @@
     big = (NBLK * BROWS, NRUNS)
     swap = [(0, 1), (1, 0)]
     mate_x = lax.ppermute(timestreams, "core", swap)
-    part, x, synth, tw, pack, line = call(
+    part, x, synth, tw, line = call(
         analysis_kernel,
         [
-            sds((2 * NMODE + 8, FKEEP)), sds((DETS, SEG)), sds((2 * CHUNK, 2 * FKEEP), BF),
-            sds((NCHUNK, 2 * FKEEP)), sds((DETS, 128)), sds((1, NRUNS), I32),
+            sds((PART + DETS, FKEEP)), sds((DETS, SEG)), sds((4 * FKEEP, WIDE), BF),
+            sds((NCHUNK, 2 * FKEEP)), sds((1, NRUNS), I32),
         ],
         [HBM] * 9, "analysis", 400_000_000,
         timestreams, templates, validity.reshape(1, DETS), tile_index, row_offset, col_start,
@@ -433,31 +428,29 @@
         scratch=[
             pltpu.VMEM((DETS, NMODE), F32), pltpu.VMEM((1, DETS), I32), pltpu.VMEM(small, I32),
             pltpu.VMEM(small, I32), pltpu.VMEM(small, I32),
-            pltpu.VMEM((2 * CHUNK, 2 * FKEEP), BF), pltpu.SemaphoreType.DMA((8 + SEG // XPIECE,)),
+            pltpu.VMEM((2 * CHUNK, 2 * FKEEP), BF), pltpu.SemaphoreType.DMA((9,)),
         ],
     )
     mate = lax.ppermute(part, "core", swap)
     (hot,) = call(
         first_index_kernel, [sds(big, BF)], [SMEM, VMEM], "index1", 100_000_000, core, line
     )
-    mate_pack = lax.ppermute(pack, "core", swap)
-    part, hot, line, mate_pack = lax.optimization_barrier((part + mate, hot, line, mate_pack))
-    others = [lax.ppermute(part, "y", [(k, k ^ m) for k in range(NY)]) for m in (2, 3, 1)]
-    twice = (2 * NRUNS, 128)
-    mate_hot, zhot, idx, edge, mask, zh, rhs, w = call(
+    sums, hot, line = lax.optimization_barrier((part[:PART] + mate[:PART], hot, line))
+    others = [lax.ppermute(sums, "y", [(k, k ^ m) for k in range(NY)]) for m in (2, 3, 1)]
+    mate_hot, idx, hits, rhs, w = call(
         second_index_kernel,
         [
-            sds(big, BF), sds((ZROWS, 2 * NRUNS), BF), sds(twice, I32), sds(twice, I32),
-            sds(twice), sds((ZROWS, 128)), sds((NMODE, 128)), sds((2 * DETS, 128)),
+            sds(big, BF), sds((2 * NRUNS, 128), I32), sds((2 * NBLK, 128)),
+            sds((NMODE, 128)), sds((2 * DETS, 128)),
         ],
         [SMEM] + [VMEM] * 3, "index2", 100_000_000,
-        core, line, pack, mate_pack,
+        core, line, part, mate,
     )
     blocks, cleaned = call(
         clean_kernel,
         [sds((NBLK * BROWS, 128)), sds((DETS, SEG))],
-        [SMEM] + [VMEM] * 17, "clean", 2_000_000_000,
-        core, part, *others, rhs, w, x, mate_x, synth, tw, idx, edge, mask, zhot, zh, hot, mate_hot,
+        [VMEM] * 14, "clean", 2_000_000_000,
+        sums, *others, rhs, w, x, mate_x, synth, tw, idx, hits, hot, mate_hot,
         out_specs=[VMEM, HBM],
         scratch=[pltpu.VMEM((DETS, SEG), F32), pltpu.SemaphoreType.DMA],
     )

time: 40.2 us -> 39.2 us (0.975)
  Pallas kernels: 9.77 us -> 8.79 us
    pallas_call x5, Pallas kernels: 9.77 us -> 8.79 us  [call(): pl.pallas_call(kernel, out_shape=outs, in_specs=specs, out_specs=out_spec...]
    ppermute x4 -> x3, starting transfers between devices: 4.66 us -> 4.63 us  [body(): lax.ppermute(sums, 'y', [(k, k ^ m) for k in range(NY)])]
    ppermute x4 -> x3, waiting for transfers between devices: 2.83 us -> 2.8 us  [body(): lax.ppermute(sums, 'y', [(k, k ^ m) for k in range(NY)])]
  transfers between devices with their start and end apart: 6 -> 5, of which waited for: 3 -> 2; matrix products, arithmetic and copies ran while one was open for 0% -> 0% of each run, Pallas kernels for 12% -> 12%
where the time goes in v9:
time: 39.2 us; the launch traced here: 39 us
  blocking collectives  21.4 us (55%)
  Pallas kernels  8.79 us (22%)
  starting transfers between devices  5.28 us (13%)
  waiting for transfers between devices  2.84 us (7%)
  between operations  0.67 us (2%)
    all_to_all x1, blocking collectives, body(): blocks = lax.all_to_all(blocks, ('y', 'z', 'x'), 0, 0, tiled=True)  21.4 us
    pallas_call x5, Pallas kernels, call(): pl.pallas_call(kernel, out_shape=outs, in_specs=specs, out_specs=out_spec...  8.79 us
    ppermute x3, starting transfers between devices, body(): lax.ppermute(sums, 'y', [(k, k ^ m) for k in range(NY)])  4.63 us
    ppermute x3, waiting for transfers between devices, body(): lax.ppermute(sums, 'y', [(k, k ^ m) for k in range(NY)])  2.8 us
  transfers between devices with their start and end apart: 5, of which 2 were waited for; matrix products, arithmetic and copies ran while one was open for 0% of the time, Pallas kernels for 12%

profile of v9, /device:TPU:0, one launch (start us, length us, event | category | flops | bytes accessed | tf_op | source)
XLA Modules:
  0.0 39.0 jit_solution(479934811927299683)
XLA Ops:
  0.6 0.1 collective-permute-start.4
  0.7 2.0 %analysis.1 = (f32[104,128]{1,0:T(8,128)S(1)}, f32[32,4096]{1,0:T(8,128)S(1)}, bf16[512,1024]{1,0:T(8,128)(2,1)S(1)}, f32[16,256]{1,0:T(8,128)S(1)}, s32[1,1024]{1,0:T(1,128)S(1)}) custom-call(f32[32,4096]{1,0:T(8,128)} %x_hbm.1, f32[32,32]{1,0:T(8,128)} %t_hbm.1, s32[1,32]{1,0:T(1,128)} %bitcast.6, s32[32,32]{1,0:T(8,128)} %ti_hbm.1, s32[32,32]{1,0:T(8,128)} %ro_hbm.1, ...), custom_call_target="tpu_custom_call" | custom-call | flops 400000000 | bytes 5873792 | tf_op jit(solution)/shard_map/analysis/pallas_call | solution.py:396
  2.7 0.6 %collective-permute-start = (f32[104,128]{1,0:T(8,128)S(1)}, f32[104,128]{1,0:T(8,128)S(1)}, u32[]{:S(2)}, u32[]{:S(2)}) collective-permute-start(f32[104,128]{1,0:T(8,128)S(1)} %get-tuple-element.17.mine_ref), channel_id=1, source_target_pairs={{0,16},{16,0},{1,17},{17,1},{2,18},{18,2},{3,19},{19,3},{4,20},{20... | collective-permute-start | bytes 159752 | tf_op jit(solution)/shard_map/ppermute | solution.py:434
  3.3 0.8 %index1.1.hot_ref = bf16[1024,1024]{1,0:T(8,128)(2,1)S(1)} custom-call(s32[1]{0:T(128)} %bitcast.1.core_ref, s32[1,1024]{1,0:T(1,128)S(1)} %get-tuple-element.20.line_ref), custom_call_target="tpu_custom_call" | custom-call | flops 100000000 | bytes 4198404 | tf_op jit(solution)/shard_map/index1/pallas_call | solution.py:396
  4.1 0.0 collective-permute-done.other_ref
  4.2 1.7 %collective-permute-start.3 = (f32[72,128]{1,0:T(8,128)S(1)}, f32[72,128]{1,0:T(8,128)S(1)}, u32[]{:S(2)}, u32[]{:S(2)}) collective-permute-start(f32[72,128]{1,0:T(8,128)S(1)} %slice_add_fusion.p_ref), channel_id=1, source_target_pairs={{0,32},{32,0},{64,96},{96,64},{1,33},{33,1},{65,97},{97,65},{2,34}... | collective-permute-start | bytes 110600 | tf_op jit(solution)/shard_map/ppermute | solution.py:439
  5.9 2.2 %collective-permute-start.2 = (f32[72,128]{1,0:T(8,128)S(1)}, f32[72,128]{1,0:T(8,128)S(1)}, u32[]{:S(2)}, u32[]{:S(2)}) collective-permute-start(f32[72,128]{1,0:T(8,128)S(1)} %slice_add_fusion.p_ref), channel_id=1, source_target_pairs={{0,96},{32,64},{64,32},{96,0},{1,97},{33,65},{65,33},{97,1},{2,98}... | collective-permute-start | bytes 110600 | tf_op jit(solution)/shard_map/ppermute | solution.py:439
  8.1 0.7 %collective-permute-start.1 = (f32[72,128]{1,0:T(8,128)S(1)}, f32[72,128]{1,0:T(8,128)S(1)}, u32[]{:S(2)}, u32[]{:S(2)}) collective-permute-start(f32[72,128]{1,0:T(8,128)S(1)} %slice_add_fusion.p_ref), channel_id=1, source_target_pairs={{0,64},{32,96},{64,0},{96,32},{1,65},{33,97},{65,1},{97,33},{2,66}... | collective-permute-start | bytes 110600 | tf_op jit(solution)/shard_map/ppermute | solution.py:439
  8.8 1.9 %index2.1 = (bf16[1024,1024]{1,0:T(8,128)(2,1)S(1)}, s32[2048,128]{1,0:T(8,128)S(1)}, f32[128,128]{1,0:T(8,128)S(1)}, f32[32,128]{1,0:T(8,128)S(1)}, f32[64,128]{1,0:T(8,128)S(1)}) custom-call(s32[1]{0:T(128)} %bitcast.1.core_ref, s32[1,1024]{1,0:T(1,128)S(1)} %get-tuple-element.20.line_ref, f32[104,128]{1,0:T(8,128)S(1)} %get-tuple-element.17.mine_ref, ...), custom_call_target="tpu_custom_call" | custom-call | flops 100000000 | bytes 5468164 | tf_op jit(solution)/shard_map/index2/pallas_call | solution.py:396
  10.8 0.0 collective-permute-done.3.s_ref
  10.8 0.3 collective-permute-done.2.r_ref
  11.1 2.5 %collective-permute-done.1.q_ref = f32[72,128]{1,0:T(8,128)S(1)} collective-permute-done((f32[72,128]{1,0:T(8,128)S(1)}, f32[72,128]{1,0:T(8,128)S(1)}, u32[]{:S(2)}, u32[]{:S(2)}) %collective-permute-start.1) | collective-permute-done | bytes 36896 | tf_op jit(solution)/shard_map/ppermute | solution.py:439
  13.6 0.0 collective-permute-done.4.other_ref
  13.6 3.2 %clean.1 = (f32[1024,128]{1,0:T(8,128)S(1)}, f32[32,4096]{1,0:T(8,128)}) custom-call(f32[72,128]{1,0:T(8,128)S(1)} %slice_add_fusion.p_ref, f32[72,128]{1,0:T(8,128)S(1)} %collective-permute-done.1.q_ref, f32[72,128]{1,0:T(8,128)S(1)} %collective-permute-done.2.r_ref, f32[72,128]{1,0:T(8,128)S(1)} %collective-permute-done.3.s_ref, ...), custom_call_target="tpu_custom_call" | custom-call | flops 2000000000 | bytes 13910016 | tf_op jit(solution)/shard_map/clean/pallas_call | solution.py:396
  16.8 21.4 %all_to_all.11 = f32[64,16,128]{2,1,0:T(8,128)S(1)} all-to-all(f32[64,16,128]{2,1,0:T(8,128)S(1)} %bitcast.5), channel_id=1, replica_groups=mesh['y'=4,'core'=2,'z'=4,'x'=4] {'y','z','x'}, dimensions={0} | all-to-all | bytes 1048576 | tf_op jit(solution)/shard_map/all_to_all | solution.py:457
  38.2 0.8 %beam.1 = f32[8,128]{1,0:T(8,128)} custom-call(f32[1024,128]{1,0:T(8,128)S(1)} %bitcast.4), custom_call_target="tpu_custom_call" | custom-call | flops 1000000 | bytes 528384 | tf_op jit(solution)/shard_map/beam/pallas_call | solution.py:396
  (1 shorter events, 0.0 us)
Async XLA Ops:
  0.6 12.9 %collective-permute-start.4 = (f32[32,4096]{1,0:T(8,128)}, f32[32,4096]{1,0:T(8,128)S(1)}, u32[]{:S(2)}, u32[]{:S(2)}) collective-permute-start(f32[32,4096]{1,0:T(8,128)} %x_hbm.1), channel_id=1, source_target_pairs={{0,16},{16,0},{1,17},{17,1},{2,18},{18,2},{3,19},{19,3},{4,20},{20... | collective-permute-start | bytes 1572872 | tf_op jit(solution)/shard_map/ppermute | solution.py:418
  2.7 1.5 %collective-permute-start = (f32[104,128]{1,0:T(8,128)S(1)}, f32[104,128]{1,0:T(8,128)S(1)}, u32[]{:S(2)}, u32[]{:S(2)}) collective-permute-start(f32[104,128]{1,0:T(8,128)S(1)} %get-tuple-element.17.mine_ref), channel_id=1, source_target_pairs={{0,16},{16,0},{1,17},{17,1},{2,18},{18,2},{3,19},{19,3},{4,20},{20... | collective-permute-start | bytes 159752 | tf_op jit(solution)/shard_map/ppermute | solution.py:434
  4.2 6.6 %collective-permute-start.3 = (f32[72,128]{1,0:T(8,128)S(1)}, f32[72,128]{1,0:T(8,128)S(1)}, u32[]{:S(2)}, u32[]{:S(2)}) collective-permute-start(f32[72,128]{1,0:T(8,128)S(1)} %slice_add_fusion.p_ref), channel_id=1, source_target_pairs={{0,32},{32,0},{64,96},{96,64},{1,33},{33,1},{65,97},{97,65},{2,34}... | collective-permute-start | bytes 110600 | tf_op jit(solution)/shard_map/ppermute | solution.py:439
  5.9 5.2 %collective-permute-start.2 = (f32[72,128]{1,0:T(8,128)S(1)}, f32[72,128]{1,0:T(8,128)S(1)}, u32[]{:S(2)}, u32[]{:S(2)}) collective-permute-start(f32[72,128]{1,0:T(8,128)S(1)} %slice_add_fusion.p_ref), channel_id=1, source_target_pairs={{0,96},{32,64},{64,32},{96,0},{1,97},{33,65},{65,33},{97,1},{2,98}... | collective-permute-start | bytes 110600 | tf_op jit(solution)/shard_map/ppermute | solution.py:439
  8.1 5.5 %collective-permute-start.1 = (f32[72,128]{1,0:T(8,128)S(1)}, f32[72,128]{1,0:T(8,128)S(1)}, u32[]{:S(2)}, u32[]{:S(2)}) collective-permute-start(f32[72,128]{1,0:T(8,128)S(1)} %slice_add_fusion.p_ref), channel_id=1, source_target_pairs={{0,64},{32,96},{64,0},{96,32},{1,65},{33,97},{65,1},{97,33},{2,66}... | collective-permute-start | bytes 110600 | tf_op jit(solution)/shard_map/ppermute | solution.py:439

commit v10 on v9

--- a/solution.py
+++ b/solution.py
@@ -31,6 +31,7 @@
 BF = jnp.bfloat16
 F32 = jnp.float32
 I32 = jnp.int32
+FIRST = 512
 PART = 2 * NMODE + 8
 
 
@@ -119,31 +120,32 @@
         copy.start()
     copies[0].wait()
     copies[1].wait()
+    copies[2].wait()
+    copies[3].wait()
+    copies[4].wait()
+    copies[5].wait()
+    copies[6].wait()
+    copies[7].wait()
     w = column(v_ref[...].astype(F32), DETS)
     t = t_ref[...]
     wt = t * w
+    eh = basis_ref[:CHUNK, :]
+    el = basis_ref[CHUNK:, :]
+    wide = jnp.broadcast_to(w, (DETS, CHUNK))
+    x = jnp.concatenate(
+        [wide * x_ref[:, c * CHUNK : (c + 1) * CHUNK] for c in range(NCHUNK)], axis=0
+    )
+    hi, lo = split(x)
+    y = mm(hi, eh) + mm(lo, eh) + mm(hi, el)
     gram = mm0(wt, t)
     out_ref[2 * NMODE : PART, :] = jnp.concatenate(
         [gram[8 * i : 8 * i + 8, :] for i in range(NMODE // 8)], axis=1
     )
-    for copy in copies[-5:-2]:
-        copy.wait()
     line = ti_ref[...] * TROWS + ro_ref[...]
     line_ref[...] = run_row(line)
     out_ref[PART:, :] = jnp.concatenate(
         [t, line.astype(F32), cs_ref[...].astype(F32), jnp.broadcast_to(w, (DETS, 32))], axis=1
     )
-    copies[2].wait()
-    eh = basis_ref[:CHUNK, :]
-    el = basis_ref[CHUNK:, :]
-    copies[3].wait()
-    wide = jnp.broadcast_to(w, (DETS, CHUNK))
-    x = jnp.concatenate(
-        [wide * x_ref[:, c * CHUNK : (c + 1) * CHUNK] for c in range(NCHUNK)], axis=0
-    )
-    hi, lo = split(x)
-    y = mm(hi, eh) + mm(lo, eh) + mm(hi, el)
-    copies[-2].wait()
     re = jnp.zeros((DETS, FKEEP), F32)
     im = jnp.zeros((DETS, FKEEP), F32)
     for c in range(NCHUNK):
@@ -157,7 +159,7 @@
     both = mm0_split(wt, jnp.concatenate([re, im], axis=1))
     out_ref[:NMODE, :] = both[:, :FKEEP]
     out_ref[NMODE : 2 * NMODE, :] = both[:, FKEEP:]
-    copies[-1].wait()
+    copies[8].wait()
 
 
 def edge_col(lane):
@@ -175,13 +177,13 @@
 
 
 def fill_hot(ref, ids, line):
-    for q in range(NRUNS // 128):
+    for q in range(line.shape[1] // 128):
         sl = slice(q * 128, (q + 1) * 128)
         ref[:, sl] = jnp.where(ids == line[:, sl], 1.0, 0.0).astype(BF)
 
 
 def first_index_kernel(core_ref, line_ref, hot_ref):
-    fill_hot(hot_ref, ids_of_blocks(core_ref[0]), line_ref[...])
+    fill_hot(hot_ref, ids_of_blocks(core_ref[0]), line_ref[:, :FIRST])
 
 
 def shifted_tiles(z, by):
@@ -198,8 +200,8 @@
     packs = (mine_ref[PART:, :], other_ref[PART:, :])
     lines = [pack[:, 32:64].astype(jnp.int32) for pack in packs]
     rows = (line_ref[...], run_row(lines[1]))
-    fill_hot(hot_ref, ids_of_blocks(core), rows[1])
     line = jnp.concatenate(rows, axis=1)
+    fill_hot(hot_ref, ids_of_blocks(core), line[:, FIRST:])
     zid = (((line & (TROWS - 1)) + RADIUS) >> 3) * NT + (line >> 6)
     zl = lax.broadcasted_iota(jnp.int32, (ZROWS, 2 * NRUNS), 0)
     zhot = jnp.where(zl == zid, 1.0, 0.0).astype(BF)
@@ -296,7 +298,7 @@
 
 def clean_kernel(
     p_ref, q_ref, r_ref, s_ref, rhs_ref, w_ref, x_ref, other_ref, synth_ref, tw_ref,
-    idx_ref, hits_ref, hot_ref, other_hot_ref,
+    idx_ref, hits_ref, hot_ref, more_hot_ref,
     blocks_ref, out_hbm, clean_ref, sem,
 ):
     p = (p_ref[...] + q_ref[...]) + (r_ref[...] + s_ref[...])
@@ -329,7 +331,7 @@
     vals = jnp.concatenate(
         split(jnp.take_along_axis(run, idx_ref[...], axis=1, mode="promise_in_bounds")), axis=1
     )
-    s = mm(hot_ref[...], vals[:NRUNS]) + mm(other_hot_ref[...], vals[NRUNS:])
+    s = mm(hot_ref[...], vals[:FIRST]) + mm(more_hot_ref[...], vals[FIRST:])
     s = s[:, :128] + s[:, 128:]
     blocks_ref[...] = s
     edges = edge_rows(s)
@@ -413,7 +415,6 @@
     basis, synth, tw = tables()
     core = lax.axis_index("core").reshape(1)
     small = (DETS, SEG // RUN)
-    big = (NBLK * BROWS, NRUNS)
     swap = [(0, 1), (1, 0)]
     mate_x = lax.ppermute(timestreams, "core", swap)
     part, x, synth, tw, line = call(
@@ -433,24 +434,25 @@
     )
     mate = lax.ppermute(part, "core", swap)
     (hot,) = call(
-        first_index_kernel, [sds(big, BF)], [SMEM, VMEM], "index1", 100_000_000, core, line
+        first_index_kernel, [sds((NBLK * BROWS, FIRST), BF)], [SMEM, VMEM], "index1", 100_000_000, core, line
     )
     sums, hot, line = lax.optimization_barrier((part[:PART] + mate[:PART], hot, line))
     others = [lax.ppermute(sums, "y", [(k, k ^ m) for k in range(NY)]) for m in (2, 3, 1)]
-    mate_hot, idx, hits, rhs, w = call(
+    more_hot, idx, hits, rhs, w = call(
         second_index_kernel,
         [
-            sds(big, BF), sds((2 * NRUNS, 128), I32), sds((2 * NBLK, 128)),
+            sds((NBLK * BROWS, 2 * NRUNS - FIRST), BF), sds((2 * NRUNS, 128), I32),
+            sds((2 * NBLK, 128)),
             sds((NMODE, 128)), sds((2 * DETS, 128)),
         ],
-        [SMEM] + [VMEM] * 3, "index2", 100_000_000,
+        [SMEM] + [VMEM] * 3, "index2", 3_000_000_000,
         core, line, part, mate,
     )
     blocks, cleaned = call(
         clean_kernel,
         [sds((NBLK * BROWS, 128)), sds((DETS, SEG))],
         [VMEM] * 14, "clean", 2_000_000_000,
-        sums, *others, rhs, w, x, mate_x, synth, tw, idx, hits, hot, mate_hot,
+        sums, *others, rhs, w, x, mate_x, synth, tw, idx, hits, hot, more_hot,
         out_specs=[VMEM, HBM],
         scratch=[pltpu.VMEM((DETS, SEG), F32), pltpu.SemaphoreType.DMA],
     )

time: 39.2 us -> 38.5 us (0.982)
  Pallas kernels: 8.79 us -> 8.22 us
    pallas_call x5, Pallas kernels: 8.79 us -> 8.22 us  [call(): pl.pallas_call(kernel, out_shape=outs, in_specs=specs, out_specs=out_spec...]
    ppermute x1, starting transfers between devices: 0.57 us -> 0.09 us  [body(): mate = lax.ppermute(part, 'core', swap)]
    ppermute x1, starting transfers between devices: 0.08 us -> 0.5 us  [body(): mate_x = lax.ppermute(timestreams, 'core', swap)]
  transfers between devices with their start and end apart: 5 -> 5, of which waited for: 2 -> 3; matrix products, arithmetic and copies ran while one was open for 0% -> 0% of each run, Pallas kernels for 12% -> 6%
where the time goes in v10:
time: 38.5 us; the launch traced here: 38.3 us
  blocking collectives  21.2 us (55%)
  Pallas kernels  8.22 us (21%)
  starting transfers between devices  5.13 us (13%)
  waiting for transfers between devices  3.09 us (8%)
  between operations  0.68 us (2%)
    all_to_all x1, blocking collectives, body(): blocks = lax.all_to_all(blocks, ('y', 'z', 'x'), 0, 0, tiled=True)  21.2 us
    pallas_call x5, Pallas kernels, call(): pl.pallas_call(kernel, out_shape=outs, in_specs=specs, out_specs=out_spec...  8.22 us
    ppermute x3, starting transfers between devices, body(): lax.ppermute(sums, 'y', [(k, k ^ m) for k in range(NY)])  4.55 us
    ppermute x3, waiting for transfers between devices, body(): lax.ppermute(sums, 'y', [(k, k ^ m) for k in range(NY)])  2.84 us
  transfers between devices with their start and end apart: 5, of which 3 were waited for; matrix products, arithmetic and copies ran while one was open for 0% of the time, Pallas kernels for 6%

profile of v10, /device:TPU:0, one launch (start us, length us, event | category | flops | bytes accessed | tf_op | source)
XLA Modules:
  0.0 38.3 jit_solution(17047215713588409195)
XLA Ops:
  0.6 1.8 %analysis.1 = (f32[104,128]{1,0:T(8,128)S(1)}, f32[32,4096]{1,0:T(8,128)S(1)}, bf16[512,1024]{1,0:T(8,128)(2,1)S(1)}, f32[16,256]{1,0:T(8,128)S(1)}, s32[1,1024]{1,0:T(1,128)S(1)}) custom-call(f32[32,4096]{1,0:T(8,128)} %x_hbm.1, f32[32,32]{1,0:T(8,128)} %t_hbm.1, s32[1,32]{1,0:T(1,128)} %bitcast.6, s32[32,32]{1,0:T(8,128)} %ti_hbm.1, s32[32,32]{1,0:T(8,128)} %ro_hbm.1, ...), custom_call_target="tpu_custom_call" | custom-call | flops 400000000 | bytes 5873792 | tf_op jit(solution)/shard_map/analysis/pallas_call | solution.py:398
  2.5 0.1 collective-permute-start
  2.6 0.5 %collective-permute-start.4 = (f32[32,4096]{1,0:T(8,128)}, f32[32,4096]{1,0:T(8,128)S(1)}, u32[]{:S(2)}, u32[]{:S(2)}) collective-permute-start(f32[32,4096]{1,0:T(8,128)} %x_hbm.1), channel_id=1, source_target_pairs={{0,16},{16,0},{1,17},{17,1},{2,18},{18,2},{3,19},{19,3},{4,20},{20... | collective-permute-start | bytes 1572872 | tf_op jit(solution)/shard_map/ppermute | solution.py:419
  3.1 0.5 %index1.1.hot_ref = bf16[1024,512]{1,0:T(8,128)(2,1)S(1)} custom-call(s32[1]{0:T(128)} %bitcast.1.core_ref, s32[1,1024]{1,0:T(1,128)S(1)} %get-tuple-element.20.line_ref), custom_call_target="tpu_custom_call" | custom-call | flops 100000000 | bytes 2101252 | tf_op jit(solution)/shard_map/index1/pallas_call | solution.py:398
  3.6 0.2 collective-permute-done.other_ref
  3.8 1.6 %collective-permute-start.3 = (f32[72,128]{1,0:T(8,128)S(1)}, f32[72,128]{1,0:T(8,128)S(1)}, u32[]{:S(2)}, u32[]{:S(2)}) collective-permute-start(f32[72,128]{1,0:T(8,128)S(1)} %slice_add_fusion.p_ref), channel_id=1, source_target_pairs={{0,32},{32,0},{64,96},{96,64},{1,33},{33,1},{65,97},{97,65},{2,34}... | collective-permute-start | bytes 110600 | tf_op jit(solution)/shard_map/ppermute | solution.py:440
  5.5 2.2 %collective-permute-start.2 = (f32[72,128]{1,0:T(8,128)S(1)}, f32[72,128]{1,0:T(8,128)S(1)}, u32[]{:S(2)}, u32[]{:S(2)}) collective-permute-start(f32[72,128]{1,0:T(8,128)S(1)} %slice_add_fusion.p_ref), channel_id=1, source_target_pairs={{0,96},{32,64},{64,32},{96,0},{1,97},{33,65},{65,33},{97,1},{2,98}... | collective-permute-start | bytes 110600 | tf_op jit(solution)/shard_map/ppermute | solution.py:440
  7.6 0.7 %collective-permute-start.1 = (f32[72,128]{1,0:T(8,128)S(1)}, f32[72,128]{1,0:T(8,128)S(1)}, u32[]{:S(2)}, u32[]{:S(2)}) collective-permute-start(f32[72,128]{1,0:T(8,128)S(1)} %slice_add_fusion.p_ref), channel_id=1, source_target_pairs={{0,64},{32,96},{64,0},{96,32},{1,65},{33,97},{65,1},{97,33},{2,66}... | collective-permute-start | bytes 110600 | tf_op jit(solution)/shard_map/ppermute | solution.py:440
  8.4 1.9 %index2.1 = (bf16[1024,1536]{1,0:T(8,128)(2,1)S(1)}, s32[2048,128]{1,0:T(8,128)S(1)}, f32[128,128]{1,0:T(8,128)S(1)}, f32[32,128]{1,0:T(8,128)S(1)}, f32[64,128]{1,0:T(8,128)S(1)}) custom-call(s32[1]{0:T(128)} %bitcast.1.core_ref, s32[1,1024]{1,0:T(1,128)S(1)} %get-tuple-element.20.line_ref, f32[104,128]{1,0:T(8,128)S(1)} %get-tuple-element.17.mine_ref, ...), custom_call_target="tpu_custom_call" | custom-call | flops 3000000000 | bytes 7565316 | tf_op jit(solution)/shard_map/index2/pallas_call | solution.py:398
  10.3 0.0 collective-permute-done.3.s_ref
  10.3 0.4 collective-permute-done.2.r_ref
  10.6 2.5 %collective-permute-done.1.q_ref = f32[72,128]{1,0:T(8,128)S(1)} collective-permute-done((f32[72,128]{1,0:T(8,128)S(1)}, f32[72,128]{1,0:T(8,128)S(1)}, u32[]{:S(2)}, u32[]{:S(2)}) %collective-permute-start.1) | collective-permute-done | bytes 36896 | tf_op jit(solution)/shard_map/ppermute | solution.py:440
  13.1 0.0 collective-permute-done.4.other_ref
  13.1 3.2 %clean.1 = (f32[1024,128]{1,0:T(8,128)S(1)}, f32[32,4096]{1,0:T(8,128)}) custom-call(f32[72,128]{1,0:T(8,128)S(1)} %slice_add_fusion.p_ref, f32[72,128]{1,0:T(8,128)S(1)} %collective-permute-done.1.q_ref, f32[72,128]{1,0:T(8,128)S(1)} %collective-permute-done.2.r_ref, f32[72,128]{1,0:T(8,128)S(1)} %collective-permute-done.3.s_ref, ...), custom_call_target="tpu_custom_call" | custom-call | flops 2000000000 | bytes 13910016 | tf_op jit(solution)/shard_map/clean/pallas_call | solution.py:398
  16.3 21.2 %all_to_all.11 = f32[64,16,128]{2,1,0:T(8,128)S(1)} all-to-all(f32[64,16,128]{2,1,0:T(8,128)S(1)} %bitcast.5), channel_id=1, replica_groups=mesh['y'=4,'core'=2,'z'=4,'x'=4] {'y','z','x'}, dimensions={0} | all-to-all | bytes 1048576 | tf_op jit(solution)/shard_map/all_to_all | solution.py:459
  37.5 0.8 %beam.1 = f32[8,128]{1,0:T(8,128)} custom-call(f32[1024,128]{1,0:T(8,128)S(1)} %bitcast.4), custom_call_target="tpu_custom_call" | custom-call | flops 1000000 | bytes 528384 | tf_op jit(solution)/shard_map/beam/pallas_call | solution.py:398
  (1 shorter events, 0.0 us)
Async XLA Ops:
  2.5 1.3 %collective-permute-start = (f32[104,128]{1,0:T(8,128)S(1)}, f32[104,128]{1,0:T(8,128)S(1)}, u32[]{:S(2)}, u32[]{:S(2)}) collective-permute-start(f32[104,128]{1,0:T(8,128)S(1)} %get-tuple-element.17.mine_ref), channel_id=1, source_target_pairs={{0,16},{16,0},{1,17},{17,1},{2,18},{18,2},{3,19},{19,3},{4,20},{20... | collective-permute-start | bytes 159752 | tf_op jit(solution)/shard_map/ppermute | solution.py:435
  2.6 10.5 %collective-permute-start.4 = (f32[32,4096]{1,0:T(8,128)}, f32[32,4096]{1,0:T(8,128)S(1)}, u32[]{:S(2)}, u32[]{:S(2)}) collective-permute-start(f32[32,4096]{1,0:T(8,128)} %x_hbm.1), channel_id=1, source_target_pairs={{0,16},{16,0},{1,17},{17,1},{2,18},{18,2},{3,19},{19,3},{4,20},{20... | collective-permute-start | bytes 1572872 | tf_op jit(solution)/shard_map/ppermute | solution.py:419
  3.8 6.4 %collective-permute-start.3 = (f32[72,128]{1,0:T(8,128)S(1)}, f32[72,128]{1,0:T(8,128)S(1)}, u32[]{:S(2)}, u32[]{:S(2)}) collective-permute-start(f32[72,128]{1,0:T(8,128)S(1)} %slice_add_fusion.p_ref), channel_id=1, source_target_pairs={{0,32},{32,0},{64,96},{96,64},{1,33},{33,1},{65,97},{97,65},{2,34}... | collective-permute-start | bytes 110600 | tf_op jit(solution)/shard_map/ppermute | solution.py:440
  5.5 5.2 %collective-permute-start.2 = (f32[72,128]{1,0:T(8,128)S(1)}, f32[72,128]{1,0:T(8,128)S(1)}, u32[]{:S(2)}, u32[]{:S(2)}) collective-permute-start(f32[72,128]{1,0:T(8,128)S(1)} %slice_add_fusion.p_ref), channel_id=1, source_target_pairs={{0,96},{32,64},{64,32},{96,0},{1,97},{33,65},{65,33},{97,1},{2,98}... | collective-permute-start | bytes 110600 | tf_op jit(solution)/shard_map/ppermute | solution.py:440
  7.6 5.5 %collective-permute-start.1 = (f32[72,128]{1,0:T(8,128)S(1)}, f32[72,128]{1,0:T(8,128)S(1)}, u32[]{:S(2)}, u32[]{:S(2)}) collective-permute-start(f32[72,128]{1,0:T(8,128)S(1)} %slice_add_fusion.p_ref), channel_id=1, source_target_pairs={{0,64},{32,96},{64,0},{96,32},{1,65},{33,97},{65,1},{97,33},{2,66}... | collective-permute-start | bytes 110600 | tf_op jit(solution)/shard_map/ppermute | solution.py:440

commit v11 on v10

--- a/solution.py
+++ b/solution.py
@@ -437,7 +437,7 @@
         first_index_kernel, [sds((NBLK * BROWS, FIRST), BF)], [SMEM, VMEM], "index1", 100_000_000, core, line
     )
     sums, hot, line = lax.optimization_barrier((part[:PART] + mate[:PART], hot, line))
-    others = [lax.ppermute(sums, "y", [(k, k ^ m) for k in range(NY)]) for m in (2, 3, 1)]
+    others = [lax.ppermute(sums, "y", [(k, (k + m) % NY) for k in range(NY)]) for m in (1, 3, 2)]
     more_hot, idx, hits, rhs, w = call(
         second_index_kernel,
         [

time: 38.5 us -> 38.5 us (level)
  starting transfers between devices: 5.13 us -> 5.88 us
  waiting for transfers between devices: 3.09 us -> 2.54 us
    ppermute x3, starting transfers between devices: 4.55 us -> 5.29 us  [body(): lax.ppermute(sums, 'y', [(k, (k + m) % NY) for k in range(NY)])]
    ppermute x3, waiting for transfers between devices: 2.84 us -> 2.3 us  [body(): lax.ppermute(sums, 'y', [(k, (k + m) % NY) for k in range(NY)])]
  transfers between devices with their start and end apart: 5 -> 5, of which waited for: 3 -> 2; matrix products, arithmetic and copies ran while one was open for 0% -> 0% of each run, Pallas kernels for 6% -> 6%
where the time goes in v11:
time: 38.5 us; the launch traced here: 38.3 us
  blocking collectives  21 us (55%)
  Pallas kernels  8.22 us (21%)
  starting transfers between devices  5.88 us (15%)
  waiting for transfers between devices  2.54 us (7%)
  between operations  0.68 us (2%)
    all_to_all x1, blocking collectives, body(): blocks = lax.all_to_all(blocks, ('y', 'z', 'x'), 0, 0, tiled=True)  21 us
    pallas_call x5, Pallas kernels, call(): pl.pallas_call(kernel, out_shape=outs, in_specs=specs, out_specs=out_spec...  8.22 us
    ppermute x3, starting transfers between devices, body(): lax.ppermute(sums, 'y', [(k, (k + m) % NY) for k in range(NY)])  5.29 us
    ppermute x3, waiting for transfers between devices, body(): lax.ppermute(sums, 'y', [(k, (k + m) % NY) for k in range(NY)])  2.3 us
  transfers between devices with their start and end apart: 5, of which 2 were waited for; matrix products, arithmetic and copies ran while one was open for 0% of the time, Pallas kernels for 6%

profile of v11, /device:TPU:0, one launch (start us, length us, event | category | flops | bytes accessed | tf_op | source)
XLA Modules:
  0.0 38.3 jit_solution(17087715403576825617)
XLA Ops:
  0.6 1.8 %analysis.1 = (f32[104,128]{1,0:T(8,128)S(1)}, f32[32,4096]{1,0:T(8,128)S(1)}, bf16[512,1024]{1,0:T(8,128)(2,1)S(1)}, f32[16,256]{1,0:T(8,128)S(1)}, s32[1,1024]{1,0:T(1,128)S(1)}) custom-call(f32[32,4096]{1,0:T(8,128)} %x_hbm.1, f32[32,32]{1,0:T(8,128)} %t_hbm.1, s32[1,32]{1,0:T(1,128)} %bitcast.6, s32[32,32]{1,0:T(8,128)} %ti_hbm.1, s32[32,32]{1,0:T(8,128)} %ro_hbm.1, ...), custom_call_target="tpu_custom_call" | custom-call | flops 400000000 | bytes 5873792 | tf_op jit(solution)/shard_map/analysis/pallas_call | solution.py:398
  2.5 0.1 collective-permute-start
  2.6 0.5 %collective-permute-start.4 = (f32[32,4096]{1,0:T(8,128)}, f32[32,4096]{1,0:T(8,128)S(1)}, u32[]{:S(2)}, u32[]{:S(2)}) collective-permute-start(f32[32,4096]{1,0:T(8,128)} %x_hbm.1), channel_id=1, source_target_pairs={{0,16},{16,0},{1,17},{17,1},{2,18},{18,2},{3,19},{19,3},{4,20},{20... | collective-permute-start | bytes 1572872 | tf_op jit(solution)/shard_map/ppermute | solution.py:419
  3.1 0.5 %index1.1.hot_ref = bf16[1024,512]{1,0:T(8,128)(2,1)S(1)} custom-call(s32[1]{0:T(128)} %bitcast.1.core_ref, s32[1,1024]{1,0:T(1,128)S(1)} %get-tuple-element.20.line_ref), custom_call_target="tpu_custom_call" | custom-call | flops 100000000 | bytes 2101252 | tf_op jit(solution)/shard_map/index1/pallas_call | solution.py:398
  3.6 0.2 collective-permute-done.other_ref
  3.8 3.3 %collective-permute-start.3 = (f32[72,128]{1,0:T(8,128)S(1)}, f32[72,128]{1,0:T(8,128)S(1)}, u32[]{:S(2)}, u32[]{:S(2)}) collective-permute-start(f32[72,128]{1,0:T(8,128)S(1)} %slice_add_fusion.p_ref), channel_id=1, source_target_pairs={{0,64},{32,96},{64,0},{96,32},{1,65},{33,97},{65,1},{97,33},{2,66}... | collective-permute-start | bytes 110600 | tf_op jit(solution)/shard_map/ppermute | solution.py:440
  7.1 1.1 %collective-permute-start.2 = (f32[72,128]{1,0:T(8,128)S(1)}, f32[72,128]{1,0:T(8,128)S(1)}, u32[]{:S(2)}, u32[]{:S(2)}) collective-permute-start(f32[72,128]{1,0:T(8,128)S(1)} %slice_add_fusion.p_ref), channel_id=1, source_target_pairs={{0,96},{32,0},{64,32},{96,64},{1,97},{33,1},{65,33},{97,65},{2,98}... | collective-permute-start | bytes 110600 | tf_op jit(solution)/shard_map/ppermute | solution.py:440
  8.1 1.0 %collective-permute-start.1 = (f32[72,128]{1,0:T(8,128)S(1)}, f32[72,128]{1,0:T(8,128)S(1)}, u32[]{:S(2)}, u32[]{:S(2)}) collective-permute-start(f32[72,128]{1,0:T(8,128)S(1)} %slice_add_fusion.p_ref), channel_id=1, source_target_pairs={{0,32},{32,64},{64,96},{96,0},{1,33},{33,65},{65,97},{97,1},{2,34}... | collective-permute-start | bytes 110600 | tf_op jit(solution)/shard_map/ppermute | solution.py:440
  9.1 1.9 %index2.1 = (bf16[1024,1536]{1,0:T(8,128)(2,1)S(1)}, s32[2048,128]{1,0:T(8,128)S(1)}, f32[128,128]{1,0:T(8,128)S(1)}, f32[32,128]{1,0:T(8,128)S(1)}, f32[64,128]{1,0:T(8,128)S(1)}) custom-call(s32[1]{0:T(128)} %bitcast.1.core_ref, s32[1,1024]{1,0:T(1,128)S(1)} %get-tuple-element.20.line_ref, f32[104,128]{1,0:T(8,128)S(1)} %get-tuple-element.17.mine_ref, ...), custom_call_target="tpu_custom_call" | custom-call | flops 3000000000 | bytes 7565316 | tf_op jit(solution)/shard_map/index2/pallas_call | solution.py:398
  11.0 0.0 collective-permute-done.3.s_ref
  11.0 0.0 collective-permute-done.2.r_ref
  11.0 2.3 %collective-permute-done.1.q_ref = f32[72,128]{1,0:T(8,128)S(1)} collective-permute-done((f32[72,128]{1,0:T(8,128)S(1)}, f32[72,128]{1,0:T(8,128)S(1)}, u32[]{:S(2)}, u32[]{:S(2)}) %collective-permute-start.1) | collective-permute-done | bytes 36896 | tf_op jit(solution)/shard_map/ppermute | solution.py:440
  13.3 0.0 collective-permute-done.4.other_ref
  13.3 3.2 %clean.1 = (f32[1024,128]{1,0:T(8,128)S(1)}, f32[32,4096]{1,0:T(8,128)}) custom-call(f32[72,128]{1,0:T(8,128)S(1)} %slice_add_fusion.p_ref, f32[72,128]{1,0:T(8,128)S(1)} %collective-permute-done.1.q_ref, f32[72,128]{1,0:T(8,128)S(1)} %collective-permute-done.2.r_ref, f32[72,128]{1,0:T(8,128)S(1)} %collective-permute-done.3.s_ref, ...), custom_call_target="tpu_custom_call" | custom-call | flops 2000000000 | bytes 13910016 | tf_op jit(solution)/shard_map/clean/pallas_call | solution.py:398
  16.5 21.0 %all_to_all.11 = f32[64,16,128]{2,1,0:T(8,128)S(1)} all-to-all(f32[64,16,128]{2,1,0:T(8,128)S(1)} %bitcast.5), channel_id=1, replica_groups=mesh['y'=4,'core'=2,'z'=4,'x'=4] {'y','z','x'}, dimensions={0} | all-to-all | bytes 1048576 | tf_op jit(solution)/shard_map/all_to_all | solution.py:459
  37.5 0.8 %beam.1 = f32[8,128]{1,0:T(8,128)} custom-call(f32[1024,128]{1,0:T(8,128)S(1)} %bitcast.4), custom_call_target="tpu_custom_call" | custom-call | flops 1000000 | bytes 528384 | tf_op jit(solution)/shard_map/beam/pallas_call | solution.py:398
  (1 shorter events, 0.0 us)
Async XLA Ops:
  2.5 1.3 %collective-permute-start = (f32[104,128]{1,0:T(8,128)S(1)}, f32[104,128]{1,0:T(8,128)S(1)}, u32[]{:S(2)}, u32[]{:S(2)}) collective-permute-start(f32[104,128]{1,0:T(8,128)S(1)} %get-tuple-element.17.mine_ref), channel_id=1, source_target_pairs={{0,16},{16,0},{1,17},{17,1},{2,18},{18,2},{3,19},{19,3},{4,20},{20... | collective-permute-start | bytes 159752 | tf_op jit(solution)/shard_map/ppermute | solution.py:435
  2.6 10.7 %collective-permute-start.4 = (f32[32,4096]{1,0:T(8,128)}, f32[32,4096]{1,0:T(8,128)S(1)}, u32[]{:S(2)}, u32[]{:S(2)}) collective-permute-start(f32[32,4096]{1,0:T(8,128)} %x_hbm.1), channel_id=1, source_target_pairs={{0,16},{16,0},{1,17},{17,1},{2,18},{18,2},{3,19},{19,3},{4,20},{20... | collective-permute-start | bytes 1572872 | tf_op jit(solution)/shard_map/ppermute | solution.py:419
  3.8 7.2 %collective-permute-start.3 = (f32[72,128]{1,0:T(8,128)S(1)}, f32[72,128]{1,0:T(8,128)S(1)}, u32[]{:S(2)}, u32[]{:S(2)}) collective-permute-start(f32[72,128]{1,0:T(8,128)S(1)} %slice_add_fusion.p_ref), channel_id=1, source_target_pairs={{0,64},{32,96},{64,0},{96,32},{1,65},{33,97},{65,1},{97,33},{2,66}... | collective-permute-start | bytes 110600 | tf_op jit(solution)/shard_map/ppermute | solution.py:440
  7.1 4.0 %collective-permute-start.2 = (f32[72,128]{1,0:T(8,128)S(1)}, f32[72,128]{1,0:T(8,128)S(1)}, u32[]{:S(2)}, u32[]{:S(2)}) collective-permute-start(f32[72,128]{1,0:T(8,128)S(1)} %slice_add_fusion.p_ref), channel_id=1, source_target_pairs={{0,96},{32,0},{64,32},{96,64},{1,97},{33,1},{65,33},{97,65},{2,98}... | collective-permute-start | bytes 110600 | tf_op jit(solution)/shard_map/ppermute | solution.py:440
  8.1 5.2 %collective-permute-start.1 = (f32[72,128]{1,0:T(8,128)S(1)}, f32[72,128]{1,0:T(8,128)S(1)}, u32[]{:S(2)}, u32[]{:S(2)}) collective-permute-start(f32[72,128]{1,0:T(8,128)S(1)} %slice_add_fusion.p_ref), channel_id=1, source_target_pairs={{0,32},{32,64},{64,96},{96,0},{1,33},{33,65},{65,97},{97,1},{2,34}... | collective-permute-start | bytes 110600 | tf_op jit(solution)/shard_map/ppermute | solution.py:440

commit v12 on v11

--- a/solution.py
+++ b/solution.py
@@ -171,9 +171,9 @@
     l = lax.broadcasted_iota(jnp.int32, (NBLK * BROWS, 128), 0)
     i = l & (BROWS - 1)
     b = l >> 4
-    row = (b >> 4) * (2 * OWN) + core * OWN - RADIUS + i
+    row = (b & (NY - 1)) * (2 * OWN) + core * OWN - RADIUS + i
     ok = (i < OWN + 2 * RADIUS) & (row >= 0) & (row < TROWS)
-    return jnp.where(ok, (b & (NT - 1)) * TROWS + row, -1)
+    return jnp.where(ok, (b >> 2) * TROWS + row, -1)
 
 
 def fill_hot(ref, ids, line):
@@ -225,8 +225,10 @@
     for n, v in enumerate((shifted_tiles(z, -1) + right, z)):
         moved = jnp.concatenate([jnp.zeros((nd, NT, 64), F32), v[1:, :, :64]], axis=2)
         v = v[:nd] + moved
-        picked = [jnp.where(core == 1, v[2 * y + 1], v[2 * y]) for y in range(NY)]
-        hits_ref[n * NBLK : (n + 1) * NBLK, :] = jnp.concatenate(picked, axis=0)
+        for y in range(NY):
+            hits_ref[pl.ds(n * NBLK + y, NT, stride=NY), :] = jnp.where(
+                core == 1, v[2 * y + 1], v[2 * y]
+            )
     zero = jnp.zeros((NMODE, 32), F32)
     rhs_ref[...] = jnp.concatenate(
         [zero, packs[0][:, :NMODE].T, packs[1][:, :NMODE].T, zero], axis=1
@@ -335,11 +337,11 @@
     s = s[:, :128] + s[:, 128:]
     blocks_ref[...] = s
     edges = edge_rows(s)
-    tile = lax.broadcasted_iota(jnp.int32, edges.shape, 0) & (NT - 1)
+    tile = lax.broadcasted_iota(jnp.int32, edges.shape, 0) >> 2
     slot = (lax.broadcasted_iota(jnp.int32, edges.shape, 1) & 63) >> 3
-    zero = jnp.zeros((1, 128), F32)
-    left = jnp.where(tile == 0, 0.0, jnp.concatenate([zero, edges[:-1]], axis=0))
-    right = jnp.where(tile == NT - 1, 0.0, jnp.concatenate([edges[1:], zero], axis=0))
+    zero = jnp.zeros((NY, 128), F32)
+    left = jnp.where(tile == 0, 0.0, jnp.concatenate([zero, edges[:-NY]], axis=0))
+    right = jnp.where(tile == NT - 1, 0.0, jnp.concatenate([edges[NY:], zero], axis=0))
     near = jnp.where(slot < RADIUS, left, right) + hits_ref[:NBLK, :]
     blocks_ref[pl.ds(14, NBLK, stride=BROWS), :] = near
     blocks_ref[pl.ds(15, NBLK, stride=BROWS), :] = hits_ref[NBLK:, :]
@@ -456,7 +458,7 @@
         out_specs=[VMEM, HBM],
         scratch=[pltpu.VMEM((DETS, SEG), F32), pltpu.SemaphoreType.DMA],
     )
-    blocks = lax.all_to_all(blocks, ("y", "z", "x"), 0, 0, tiled=True)
+    blocks = lax.all_to_all(blocks, ("z", "x", "y"), 0, 0, tiled=True)
     (beamed,) = call(
         beam_kernel, [sds((OWN, TCOLS))], [VMEM], "beam", 1_000_000, blocks
     )

time: 38.5 us -> 38.3 us (level)
  no operation moved by 1% of the time
where the time goes in v12:
time: 38.3 us; the launch traced here: 38.1 us
  blocking collectives  20.8 us (54%)
  Pallas kernels  8.22 us (21%)
  starting transfers between devices  5.88 us (15%)
  waiting for transfers between devices  2.54 us (7%)
  between operations  0.68 us (2%)
    all_to_all x1, blocking collectives, body(): blocks = lax.all_to_all(blocks, ('z', 'x', 'y'), 0, 0, tiled=True)  20.8 us
    pallas_call x5, Pallas kernels, call(): pl.pallas_call(kernel, out_shape=outs, in_specs=specs, out_specs=out_spec...  8.22 us
    ppermute x3, starting transfers between devices, body(): lax.ppermute(sums, 'y', [(k, (k + m) % NY) for k in range(NY)])  5.29 us
    ppermute x3, waiting for transfers between devices, body(): lax.ppermute(sums, 'y', [(k, (k + m) % NY) for k in range(NY)])  2.3 us
  transfers between devices with their start and end apart: 5, of which 2 were waited for; matrix products, arithmetic and copies ran while one was open for 0% of the time, Pallas kernels for 6%

profile of v12, /device:TPU:0, one launch (start us, length us, event | category | flops | bytes accessed | tf_op | source)
XLA Modules:
  0.0 38.1 jit_solution(17607707841584793947)
XLA Ops:
  0.6 1.8 %analysis.1 = (f32[104,128]{1,0:T(8,128)S(1)}, f32[32,4096]{1,0:T(8,128)S(1)}, bf16[512,1024]{1,0:T(8,128)(2,1)S(1)}, f32[16,256]{1,0:T(8,128)S(1)}, s32[1,1024]{1,0:T(1,128)S(1)}) custom-call(f32[32,4096]{1,0:T(8,128)} %x_hbm.1, f32[32,32]{1,0:T(8,128)} %t_hbm.1, s32[1,32]{1,0:T(1,128)} %bitcast.6, s32[32,32]{1,0:T(8,128)} %ti_hbm.1, s32[32,32]{1,0:T(8,128)} %ro_hbm.1, ...), custom_call_target="tpu_custom_call" | custom-call | flops 400000000 | bytes 5873792 | tf_op jit(solution)/shard_map/analysis/pallas_call | solution.py:400
  2.5 0.1 collective-permute-start
  2.6 0.5 %collective-permute-start.4 = (f32[32,4096]{1,0:T(8,128)}, f32[32,4096]{1,0:T(8,128)S(1)}, u32[]{:S(2)}, u32[]{:S(2)}) collective-permute-start(f32[32,4096]{1,0:T(8,128)} %x_hbm.1), channel_id=1, source_target_pairs={{0,16},{16,0},{1,17},{17,1},{2,18},{18,2},{3,19},{19,3},{4,20},{20... | collective-permute-start | bytes 1572872 | tf_op jit(solution)/shard_map/ppermute | solution.py:421
  3.1 0.5 %index1.1.hot_ref = bf16[1024,512]{1,0:T(8,128)(2,1)S(1)} custom-call(s32[1]{0:T(128)} %bitcast.1.core_ref, s32[1,1024]{1,0:T(1,128)S(1)} %get-tuple-element.20.line_ref), custom_call_target="tpu_custom_call" | custom-call | flops 100000000 | bytes 2101252 | tf_op jit(solution)/shard_map/index1/pallas_call | solution.py:400
  3.6 0.2 collective-permute-done.other_ref
  3.8 3.3 %collective-permute-start.3 = (f32[72,128]{1,0:T(8,128)S(1)}, f32[72,128]{1,0:T(8,128)S(1)}, u32[]{:S(2)}, u32[]{:S(2)}) collective-permute-start(f32[72,128]{1,0:T(8,128)S(1)} %slice_add_fusion.p_ref), channel_id=1, source_target_pairs={{0,64},{32,96},{64,0},{96,32},{1,65},{33,97},{65,1},{97,33},{2,66}... | collective-permute-start | bytes 110600 | tf_op jit(solution)/shard_map/ppermute | solution.py:442
  7.1 1.1 %collective-permute-start.2 = (f32[72,128]{1,0:T(8,128)S(1)}, f32[72,128]{1,0:T(8,128)S(1)}, u32[]{:S(2)}, u32[]{:S(2)}) collective-permute-start(f32[72,128]{1,0:T(8,128)S(1)} %slice_add_fusion.p_ref), channel_id=1, source_target_pairs={{0,96},{32,0},{64,32},{96,64},{1,97},{33,1},{65,33},{97,65},{2,98}... | collective-permute-start | bytes 110600 | tf_op jit(solution)/shard_map/ppermute | solution.py:442
  8.1 1.0 %collective-permute-start.1 = (f32[72,128]{1,0:T(8,128)S(1)}, f32[72,128]{1,0:T(8,128)S(1)}, u32[]{:S(2)}, u32[]{:S(2)}) collective-permute-start(f32[72,128]{1,0:T(8,128)S(1)} %slice_add_fusion.p_ref), channel_id=1, source_target_pairs={{0,32},{32,64},{64,96},{96,0},{1,33},{33,65},{65,97},{97,1},{2,34}... | collective-permute-start | bytes 110600 | tf_op jit(solution)/shard_map/ppermute | solution.py:442
  9.1 1.9 %index2.1 = (bf16[1024,1536]{1,0:T(8,128)(2,1)S(1)}, s32[2048,128]{1,0:T(8,128)S(1)}, f32[128,128]{1,0:T(8,128)S(1)}, f32[32,128]{1,0:T(8,128)S(1)}, f32[64,128]{1,0:T(8,128)S(1)}) custom-call(s32[1]{0:T(128)} %bitcast.1.core_ref, s32[1,1024]{1,0:T(1,128)S(1)} %get-tuple-element.20.line_ref, f32[104,128]{1,0:T(8,128)S(1)} %get-tuple-element.17.mine_ref, ...), custom_call_target="tpu_custom_call" | custom-call | flops 3000000000 | bytes 7565316 | tf_op jit(solution)/shard_map/index2/pallas_call | solution.py:400
  11.0 0.0 collective-permute-done.3.s_ref
  11.0 0.0 collective-permute-done.2.r_ref
  11.0 2.3 %collective-permute-done.1.q_ref = f32[72,128]{1,0:T(8,128)S(1)} collective-permute-done((f32[72,128]{1,0:T(8,128)S(1)}, f32[72,128]{1,0:T(8,128)S(1)}, u32[]{:S(2)}, u32[]{:S(2)}) %collective-permute-start.1) | collective-permute-done | bytes 36896 | tf_op jit(solution)/shard_map/ppermute | solution.py:442
  13.3 0.0 collective-permute-done.4.other_ref
  13.3 3.2 %clean.1 = (f32[1024,128]{1,0:T(8,128)S(1)}, f32[32,4096]{1,0:T(8,128)}) custom-call(f32[72,128]{1,0:T(8,128)S(1)} %slice_add_fusion.p_ref, f32[72,128]{1,0:T(8,128)S(1)} %collective-permute-done.1.q_ref, f32[72,128]{1,0:T(8,128)S(1)} %collective-permute-done.2.r_ref, f32[72,128]{1,0:T(8,128)S(1)} %collective-permute-done.3.s_ref, ...), custom_call_target="tpu_custom_call" | custom-call | flops 2000000000 | bytes 13910016 | tf_op jit(solution)/shard_map/clean/pallas_call | solution.py:400
  16.5 20.8 %all_to_all.11 = f32[64,16,128]{2,1,0:T(8,128)S(1)} all-to-all(f32[64,16,128]{2,1,0:T(8,128)S(1)} %bitcast.5), channel_id=1, replica_groups=mesh['y'=4,'core'=2,'z'=4,'x'=4] {'z','x','y'}, dimensions={0} | all-to-all | bytes 1048576 | tf_op jit(solution)/shard_map/all_to_all | solution.py:461
  37.4 0.8 %beam.1 = f32[8,128]{1,0:T(8,128)} custom-call(f32[1024,128]{1,0:T(8,128)S(1)} %bitcast.4), custom_call_target="tpu_custom_call" | custom-call | flops 1000000 | bytes 528384 | tf_op jit(solution)/shard_map/beam/pallas_call | solution.py:400
  (1 shorter events, 0.0 us)
Async XLA Ops:
  2.5 1.3 %collective-permute-start = (f32[104,128]{1,0:T(8,128)S(1)}, f32[104,128]{1,0:T(8,128)S(1)}, u32[]{:S(2)}, u32[]{:S(2)}) collective-permute-start(f32[104,128]{1,0:T(8,128)S(1)} %get-tuple-element.17.mine_ref), channel_id=1, source_target_pairs={{0,16},{16,0},{1,17},{17,1},{2,18},{18,2},{3,19},{19,3},{4,20},{20... | collective-permute-start | bytes 159752 | tf_op jit(solution)/shard_map/ppermute | solution.py:437
  2.6 10.7 %collective-permute-start.4 = (f32[32,4096]{1,0:T(8,128)}, f32[32,4096]{1,0:T(8,128)S(1)}, u32[]{:S(2)}, u32[]{:S(2)}) collective-permute-start(f32[32,4096]{1,0:T(8,128)} %x_hbm.1), channel_id=1, source_target_pairs={{0,16},{16,0},{1,17},{17,1},{2,18},{18,2},{3,19},{19,3},{4,20},{20... | collective-permute-start | bytes 1572872 | tf_op jit(solution)/shard_map/ppermute | solution.py:421
  3.8 7.2 %collective-permute-start.3 = (f32[72,128]{1,0:T(8,128)S(1)}, f32[72,128]{1,0:T(8,128)S(1)}, u32[]{:S(2)}, u32[]{:S(2)}) collective-permute-start(f32[72,128]{1,0:T(8,128)S(1)} %slice_add_fusion.p_ref), channel_id=1, source_target_pairs={{0,64},{32,96},{64,0},{96,32},{1,65},{33,97},{65,1},{97,33},{2,66}... | collective-permute-start | bytes 110600 | tf_op jit(solution)/shard_map/ppermute | solution.py:442
  7.1 4.0 %collective-permute-start.2 = (f32[72,128]{1,0:T(8,128)S(1)}, f32[72,128]{1,0:T(8,128)S(1)}, u32[]{:S(2)}, u32[]{:S(2)}) collective-permute-start(f32[72,128]{1,0:T(8,128)S(1)} %slice_add_fusion.p_ref), channel_id=1, source_target_pairs={{0,96},{32,0},{64,32},{96,64},{1,97},{33,1},{65,33},{97,65},{2,98}... | collective-permute-start | bytes 110600 | tf_op jit(solution)/shard_map/ppermute | solution.py:442
  8.1 5.2 %collective-permute-start.1 = (f32[72,128]{1,0:T(8,128)S(1)}, f32[72,128]{1,0:T(8,128)S(1)}, u32[]{:S(2)}, u32[]{:S(2)}) collective-permute-start(f32[72,128]{1,0:T(8,128)S(1)} %slice_add_fusion.p_ref), channel_id=1, source_target_pairs={{0,32},{32,64},{64,96},{96,0},{1,33},{33,65},{65,97},{97,1},{2,34}... | collective-permute-start | bytes 110600 | tf_op jit(solution)/shard_map/ppermute | solution.py:442

commit v13 on v12

--- a/solution.py
+++ b/solution.py
@@ -110,7 +110,7 @@
         pltpu.make_async_copy(src, dst, sems.at[n])
         for n, (src, dst) in enumerate(
             [
-                (t_hbm, t_ref), (v_hbm, v_ref), (basis_hbm, basis_ref), (x_hbm, x_ref),
+                (v_hbm, v_ref), (t_hbm, t_ref), (x_hbm, x_ref), (basis_hbm, basis_ref),
                 (ti_hbm, ti_ref), (ro_hbm, ro_ref), (cs_hbm, cs_ref),
                 (tw_hbm, tw_ref), (synth_hbm, synth_ref),
             ]
@@ -439,7 +439,7 @@
         first_index_kernel, [sds((NBLK * BROWS, FIRST), BF)], [SMEM, VMEM], "index1", 100_000_000, core, line
     )
     sums, hot, line = lax.optimization_barrier((part[:PART] + mate[:PART], hot, line))
-    others = [lax.ppermute(sums, "y", [(k, (k + m) % NY) for k in range(NY)]) for m in (1, 3, 2)]
+    others = [lax.ppermute(sums, "y", [(k, k ^ m) for k in range(NY)]) for m in (3, 1, 2)]
     more_hot, idx, hits, rhs, w = call(
         second_index_kernel,
         [

time: 38.3 us -> 38.2 us (level)
  starting transfers between devices: 5.88 us -> 4.93 us
  waiting for transfers between devices: 2.54 us -> 3.13 us
    ppermute x3, starting transfers between devices: 5.29 us -> 4.35 us  [body(): lax.ppermute(sums, 'y', [(k, k ^ m) for k in range(NY)])]
    ppermute x3, waiting for transfers between devices: 2.3 us -> 2.89 us  [body(): lax.ppermute(sums, 'y', [(k, k ^ m) for k in range(NY)])]
  transfers between devices with their start and end apart: 5 -> 5, of which waited for: 2 -> 3; matrix products, arithmetic and copies ran while one was open for 0% -> 0% of each run, Pallas kernels for 6% -> 6%
where the time goes in v13:
time: 38.2 us; the launch traced here: 38.1 us
  blocking collectives  21.1 us (55%)
  Pallas kernels  8.2 us (21%)
  starting transfers between devices  4.93 us (13%)
  waiting for transfers between devices  3.13 us (8%)
  between operations  0.68 us (2%)
    all_to_all x1, blocking collectives, body(): blocks = lax.all_to_all(blocks, ('z', 'x', 'y'), 0, 0, tiled=True)  21.1 us
    pallas_call x5, Pallas kernels, call(): pl.pallas_call(kernel, out_shape=outs, in_specs=specs, out_specs=out_spec...  8.2 us
    ppermute x3, starting transfers between devices, body(): lax.ppermute(sums, 'y', [(k, k ^ m) for k in range(NY)])  4.35 us
    ppermute x3, waiting for transfers between devices, body(): lax.ppermute(sums, 'y', [(k, k ^ m) for k in range(NY)])  2.89 us
  transfers between devices with their start and end apart: 5, of which 3 were waited for; matrix products, arithmetic and copies ran while one was open for 0% of the time, Pallas kernels for 6%

profile of v13, /device:TPU:0, one launch (start us, length us, event | category | flops | bytes accessed | tf_op | source)
XLA Modules:
  0.0 38.1 jit_solution(14089302999649080634)
XLA Ops:
  0.6 1.8 %analysis.1 = (f32[104,128]{1,0:T(8,128)S(1)}, f32[32,4096]{1,0:T(8,128)S(1)}, bf16[512,1024]{1,0:T(8,128)(2,1)S(1)}, f32[16,256]{1,0:T(8,128)S(1)}, s32[1,1024]{1,0:T(1,128)S(1)}) custom-call(f32[32,4096]{1,0:T(8,128)} %x_hbm.1, f32[32,32]{1,0:T(8,128)} %t_hbm.1, s32[1,32]{1,0:T(1,128)} %bitcast.6, s32[32,32]{1,0:T(8,128)} %ti_hbm.1, s32[32,32]{1,0:T(8,128)} %ro_hbm.1, ...), custom_call_target="tpu_custom_call" | custom-call | flops 400000000 | bytes 5873792 | tf_op jit(solution)/shard_map/analysis/pallas_call | solution.py:400
  2.5 0.1 collective-permute-start
  2.6 0.5 %collective-permute-start.4 = (f32[32,4096]{1,0:T(8,128)}, f32[32,4096]{1,0:T(8,128)S(1)}, u32[]{:S(2)}, u32[]{:S(2)}) collective-permute-start(f32[32,4096]{1,0:T(8,128)} %x_hbm.1), channel_id=1, source_target_pairs={{0,16},{16,0},{1,17},{17,1},{2,18},{18,2},{3,19},{19,3},{4,20},{20... | collective-permute-start | bytes 1572872 | tf_op jit(solution)/shard_map/ppermute | solution.py:421
  3.0 0.5 %index1.1.hot_ref = bf16[1024,512]{1,0:T(8,128)(2,1)S(1)} custom-call(s32[1]{0:T(128)} %bitcast.1.core_ref, s32[1,1024]{1,0:T(1,128)S(1)} %get-tuple-element.20.line_ref), custom_call_target="tpu_custom_call" | custom-call | flops 100000000 | bytes 2101252 | tf_op jit(solution)/shard_map/index1/pallas_call | solution.py:400
  3.5 0.2 collective-permute-done.other_ref
  3.8 3.3 %collective-permute-start.3 = (f32[72,128]{1,0:T(8,128)S(1)}, f32[72,128]{1,0:T(8,128)S(1)}, u32[]{:S(2)}, u32[]{:S(2)}) collective-permute-start(f32[72,128]{1,0:T(8,128)S(1)} %slice_add_fusion.p_ref), channel_id=1, source_target_pairs={{0,64},{32,96},{64,0},{96,32},{1,65},{33,97},{65,1},{97,33},{2,66}... | collective-permute-start | bytes 110600 | tf_op jit(solution)/shard_map/ppermute | solution.py:442
  7.1 0.7 %collective-permute-start.2 = (f32[72,128]{1,0:T(8,128)S(1)}, f32[72,128]{1,0:T(8,128)S(1)}, u32[]{:S(2)}, u32[]{:S(2)}) collective-permute-start(f32[72,128]{1,0:T(8,128)S(1)} %slice_add_fusion.p_ref), channel_id=1, source_target_pairs={{0,32},{32,0},{64,96},{96,64},{1,33},{33,1},{65,97},{97,65},{2,34}... | collective-permute-start | bytes 110600 | tf_op jit(solution)/shard_map/ppermute | solution.py:442
  7.7 0.4 %collective-permute-start.1 = (f32[72,128]{1,0:T(8,128)S(1)}, f32[72,128]{1,0:T(8,128)S(1)}, u32[]{:S(2)}, u32[]{:S(2)}) collective-permute-start(f32[72,128]{1,0:T(8,128)S(1)} %slice_add_fusion.p_ref), channel_id=1, source_target_pairs={{0,96},{32,64},{64,32},{96,0},{1,97},{33,65},{65,33},{97,1},{2,98}... | collective-permute-start | bytes 110600 | tf_op jit(solution)/shard_map/ppermute | solution.py:442
  8.1 1.9 %index2.1 = (bf16[1024,1536]{1,0:T(8,128)(2,1)S(1)}, s32[2048,128]{1,0:T(8,128)S(1)}, f32[128,128]{1,0:T(8,128)S(1)}, f32[32,128]{1,0:T(8,128)S(1)}, f32[64,128]{1,0:T(8,128)S(1)}) custom-call(s32[1]{0:T(128)} %bitcast.1.core_ref, s32[1,1024]{1,0:T(1,128)S(1)} %get-tuple-element.20.line_ref, f32[104,128]{1,0:T(8,128)S(1)} %get-tuple-element.17.mine_ref, ...), custom_call_target="tpu_custom_call" | custom-call | flops 3000000000 | bytes 7565316 | tf_op jit(solution)/shard_map/index2/pallas_call | solution.py:400
  10.0 0.0 collective-permute-done.3.s_ref
  10.0 1.0 %collective-permute-done.2.r_ref = f32[72,128]{1,0:T(8,128)S(1)} collective-permute-done((f32[72,128]{1,0:T(8,128)S(1)}, f32[72,128]{1,0:T(8,128)S(1)}, u32[]{:S(2)}, u32[]{:S(2)}) %collective-permute-start.2) | collective-permute-done | bytes 36896 | tf_op jit(solution)/shard_map/ppermute | solution.py:442
  11.0 1.9 %collective-permute-done.1.q_ref = f32[72,128]{1,0:T(8,128)S(1)} collective-permute-done((f32[72,128]{1,0:T(8,128)S(1)}, f32[72,128]{1,0:T(8,128)S(1)}, u32[]{:S(2)}, u32[]{:S(2)}) %collective-permute-start.1) | collective-permute-done | bytes 36896 | tf_op jit(solution)/shard_map/ppermute | solution.py:442
  12.9 0.0 collective-permute-done.4.other_ref
  12.9 3.2 %clean.1 = (f32[1024,128]{1,0:T(8,128)S(1)}, f32[32,4096]{1,0:T(8,128)}) custom-call(f32[72,128]{1,0:T(8,128)S(1)} %slice_add_fusion.p_ref, f32[72,128]{1,0:T(8,128)S(1)} %collective-permute-done.1.q_ref, f32[72,128]{1,0:T(8,128)S(1)} %collective-permute-done.2.r_ref, f32[72,128]{1,0:T(8,128)S(1)} %collective-permute-done.3.s_ref, ...), custom_call_target="tpu_custom_call" | custom-call | flops 2000000000 | bytes 13910016 | tf_op jit(solution)/shard_map/clean/pallas_call | solution.py:400
  16.2 21.1 %all_to_all.11 = f32[64,16,128]{2,1,0:T(8,128)S(1)} all-to-all(f32[64,16,128]{2,1,0:T(8,128)S(1)} %bitcast.5), channel_id=1, replica_groups=mesh['y'=4,'core'=2,'z'=4,'x'=4] {'z','x','y'}, dimensions={0} | all-to-all | bytes 1048576 | tf_op jit(solution)/shard_map/all_to_all | solution.py:461
  37.3 0.8 %beam.1 = f32[8,128]{1,0:T(8,128)} custom-call(f32[1024,128]{1,0:T(8,128)S(1)} %bitcast.4), custom_call_target="tpu_custom_call" | custom-call | flops 1000000 | bytes 528384 | tf_op jit(solution)/shard_map/beam/pallas_call | solution.py:400
  (1 shorter events, 0.0 us)
Async XLA Ops:
  2.5 1.3 %collective-permute-start = (f32[104,128]{1,0:T(8,128)S(1)}, f32[104,128]{1,0:T(8,128)S(1)}, u32[]{:S(2)}, u32[]{:S(2)}) collective-permute-start(f32[104,128]{1,0:T(8,128)S(1)} %get-tuple-element.17.mine_ref), channel_id=1, source_target_pairs={{0,16},{16,0},{1,17},{17,1},{2,18},{18,2},{3,19},{19,3},{4,20},{20... | collective-permute-start | bytes 159752 | tf_op jit(solution)/shard_map/ppermute | solution.py:437
  2.6 10.4 %collective-permute-start.4 = (f32[32,4096]{1,0:T(8,128)}, f32[32,4096]{1,0:T(8,128)S(1)}, u32[]{:S(2)}, u32[]{:S(2)}) collective-permute-start(f32[32,4096]{1,0:T(8,128)} %x_hbm.1), channel_id=1, source_target_pairs={{0,16},{16,0},{1,17},{17,1},{2,18},{18,2},{3,19},{19,3},{4,20},{20... | collective-permute-start | bytes 1572872 | tf_op jit(solution)/shard_map/ppermute | solution.py:421
  3.8 6.2 %collective-permute-start.3 = (f32[72,128]{1,0:T(8,128)S(1)}, f32[72,128]{1,0:T(8,128)S(1)}, u32[]{:S(2)}, u32[]{:S(2)}) collective-permute-start(f32[72,128]{1,0:T(8,128)S(1)} %slice_add_fusion.p_ref), channel_id=1, source_target_pairs={{0,64},{32,96},{64,0},{96,32},{1,65},{33,97},{65,1},{97,33},{2,66}... | collective-permute-start | bytes 110600 | tf_op jit(solution)/shard_map/ppermute | solution.py:442
  7.1 4.0 %collective-permute-start.2 = (f32[72,128]{1,0:T(8,128)S(1)}, f32[72,128]{1,0:T(8,128)S(1)}, u32[]{:S(2)}, u32[]{:S(2)}) collective-permute-start(f32[72,128]{1,0:T(8,128)S(1)} %slice_add_fusion.p_ref), channel_id=1, source_target_pairs={{0,32},{32,0},{64,96},{96,64},{1,33},{33,1},{65,97},{97,65},{2,34}... | collective-permute-start | bytes 110600 | tf_op jit(solution)/shard_map/ppermute | solution.py:442
  7.7 5.2 %collective-permute-start.1 = (f32[72,128]{1,0:T(8,128)S(1)}, f32[72,128]{1,0:T(8,128)S(1)}, u32[]{:S(2)}, u32[]{:S(2)}) collective-permute-start(f32[72,128]{1,0:T(8,128)S(1)} %slice_add_fusion.p_ref), channel_id=1, source_target_pairs={{0,96},{32,64},{64,32},{96,0},{1,97},{33,65},{65,33},{97,1},{2,98}... | collective-permute-start | bytes 110600 | tf_op jit(solution)/shard_map/ppermute | solution.py:442

commit v14 on v13

--- a/solution.py
+++ b/solution.py
@@ -439,7 +439,7 @@
         first_index_kernel, [sds((NBLK * BROWS, FIRST), BF)], [SMEM, VMEM], "index1", 100_000_000, core, line
     )
     sums, hot, line = lax.optimization_barrier((part[:PART] + mate[:PART], hot, line))
-    others = [lax.ppermute(sums, "y", [(k, k ^ m) for k in range(NY)]) for m in (3, 1, 2)]
+    others = [lax.ppermute(sums, "y", [(k, k ^ m) for k in range(NY)]) for m in (2, 3, 1)]
     more_hot, idx, hits, rhs, w = call(
         second_index_kernel,
         [

time: 38.2 us -> 38.3 us (level)
  no operation moved by 1% of the time
where the time goes in v14:
time: 38.3 us; the launch traced here: 38.1 us
  blocking collectives  21 us (55%)
  Pallas kernels  8.2 us (21%)
  starting transfers between devices  5.15 us (13%)
  waiting for transfers between devices  3.09 us (8%)
  between operations  0.68 us (2%)
    all_to_all x1, blocking collectives, body(): blocks = lax.all_to_all(blocks, ('z', 'x', 'y'), 0, 0, tiled=True)  21 us
    pallas_call x5, Pallas kernels, call(): pl.pallas_call(kernel, out_shape=outs, in_specs=specs, out_specs=out_spec...  8.2 us
    ppermute x3, starting transfers between devices, body(): lax.ppermute(sums, 'y', [(k, k ^ m) for k in range(NY)])  4.57 us
    ppermute x3, waiting for transfers between devices, body(): lax.ppermute(sums, 'y', [(k, k ^ m) for k in range(NY)])  2.84 us
  transfers between devices with their start and end apart: 5, of which 3 were waited for; matrix products, arithmetic and copies ran while one was open for 0% of the time, Pallas kernels for 6%

profile of v14, /device:TPU:0, one launch (start us, length us, event | category | flops | bytes accessed | tf_op | source)
XLA Modules:
  0.0 38.1 jit_solution(14305660321691231872)
XLA Ops:
  0.6 1.8 %analysis.1 = (f32[104,128]{1,0:T(8,128)S(1)}, f32[32,4096]{1,0:T(8,128)S(1)}, bf16[512,1024]{1,0:T(8,128)(2,1)S(1)}, f32[16,256]{1,0:T(8,128)S(1)}, s32[1,1024]{1,0:T(1,128)S(1)}) custom-call(f32[32,4096]{1,0:T(8,128)} %x_hbm.1, f32[32,32]{1,0:T(8,128)} %t_hbm.1, s32[1,32]{1,0:T(1,128)} %bitcast.6, s32[32,32]{1,0:T(8,128)} %ti_hbm.1, s32[32,32]{1,0:T(8,128)} %ro_hbm.1, ...), custom_call_target="tpu_custom_call" | custom-call | flops 400000000 | bytes 5873792 | tf_op jit(solution)/shard_map/analysis/pallas_call | solution.py:400
  2.5 0.1 collective-permute-start
  2.6 0.5 %collective-permute-start.4 = (f32[32,4096]{1,0:T(8,128)}, f32[32,4096]{1,0:T(8,128)S(1)}, u32[]{:S(2)}, u32[]{:S(2)}) collective-permute-start(f32[32,4096]{1,0:T(8,128)} %x_hbm.1), channel_id=1, source_target_pairs={{0,16},{16,0},{1,17},{17,1},{2,18},{18,2},{3,19},{19,3},{4,20},{20... | collective-permute-start | bytes 1572872 | tf_op jit(solution)/shard_map/ppermute | solution.py:421
  3.0 0.5 %index1.1.hot_ref = bf16[1024,512]{1,0:T(8,128)(2,1)S(1)} custom-call(s32[1]{0:T(128)} %bitcast.1.core_ref, s32[1,1024]{1,0:T(1,128)S(1)} %get-tuple-element.20.line_ref), custom_call_target="tpu_custom_call" | custom-call | flops 100000000 | bytes 2101252 | tf_op jit(solution)/shard_map/index1/pallas_call | solution.py:400
  3.5 0.2 collective-permute-done.other_ref
  3.8 1.7 %collective-permute-start.3 = (f32[72,128]{1,0:T(8,128)S(1)}, f32[72,128]{1,0:T(8,128)S(1)}, u32[]{:S(2)}, u32[]{:S(2)}) collective-permute-start(f32[72,128]{1,0:T(8,128)S(1)} %slice_add_fusion.p_ref), channel_id=1, source_target_pairs={{0,32},{32,0},{64,96},{96,64},{1,33},{33,1},{65,97},{97,65},{2,34}... | collective-permute-start | bytes 110600 | tf_op jit(solution)/shard_map/ppermute | solution.py:442
  5.5 2.2 %collective-permute-start.2 = (f32[72,128]{1,0:T(8,128)S(1)}, f32[72,128]{1,0:T(8,128)S(1)}, u32[]{:S(2)}, u32[]{:S(2)}) collective-permute-start(f32[72,128]{1,0:T(8,128)S(1)} %slice_add_fusion.p_ref), channel_id=1, source_target_pairs={{0,96},{32,64},{64,32},{96,0},{1,97},{33,65},{65,33},{97,1},{2,98}... | collective-permute-start | bytes 110600 | tf_op jit(solution)/shard_map/ppermute | solution.py:442
  7.6 0.7 %collective-permute-start.1 = (f32[72,128]{1,0:T(8,128)S(1)}, f32[72,128]{1,0:T(8,128)S(1)}, u32[]{:S(2)}, u32[]{:S(2)}) collective-permute-start(f32[72,128]{1,0:T(8,128)S(1)} %slice_add_fusion.p_ref), channel_id=1, source_target_pairs={{0,64},{32,96},{64,0},{96,32},{1,65},{33,97},{65,1},{97,33},{2,66}... | collective-permute-start | bytes 110600 | tf_op jit(solution)/shard_map/ppermute | solution.py:442
  8.4 1.9 %index2.1 = (bf16[1024,1536]{1,0:T(8,128)(2,1)S(1)}, s32[2048,128]{1,0:T(8,128)S(1)}, f32[128,128]{1,0:T(8,128)S(1)}, f32[32,128]{1,0:T(8,128)S(1)}, f32[64,128]{1,0:T(8,128)S(1)}) custom-call(s32[1]{0:T(128)} %bitcast.1.core_ref, s32[1,1024]{1,0:T(1,128)S(1)} %get-tuple-element.20.line_ref, f32[104,128]{1,0:T(8,128)S(1)} %get-tuple-element.17.mine_ref, ...), custom_call_target="tpu_custom_call" | custom-call | flops 3000000000 | bytes 7565316 | tf_op jit(solution)/shard_map/index2/pallas_call | solution.py:400
  10.2 0.0 collective-permute-done.3.s_ref
  10.3 0.4 collective-permute-done.2.r_ref
  10.6 2.5 %collective-permute-done.1.q_ref = f32[72,128]{1,0:T(8,128)S(1)} collective-permute-done((f32[72,128]{1,0:T(8,128)S(1)}, f32[72,128]{1,0:T(8,128)S(1)}, u32[]{:S(2)}, u32[]{:S(2)}) %collective-permute-start.1) | collective-permute-done | bytes 36896 | tf_op jit(solution)/shard_map/ppermute | solution.py:442
  13.1 0.0 collective-permute-done.4.other_ref
  13.1 3.2 %clean.1 = (f32[1024,128]{1,0:T(8,128)S(1)}, f32[32,4096]{1,0:T(8,128)}) custom-call(f32[72,128]{1,0:T(8,128)S(1)} %slice_add_fusion.p_ref, f32[72,128]{1,0:T(8,128)S(1)} %collective-permute-done.1.q_ref, f32[72,128]{1,0:T(8,128)S(1)} %collective-permute-done.2.r_ref, f32[72,128]{1,0:T(8,128)S(1)} %collective-permute-done.3.s_ref, ...), custom_call_target="tpu_custom_call" | custom-call | flops 2000000000 | bytes 13910016 | tf_op jit(solution)/shard_map/clean/pallas_call | solution.py:400
  16.3 21.0 %all_to_all.11 = f32[64,16,128]{2,1,0:T(8,128)S(1)} all-to-all(f32[64,16,128]{2,1,0:T(8,128)S(1)} %bitcast.5), channel_id=1, replica_groups=mesh['y'=4,'core'=2,'z'=4,'x'=4] {'z','x','y'}, dimensions={0} | all-to-all | bytes 1048576 | tf_op jit(solution)/shard_map/all_to_all | solution.py:461
  37.3 0.8 %beam.1 = f32[8,128]{1,0:T(8,128)} custom-call(f32[1024,128]{1,0:T(8,128)S(1)} %bitcast.4), custom_call_target="tpu_custom_call" | custom-call | flops 1000000 | bytes 528384 | tf_op jit(solution)/shard_map/beam/pallas_call | solution.py:400
  (1 shorter events, 0.0 us)
Async XLA Ops:
  2.5 1.3 %collective-permute-start = (f32[104,128]{1,0:T(8,128)S(1)}, f32[104,128]{1,0:T(8,128)S(1)}, u32[]{:S(2)}, u32[]{:S(2)}) collective-permute-start(f32[104,128]{1,0:T(8,128)S(1)} %get-tuple-element.17.mine_ref), channel_id=1, source_target_pairs={{0,16},{16,0},{1,17},{17,1},{2,18},{18,2},{3,19},{19,3},{4,20},{20... | collective-permute-start | bytes 159752 | tf_op jit(solution)/shard_map/ppermute | solution.py:437
  2.6 10.5 %collective-permute-start.4 = (f32[32,4096]{1,0:T(8,128)}, f32[32,4096]{1,0:T(8,128)S(1)}, u32[]{:S(2)}, u32[]{:S(2)}) collective-permute-start(f32[32,4096]{1,0:T(8,128)} %x_hbm.1), channel_id=1, source_target_pairs={{0,16},{16,0},{1,17},{17,1},{2,18},{18,2},{3,19},{19,3},{4,20},{20... | collective-permute-start | bytes 1572872 | tf_op jit(solution)/shard_map/ppermute | solution.py:421
  3.8 6.5 %collective-permute-start.3 = (f32[72,128]{1,0:T(8,128)S(1)}, f32[72,128]{1,0:T(8,128)S(1)}, u32[]{:S(2)}, u32[]{:S(2)}) collective-permute-start(f32[72,128]{1,0:T(8,128)S(1)} %slice_add_fusion.p_ref), channel_id=1, source_target_pairs={{0,32},{32,0},{64,96},{96,64},{1,33},{33,1},{65,97},{97,65},{2,34}... | collective-permute-start | bytes 110600 | tf_op jit(solution)/shard_map/ppermute | solution.py:442
  5.5 5.2 %collective-permute-start.2 = (f32[72,128]{1,0:T(8,128)S(1)}, f32[72,128]{1,0:T(8,128)S(1)}, u32[]{:S(2)}, u32[]{:S(2)}) collective-permute-start(f32[72,128]{1,0:T(8,128)S(1)} %slice_add_fusion.p_ref), channel_id=1, source_target_pairs={{0,96},{32,64},{64,32},{96,0},{1,97},{33,65},{65,33},{97,1},{2,98}... | collective-permute-start | bytes 110600 | tf_op jit(solution)/shard_map/ppermute | solution.py:442
  7.6 5.5 %collective-permute-start.1 = (f32[72,128]{1,0:T(8,128)S(1)}, f32[72,128]{1,0:T(8,128)S(1)}, u32[]{:S(2)}, u32[]{:S(2)}) collective-permute-start(f32[72,128]{1,0:T(8,128)S(1)} %slice_add_fusion.p_ref), channel_id=1, source_target_pairs={{0,64},{32,96},{64,0},{96,32},{1,65},{33,97},{65,1},{97,33},{2,66}... | collective-permute-start | bytes 110600 | tf_op jit(solution)/shard_map/ppermute | solution.py:442
